TPU v7x, 32 devices: a whole 2x2x4 slice. The times are simulated.
32 devices in a mesh: fsdp: 16 (over z, y, x), tp: 2 (over core).
Axes of the slice: x: 2, y: 2, z: 4, core: 2. Of those that a mesh axis runs over, the one named last changes fastest.
Arguments:
- hidden_in: bfloat16 [8192, 2560], P(('fsdp', 'tp')), may hold values from -67 to 67
- seq_ids: int32 [16, 512], P('fsdp'), may hold values from 0 to 1, never falling along the last dimension, each value on 1 to 384 neighbouring positions
- block_ids: int32 [16, 512], P('fsdp'), may hold values from 0 to 3, never falling along the last dimension, each value on 1 to 256 neighbouring positions
- clip_limit: float32 [1], replicated, may hold values from 6 to 12
- cotangent: bfloat16 [8192, 2560], P(('fsdp', 'tp')), may hold values from -6 to 6
- q_down: bfloat16 [2560, 768], P(('fsdp', 'tp')), may hold values from -0.125 to 0.125
- kv_down: bfloat16 [2560, 288], P(('fsdp', 'tp')), may hold values from -0.125 to 0.125
- q_up: bfloat16 [768, 3840], P('fsdp', 'tp'), may hold values from -1 to 1
- kv_up: bfloat16 [256, 5120], P('fsdp', 'tp'), may hold values from -0.375 to 0.375
- out_proj: bfloat16 [2560, 2560], P('fsdp', 'tp'), may hold values from -0.5 to 0.5
- gate_proj: bfloat16 [2560, 6400], P('fsdp', 'tp'), may hold values from -0.125 to 0.125
- up_proj: bfloat16 [2560, 6400], P('fsdp', 'tp'), may hold values from -0.125 to 0.125
- down_proj: bfloat16 [2560, 6400], P('fsdp', 'tp'), may hold values from -0.15625 to 0.15625
- in_gain: bfloat16 [2560], P(('fsdp', 'tp')), may hold values from 0.5 to 1.5
- q_gain: bfloat16 [768], P(('fsdp', 'tp')), may hold values from 0.5 to 1.5
- kv_gain: bfloat16 [256], P(('fsdp', 'tp')), may hold values from 0.5 to 1.5
- post_gain: bfloat16 [2560], P(('fsdp', 'tp')), may hold values from 0.5 to 1.5
Outputs:
- layer_out: bfloat16 [8192, 2560], P(('fsdp', 'tp'))
- input_grad: float32 [8192, 2560], P(('fsdp', 'tp'))
- q_down_grad: float32 [2560, 768], P(('fsdp', 'tp'))
- kv_down_grad: float32 [2560, 288], P(('fsdp', 'tp'))
- q_up_grad: float32 [768, 3840], P('fsdp', 'tp')
- kv_up_grad: float32 [256, 5120], P('fsdp', 'tp')
- out_proj_grad: float32 [2560, 2560], P('fsdp', 'tp')
- gate_proj_grad: float32 [2560, 6400], P('fsdp', 'tp')
- up_proj_grad: float32 [2560, 6400], P('fsdp', 'tp')
- down_proj_grad: float32 [2560, 6400], P('fsdp', 'tp')
- in_gain_grad: float32 [2560], P(('fsdp', 'tp'))
- q_gain_grad: float32 [768], P(('fsdp', 'tp'))
- kv_gain_grad: float32 [256], P(('fsdp', 'tp'))
- post_gain_grad: float32 [2560], P(('fsdp', 'tp'))
- q_up_clipped: bfloat16 [768, 3840], P('fsdp', 'tp')
- kv_up_clipped: bfloat16 [256, 5120], P('fsdp', 'tp')
- maxima: float32 [40], P('tp')
- factors: float32 [40], P('tp')
Inputs may be any that keep to these rules, and one draw needn't show every extreme that they name: `seq_ids`: along each row the ids never fall; each row holds two sequences, each of 128 to 384 tokens. `block_ids`: along each row the ids never fall; a block has 1 to 256 tokens and some block of each row has exactly 256.
All inputs are finite; a program needn't handle non-finite values.
Results may differ from a plain program's by a relative error of at most 0.014.
The roundings to bfloat16 on the way count: a program that leaves them out, or rounds other values in their place, can miss the bound.
Values may be sent and summed in bfloat16 or wider, within the bound.
A program may use at most 320 MiB of HBM per device.

v0:
```python
import functools
import math

import jax
import jax.numpy as jnp
from jax import lax
from jax.sharding import PartitionSpec as P

NOPE = 64
ROPE = 32
VD = 64
KVR = 256


eps = 1e-05
resid_scale = 1.4 / math.sqrt(62.0)
rope_base = 10000.0


def rms_scale(value, gain):
    return value * lax.rsqrt(jnp.mean(value * value, axis=-1, keepdims=True) + eps) * gain


def rotate(value, cosine, sine):
    half = value.shape[-1] // 2
    first = value[..., :half]
    second = value[..., half:]
    return jnp.concatenate(
        [first * cosine - second * sine, second * cosine + first * sine], axis=-1
    )


def angles(seq_row, start, count):
    own_ids = lax.dynamic_slice_in_dim(seq_row, start, count)
    earlier = jnp.sum((seq_row[None, :] < own_ids[:, None]).astype(jnp.int32), axis=1)
    place = (start + jnp.arange(count, dtype=jnp.int32) - earlier).astype(jnp.float32)
    freq = jnp.power(rope_base, -jnp.arange(ROPE // 2, dtype=jnp.float32) * (2.0 / ROPE))
    turn = place[:, None] * freq[None, :]
    return (jnp.cos(turn), jnp.sin(turn))


def contract(left, right, left_dim, right_dim):
    return lax.dot_general(
        left, right, (((left_dim,), (right_dim,)), ((), ())), preferred_element_type=jnp.float32
    )


def attend(items, allowed, score_scale):
    query, key_rows, value_rows = items
    raw = jnp.einsum("hqd,hkd->hqk", query, key_rows, preferred_element_type=jnp.float32)
    masked = jnp.where(allowed[None], raw * score_scale, -1e30)
    top = jnp.max(masked, axis=-1, keepdims=True)
    weights = jnp.exp(masked - top)
    total = jnp.sum(weights, axis=-1, keepdims=True)
    mixed = jnp.einsum(
        "hqk,hkd->hqd",
        (weights / total).astype(jnp.bfloat16),
        value_rows,
        preferred_element_type=jnp.float32,
    )
    return (
        mixed.astype(jnp.bfloat16),
        top[..., 0] + jnp.log(total[..., 0]),
        jnp.max(top[..., 0], axis=-1),
    )


def attend_back(items, allowed, score_scale):
    query, key_rows, value_rows, d_mixed, log_total = items
    raw = jnp.einsum("hqd,hkd->hqk", query, key_rows, preferred_element_type=jnp.float32)
    masked = jnp.where(allowed[None], raw * score_scale, -1e30)
    chance = jnp.exp(masked - log_total[..., None])
    d_values = jnp.einsum(
        "hqk,hqd->hkd", chance.astype(jnp.bfloat16), d_mixed, preferred_element_type=jnp.float32
    )
    d_chance = jnp.einsum("hqd,hkd->hqk", d_mixed, value_rows, preferred_element_type=jnp.float32)
    inner = jnp.sum(chance * d_chance, axis=-1, keepdims=True)
    d_raw = (chance * (d_chance - inner) * score_scale).astype(jnp.bfloat16)
    d_query = jnp.einsum("hqk,hkd->hqd", d_raw, key_rows, preferred_element_type=jnp.float32)
    d_key_rows = jnp.einsum("hqk,hqd->hkd", d_raw, query, preferred_element_type=jnp.float32)
    return (d_query, d_key_rows, d_values)


def shards(
    hidden_in,
    seq_ids,
    block_ids,
    clip_limit,
    cotangent,
    q_down,
    kv_down,
    q_up,
    kv_up,
    out_proj,
    gate_proj,
    up_proj,
    down_proj,
    in_gain,
    q_gain,
    kv_gain,
    post_gain,
):
    tokens_here = hidden_in.shape[0]
    seq_row = seq_ids[0]
    block_row = block_ids[0]
    group = seq_row.shape[0]
    heads = q_up.shape[1] // (NOPE + ROPE)
    stride = math.gcd(heads, 4)
    packs = heads // stride
    score_scale = 1.0 / math.sqrt(NOPE + ROPE)
    first_row = lax.axis_index("tp") * tokens_here
    q_down_full, kv_down_full, in_full, post_full, q_gain_full, kv_gain_full = (
        lax.all_gather(q_down, ("fsdp", "tp"), axis=0, tiled=True),
        lax.all_gather(kv_down, ("fsdp", "tp"), axis=0, tiled=True),
        lax.all_gather(in_gain, ("fsdp", "tp"), axis=0, tiled=True),
        lax.all_gather(post_gain, ("fsdp", "tp"), axis=0, tiled=True),
        lax.all_gather(q_gain, ("fsdp", "tp"), axis=0, tiled=True),
        lax.all_gather(kv_gain, ("fsdp", "tp"), axis=0, tiled=True),
    )
    in_float = in_full.astype(jnp.float32)
    post_float = post_full.astype(jnp.float32)
    q_gain_float = q_gain_full.astype(jnp.float32)
    kv_gain_float = kv_gain_full.astype(jnp.float32)
    q_up_full, kv_up_full, out_full, gate_full, up_full, down_full = (
        lax.all_gather(q_up, "fsdp", axis=0, tiled=True),
        lax.all_gather(kv_up, "fsdp", axis=0, tiled=True),
        lax.all_gather(out_proj, "fsdp", axis=0, tiled=True),
        lax.all_gather(gate_proj, "fsdp", axis=0, tiled=True),
        lax.all_gather(up_proj, "fsdp", axis=0, tiled=True),
        lax.all_gather(down_proj, "fsdp", axis=0, tiled=True),
    )
    x_float = hidden_in.astype(jnp.float32)
    x_normed = rms_scale(x_float, in_float).astype(jnp.bfloat16)
    q_pre = jnp.dot(x_normed, q_down_full, preferred_element_type=jnp.float32)
    c_pre = jnp.dot(x_normed, kv_down_full, preferred_element_type=jnp.float32)
    own_cos, own_sin = angles(seq_row, first_row, tokens_here)
    q_latent = rms_scale(q_pre, q_gain_float).astype(jnp.bfloat16)
    kv_latent = rms_scale(c_pre[:, :KVR], kv_gain_float).astype(jnp.bfloat16)
    key_rot = rotate(c_pre[:, KVR:], own_cos, own_sin).astype(jnp.bfloat16)
    q_lat_all, kv_lat_all, key_rot_all = (
        lax.all_gather(q_latent, "tp", axis=0, tiled=True),
        lax.all_gather(kv_latent, "tp", axis=0, tiled=True),
        lax.all_gather(key_rot, "tp", axis=0, tiled=True),
    )
    all_cos, all_sin = angles(seq_row, 0, group)
    q_full = (
        jnp.dot(q_lat_all, q_up_full, preferred_element_type=jnp.float32)
        .reshape(group, heads, NOPE + ROPE)
        .transpose(1, 0, 2)
    )
    kv_full = (
        jnp.dot(kv_lat_all, kv_up_full, preferred_element_type=jnp.float32)
        .reshape(group, heads, NOPE + VD)
        .transpose(1, 0, 2)
    )
    queries = jnp.concatenate(
        [q_full[:, :, :NOPE], rotate(q_full[:, :, NOPE:], all_cos, all_sin)], axis=-1
    ).astype(jnp.bfloat16)
    key_rows = jnp.concatenate(
        [
            kv_full[:, :, :NOPE].astype(jnp.bfloat16),
            jnp.broadcast_to(key_rot_all[None], (heads, group, ROPE)),
        ],
        axis=-1,
    )
    value_rows = kv_full[:, :, NOPE:].astype(jnp.bfloat16)
    allowed = (seq_row[:, None] == seq_row[None, :]) & (block_row[None, :] <= block_row[:, None])
    query_packs = queries.reshape(packs, stride, group, NOPE + ROPE)
    key_packs = key_rows.reshape(packs, stride, group, NOPE + ROPE)
    value_packs = value_rows.reshape(packs, stride, group, VD)
    mixed, log_total, local_peak = lax.map(
        functools.partial(attend, allowed=allowed, score_scale=score_scale),
        (query_packs, key_packs, value_packs),
    )
    attn = mixed.reshape(heads, group, VD).transpose(1, 0, 2).reshape(group, heads * VD)
    branch_part = contract(attn, out_full, 1, 1)
    branch = lax.psum_scatter(branch_part, "tp", scatter_dimension=0, tiled=True)
    mid = x_float + resid_scale * branch
    mid_normed = rms_scale(mid, post_float).astype(jnp.bfloat16)
    mid_all = lax.all_gather(mid_normed, "tp", axis=0, tiled=True)
    gate = jnp.dot(mid_all, gate_full, preferred_element_type=jnp.float32)
    up_value = jnp.dot(mid_all, up_full, preferred_element_type=jnp.float32)
    sigmoid = jax.nn.sigmoid(gate)
    silu_value = gate * sigmoid
    act = (silu_value * up_value).astype(jnp.bfloat16)
    ffn_part = contract(act, down_full, 1, 1)
    ffn = lax.psum_scatter(
        ffn_part.astype(jnp.bfloat16), "tp", scatter_dimension=0, tiled=True
    ).astype(jnp.float32)
    layer_out = (mid + resid_scale * ffn).astype(jnp.bfloat16)
    peaks = lax.pmax(local_peak.reshape(heads), "fsdp")
    limit = clip_limit[0]
    factors = limit / jnp.maximum(peaks, limit)
    root = jnp.sqrt(factors)
    q_cols = jnp.concatenate(
        [
            jnp.broadcast_to(root[:, None], (heads, NOPE)),
            jnp.broadcast_to(factors[:, None], (heads, ROPE)),
        ],
        axis=1,
    ).reshape(heads * (NOPE + ROPE))
    kv_cols = jnp.concatenate(
        [jnp.broadcast_to(root[:, None], (heads, NOPE)), jnp.ones((heads, VD), jnp.float32)], axis=1
    ).reshape(heads * (NOPE + VD))
    q_clipped = (q_up.astype(jnp.float32) * q_cols[None, :]).astype(jnp.bfloat16)
    kv_clipped = (kv_up.astype(jnp.float32) * kv_cols[None, :]).astype(jnp.bfloat16)
    q_up_back, kv_up_back, out_back, gate_back, up_back, down_back = (
        lax.all_gather(q_up, "fsdp", axis=0, tiled=True),
        lax.all_gather(kv_up, "fsdp", axis=0, tiled=True),
        lax.all_gather(out_proj, "fsdp", axis=0, tiled=True),
        lax.all_gather(gate_proj, "fsdp", axis=0, tiled=True),
        lax.all_gather(up_proj, "fsdp", axis=0, tiled=True),
        lax.all_gather(down_proj, "fsdp", axis=0, tiled=True),
    )
    cot_float = cotangent.astype(jnp.float32)
    d_ffn = (resid_scale * cot_float).astype(jnp.bfloat16)
    d_ffn_all = lax.all_gather(d_ffn, "tp", axis=0, tiled=True)
    down_grad = contract(d_ffn_all, act, 0, 0)
    d_act = jnp.dot(d_ffn_all, down_back, preferred_element_type=jnp.float32)
    d_gate = (d_act * up_value * (sigmoid * (1.0 + gate * (1.0 - sigmoid)))).astype(jnp.bfloat16)
    d_up = (d_act * silu_value).astype(jnp.bfloat16)
    gate_grad = contract(mid_all, d_gate, 0, 0)
    up_grad = contract(mid_all, d_up, 0, 0)
    d_mid_part = contract(d_gate, gate_back, 1, 1) + contract(d_up, up_back, 1, 1)
    d_mid_normed = lax.psum_scatter(d_mid_part, "tp", scatter_dimension=0, tiled=True)
    post_pull = jax.vjp(rms_scale, mid, post_float)[1]
    d_mid_norm, post_grad = post_pull(d_mid_normed)
    d_mid = cot_float + d_mid_norm
    d_branch = (resid_scale * d_mid).astype(jnp.bfloat16)
    d_branch_all = lax.all_gather(d_branch, "tp", axis=0, tiled=True)
    out_grad = contract(d_branch_all, attn, 0, 0)
    d_attn = jnp.dot(d_branch_all, out_back, preferred_element_type=jnp.float32).astype(
        jnp.bfloat16
    )
    d_mixed = d_attn.reshape(group, heads, VD).transpose(1, 0, 2).reshape(packs, stride, group, VD)
    d_query, d_key_rows, d_values = lax.map(
        functools.partial(attend_back, allowed=allowed, score_scale=score_scale),
        (query_packs, key_packs, value_packs, d_mixed, log_total),
    )
    d_query = d_query.reshape(heads, group, NOPE + ROPE)
    d_key_rows = d_key_rows.reshape(heads, group, NOPE + ROPE)
    d_values = d_values.reshape(heads, group, VD)
    d_q_rot = rotate(d_query[:, :, NOPE:], all_cos, -all_sin)
    d_q = (
        jnp.concatenate([d_query[:, :, :NOPE], d_q_rot], axis=-1)
        .transpose(1, 0, 2)
        .reshape(group, heads * (NOPE + ROPE))
        .astype(jnp.bfloat16)
    )
    d_key_rot_part = jnp.sum(d_key_rows[:, :, NOPE:], axis=0)
    d_kv = (
        jnp.concatenate([d_key_rows[:, :, :NOPE], d_values], axis=-1)
        .transpose(1, 0, 2)
        .reshape(group, heads * (NOPE + VD))
        .astype(jnp.bfloat16)
    )
    q_up_grad = contract(q_lat_all, d_q, 0, 0)
    kv_up_grad = contract(kv_lat_all, d_kv, 0, 0)
    d_q_lat_part = contract(d_q, q_up_back, 1, 1)
    d_kv_lat_part = contract(d_kv, kv_up_back, 1, 1)
    d_q_latent, d_kv_latent, d_key_rot = (
        lax.psum_scatter(d_q_lat_part, "tp", scatter_dimension=0, tiled=True),
        lax.psum_scatter(d_kv_lat_part, "tp", scatter_dimension=0, tiled=True),
        lax.psum_scatter(d_key_rot_part, "tp", scatter_dimension=0, tiled=True),
    )
    q_pull = jax.vjp(rms_scale, q_pre, q_gain_float)[1]
    d_q_pre_float, q_gain_grad = q_pull(d_q_latent)
    kv_pull = jax.vjp(rms_scale, c_pre[:, :KVR], kv_gain_float)[1]
    d_c_lat, kv_gain_grad = kv_pull(d_kv_latent)
    d_c_pre = jnp.concatenate([d_c_lat, rotate(d_key_rot, own_cos, -own_sin)], axis=-1).astype(
        jnp.bfloat16
    )
    d_q_pre = d_q_pre_float.astype(jnp.bfloat16)
    q_down_grad = contract(x_normed, d_q_pre, 0, 0)
    kv_down_grad = contract(x_normed, d_c_pre, 0, 0)
    d_x_normed = contract(d_q_pre, q_down_full, 1, 1) + contract(d_c_pre, kv_down_full, 1, 1)
    in_pull = jax.vjp(rms_scale, x_float, in_float)[1]
    d_x_norm, in_grad = in_pull(d_x_normed)
    input_grad = d_mid + d_x_norm
    q_down_out, kv_down_out, in_out, post_out, q_gain_out, kv_gain_out = (
        lax.psum_scatter(q_down_grad, ("fsdp", "tp"), scatter_dimension=0, tiled=True),
        lax.psum_scatter(kv_down_grad, ("fsdp", "tp"), scatter_dimension=0, tiled=True),
        lax.psum_scatter(in_grad, ("fsdp", "tp"), scatter_dimension=0, tiled=True),
        lax.psum_scatter(post_grad, ("fsdp", "tp"), scatter_dimension=0, tiled=True),
        lax.psum_scatter(q_gain_grad, ("fsdp", "tp"), scatter_dimension=0, tiled=True),
        lax.psum_scatter(kv_gain_grad, ("fsdp", "tp"), scatter_dimension=0, tiled=True),
    )
    q_up_out, kv_up_out, out_out, gate_out, up_out, down_out = (
        lax.psum_scatter(q_up_grad, "fsdp", scatter_dimension=0, tiled=True),
        lax.psum_scatter(kv_up_grad, "fsdp", scatter_dimension=0, tiled=True),
        lax.psum_scatter(out_grad, "fsdp", scatter_dimension=0, tiled=True),
        lax.psum_scatter(gate_grad, "fsdp", scatter_dimension=0, tiled=True),
        lax.psum_scatter(up_grad, "fsdp", scatter_dimension=0, tiled=True),
        lax.psum_scatter(down_grad, "fsdp", scatter_dimension=0, tiled=True),
    )
    return (
        layer_out,
        input_grad,
        q_down_out,
        kv_down_out,
        q_up_out,
        kv_up_out,
        out_out,
        gate_out,
        up_out,
        down_out,
        in_out,
        q_gain_out,
        kv_gain_out,
        post_out,
        q_clipped,
        kv_clipped,
        peaks,
        factors,
    )


def solution(mesh):
    placed = (
        P(("fsdp", "tp"), None),
        P("fsdp", None),
        P("fsdp", None),
        P(),
        P(("fsdp", "tp"), None),
        P(("fsdp", "tp"), None),
        P(("fsdp", "tp"), None),
        P("fsdp", "tp"),
        P("fsdp", "tp"),
        P("fsdp", "tp"),
        P("fsdp", "tp"),
        P("fsdp", "tp"),
        P("fsdp", "tp"),
        P(("fsdp", "tp")),
        P(("fsdp", "tp")),
        P(("fsdp", "tp")),
        P(("fsdp", "tp")),
    )
    return jax.shard_map(
        shards,
        mesh=mesh,
        in_specs=placed,
        out_specs=(
            P(("fsdp", "tp"), None),
            P(("fsdp", "tp"), None),
            P(("fsdp", "tp"), None),
            P(("fsdp", "tp"), None),
            P("fsdp", "tp"),
            P("fsdp", "tp"),
            P("fsdp", "tp"),
            P("fsdp", "tp"),
            P("fsdp", "tp"),
            P("fsdp", "tp"),
            P(("fsdp", "tp")),
            P(("fsdp", "tp")),
            P(("fsdp", "tp")),
            P(("fsdp", "tp")),
            P("fsdp", "tp"),
            P("fsdp", "tp"),
            P("tp"),
            P("tp"),
        ),
        check_vma=False,
    )
```

profile of v0, /device:TPU:0, one launch (start us, length us, event | category | flops | bytes accessed | tf_op | source)
XLA Modules:
  0.0 4042.7 jit_solution(4682745554615388410)
XLA Ops:
  14.1 42.3 %all-reduce.10 = (bf16[2560]{0:T(1024)(128)(2,1)S(1)}, bf16[768]{0:T(1024)(128)(2,1)S(1)}, bf16[256]{0:T(256)(128)(2,1)S(1)}, bf16[2560]{0:T(1024)(128)(2,1)S(1)}) all-reduce(bf16[2560]{0:T(1024)(128)(2,1)S(1)} %dynamic-update-slice, bf16[768]{0:T(1024)(128)(2,1)S(1)} %dynamic-update-slice.1, ...), channel_id=1, replica_groups=mesh['fsdp'=16,'tp'=2] {'fsdp','tp'}, use_global_device_ids=true, to_apply=%add.1 | all-reduce | flops 6144 | bytes 24576
  75.4 52.8 %all-gather.18.cloned.1.call-done = bf16[256,2560]{1,0:T(8,128)(2,1)} async-done(((bf16[16,2560]{1,0:T(8,128)(2,1)}), bf16[256,2560]{1,0:T(8,128)(2,1)}) %all-gather.18.cloned.1.call-update) | async-done | bytes 1310736 | tf_op jit(solution)/shard_map/all_gather | solution.py:126
  138.1 53.2 %all-gather.12.cloned.1.call-done = bf16[2560,768]{1,0:T(8,128)(2,1)} async-done(((bf16[80,768]{1,0:T(8,128)(2,1)}), bf16[2560,768]{1,0:T(8,128)(2,1)}) %all-gather.12.cloned.1.call-update) | async-done | bytes 3932176 | tf_op jit(solution)/shard_map/all_gather | solution.py:113
  198.4 60.5 %all-gather.14.cloned.1.call-done = bf16[768,1920]{1,0:T(8,128)(2,1)} async-done(((bf16[48,1920]{1,0:T(8,128)(2,1)}), bf16[768,1920]{1,0:T(8,128)(2,1)}) %all-gather.14.cloned.1.call-update) | async-done | bytes 2949136 | tf_op jit(solution)/shard_map/all_gather | solution.py:125
  264.6 40.1 while.30
  304.7 52.5 %all-gather.20.cloned.1.call-done = bf16[2560,1280]{1,0:T(8,128)(2,1)} async-done(((bf16[160,1280]{1,0:T(8,128)(2,1)}), bf16[2560,1280]{1,0:T(8,128)(2,1)}) %all-gather.20.cloned.1.call-update) | async-done | bytes 6553616 | tf_op jit(solution)/shard_map/all_gather | solution.py:127
  366.5 11.5 reduce-scatter.15.cloned.1.call-done
  396.0 192.2 %all-gather.24.cloned.1.call-done = bf16[2560,3200]{1,0:T(8,128)(2,1)} async-done(((bf16[160,3200]{1,0:T(8,128)(2,1)}), bf16[2560,3200]{1,0:T(8,128)(2,1)}) %all-gather.24.cloned.1.call-update) | async-done | bytes 16384016 | tf_op jit(solution)/shard_map/all_gather | solution.py:128
  588.1 15.6 fusion.125
  603.8 173.6 %all-gather.26.cloned.1.call-done = bf16[2560,3200]{1,0:T(8,128)(2,1)} async-done(((bf16[160,3200]{1,0:T(8,128)(2,1)}), bf16[2560,3200]{1,0:T(8,128)(2,1)}) %all-gather.26.cloned.1.call-update) | async-done | bytes 16384016 | tf_op jit(solution)/shard_map/all_gather | solution.py:129
  777.4 15.0 fusion.126
  792.4 188.3 %all-gather.28.cloned.1.call-done = bf16[2560,3200]{1,0:T(8,128)(2,1)} async-done(((bf16[160,3200]{1,0:T(8,128)(2,1)}), bf16[2560,3200]{1,0:T(8,128)(2,1)}) %all-gather.28.cloned.1.call-update) | async-done | bytes 16384016 | tf_op jit(solution)/shard_map/all_gather | solution.py:130
  980.6 21.1 multiply_convert_fusion.1
  1001.7 16.1 fusion.127
  1017.8 14.8 convolution_add_fusion
  1032.7 11.5 reduce-scatter.19.cloned.1.call-done
  1049.7 12.7 all-gather.32.cloned.1.call-done
  1072.4 137.5 %while.31 = (s32[]{:T(128)}, f32[5,4,512,96]{2,3,1,0:T(8,128)}, f32[5,4,512,96]{2,3,1,0:T(8,128)}, bf16[5,4,512,64]{2,3,1,0:T(8,128)(2,1)S(1)}, bf16[5,4,512,96]...) while((s32[]{:T(128)}, f32[5,4,512,96]{2,3,1,0:T(8,128)}, ...), condition=%wide.region_17.18_spmd.clone, body=%wide.region_15.17_spmd.clone.sunk | while | flops 887886848 | bytes 51151992 | solution.py:236
  1225.6 13.6 convolution_convert_fusion
  1266.9 10.5 fusion.132
  1277.9 18.2 fusion.133
  1296.1 17.7 fusion.134
  1314.1 17.9 fusion.135
  1332.8 42.1 %pmax.7 = f32[20]{0:T(128)S(1)} all-reduce(f32[20]{0:T(128)S(1)} %reshape.311), channel_id=1, replica_groups=mesh['fsdp'=16,'tp'=2] {'fsdp'}, use_global_device_ids=true, to_apply=%region_41.42 | all-reduce | flops 20 | bytes 160 | tf_op jit(solution)/shard_map/pmax | solution.py:191
  1383.0 38.7 all-reduce.9
  1430.0 27.9 reduce-scatter.33.cloned.1.call-done
  1457.9 147.0 %reduce-scatter.31.cloned.1.call-done = f32[48,1920]{1,0:T(8,128)} async-done(((f32[768,1920]{1,0:T(8,128)}), f32[48,1920]{1,0:T(8,128)}) %reduce-scatter.31.cloned.1.call-update) | async-done | bytes 368656 | tf_op jit(solution)/shard_map/reduce_scatter | solution.py:289
  1604.9 128.5 %reduce-scatter.27.cloned.1.call-done = f32[80,768]{1,0:T(8,128)} async-done(((f32[2560,768]{1,0:T(8,128)}), f32[80,768]{1,0:T(8,128)}) %reduce-scatter.27.cloned.1.call-update) | async-done | bytes 245776 | tf_op jit(solution)/shard_map/reduce_scatter | solution.py:281
  1733.4 274.8 %reduce-scatter.35.cloned.1.call-done = f32[160,1280]{1,0:T(8,128)} async-done(((f32[2560,1280]{1,0:T(8,128)}), f32[160,1280]{1,0:T(8,128)}) %reduce-scatter.35.cloned.1.call-update) | async-done | bytes 819216 | tf_op jit(solution)/shard_map/reduce_scatter | solution.py:291
  2008.1 675.5 %reduce-scatter.37.cloned.1.call-done = f32[160,3200]{1,0:T(8,128)} async-done(((f32[2560,3200]{1,0:T(8,128)}), f32[160,3200]{1,0:T(8,128)}) %reduce-scatter.37.cloned.1.call-update) | async-done | bytes 2048016 | tf_op jit(solution)/shard_map/reduce_scatter | solution.py:292
  2683.7 676.1 %reduce-scatter.39.cloned.1.call-done = f32[160,3200]{1,0:T(8,128)} async-done(((f32[2560,3200]{1,0:T(8,128)}), f32[160,3200]{1,0:T(8,128)}) %reduce-scatter.39.cloned.1.call-update) | async-done | bytes 2048016 | tf_op jit(solution)/shard_map/reduce_scatter | solution.py:293
  3359.8 676.1 %reduce-scatter.41.cloned.1.call-done = f32[160,3200]{1,0:T(8,128)} async-done(((f32[2560,3200]{1,0:T(8,128)}), f32[160,3200]{1,0:T(8,128)}) %reduce-scatter.41.cloned.1.call-update) | async-done | bytes 2048016 | tf_op jit(solution)/shard_map/reduce_scatter | solution.py:294
  (343 shorter events, 328.1 us)
Async XLA Ops:
  7.2 62.6 %all-gather.16.cloned.1.call-start = ((), (), s32[]{:S(2)}) async-start(), calls=%async_computation.16 | async-start | bytes 2027520 | tf_op jit(solution)/shard_map/all_gather | solution.py:114
  7.9 120.3 %all-gather.18.cloned.1.call-start = ((), (), s32[]{:S(2)}) async-start(), calls=%async_computation.17 | async-start | bytes 1392640 | tf_op jit(solution)/shard_map/all_gather | solution.py:126
  8.7 182.6 %all-gather.12.cloned.1.call-start = ((), (), s32[]{:S(2)}) async-start(), calls=%async_computation.14 | async-start | bytes 4055040 | tf_op jit(solution)/shard_map/all_gather | solution.py:113
  9.4 249.4 %all-gather.14.cloned.1.call-start = ((), (), s32[]{:S(2)}) async-start(), calls=%async_computation.15 | async-start | bytes 3133440 | tf_op jit(solution)/shard_map/all_gather | solution.py:125
  10.0 347.2 %all-gather.20.cloned.1.call-start = ((), (), s32[]{:S(2)}) async-start(), calls=%async_computation.18 | async-start | bytes 6963200 | tf_op jit(solution)/shard_map/all_gather | solution.py:127
  10.6 367.5 %reduce-scatter.15.cloned.1.call-start = ((), (), s32[]{:S(2)}) async-start(), calls=%async_computation.19 | async-start | bytes 7864320 | tf_op jit(solution)/shard_map/reduce_scatter | solution.py:177
  56.4 134.8 %copy-start.23 = (f32[2560]{0:T(1024)}, f32[2560]{0:T(1024)S(1)}, u32[]{:S(2)}) copy-start(f32[2560]{0:T(1024)S(1)} %convert_element_type.125) | copy-start | bytes 30724
  58.1 133.2 %copy-start.33 = (f32[256]{0:T(256)}, f32[256]{0:T(256)S(1)}, u32[]{:S(2)}) copy-start(f32[256]{0:T(256)S(1)} %fusion.108) | copy-start | bytes 3076
  58.1 136.6 %copy-start.31 = (f32[768]{0:T(1024)}, f32[768]{0:T(1024)S(1)}, u32[]{:S(2)}) copy-start(f32[768]{0:T(1024)S(1)} %convert_element_type.127) | copy-start | bytes 9220
  61.6 201.3 %copy-start.28 = (f32[512,16]{0,1:T(8,128)}, f32[512,16]{0,1:T(8,128)S(1)}, u32[]{:S(2)}) copy-start(f32[512,16]{0,1:T(8,128)S(1)} %get-tuple-element.251) | copy-start | bytes 98308
  366.4 29.5 all-gather.22.cloned.1.call-start
  366.5 680.9 %copy-start.26 = (f32[2560]{0:T(1024)}, f32[2560]{0:T(1024)S(1)}, u32[]{:S(2)}) copy-start(f32[2560]{0:T(1024)S(1)} %convert_element_type.135) | copy-start | bytes 30724
  380.3 667.1 %copy-start.36 = (f32[256]{0:T(256)}, f32[256]{0:T(256)S(1)}, u32[]{:S(2)}) copy-start(f32[256]{0:T(256)S(1)} %fusion.111) | copy-start | bytes 3076
  383.2 204.9 %all-gather.24.cloned.1.call-start = ((), (), s32[]{:S(2)}) async-start(), calls=%async_computation.21 | async-start | bytes 17408000 | tf_op jit(solution)/shard_map/all_gather | solution.py:128
  384.0 393.4 %all-gather.26.cloned.1.call-start = ((), (), s32[]{:S(2)}) async-start(), calls=%async_computation.22 | async-start | bytes 17408000 | tf_op jit(solution)/shard_map/all_gather | solution.py:129
  384.7 407.7 %all-gather.30.cloned.1.call-start = ((), (), s32[]{:S(2)}) async-start(), calls=%async_computation.25 | async-start | bytes 3932160 | tf_op jit(solution)/shard_map/all_gather | solution.py:217
  386.1 594.6 %all-gather.28.cloned.1.call-start = ((), (), s32[]{:S(2)}) async-start(), calls=%async_computation.23 | async-start | bytes 17408000 | tf_op jit(solution)/shard_map/all_gather | solution.py:130
  386.8 657.4 %reduce-scatter.19.cloned.1.call-start = ((), (), s32[]{:S(2)}) async-start(), calls=%async_computation.26 | async-start | bytes 7864320 | tf_op jit(solution)/shard_map/reduce_scatter | solution.py:225
  396.0 381.4 %copy-start.60 = (bf16[512,2560]{1,0:T(8,128)(2,1)S(1)}, bf16[512,2560]{1,0:T(8,128)(2,1)}, u32[]{:S(2)}) copy-start(bf16[512,2560]{1,0:T(8,128)(2,1)} %all-gather.22.cloned.1.call-done) | copy-start | bytes 7864324
  1032.7 29.7 all-gather.32.cloned.1.call-start
  1049.6 190.0 %reduce-scatter.25.cloned.1.call-start = ((), (), s32[]{:S(2)}) async-start(), calls=%async_computation.30 | async-start | bytes 98304 | tf_op jit(solution)/shard_map/reduce_scatter | solution.py:264
  1213.9 26.9 reduce-scatter.23.cloned.1.call-start
  1217.4 41.1 %reduce-scatter.21.cloned.1.call-start = ((), (), s32[]{:S(2)}) async-start(), calls=%async_computation.28 | async-start | bytes 2359296 | tf_op jit(solution)/shard_map/reduce_scatter | solution.py:262
  1225.5 198.6 %reduce-scatter.17.cloned.1.call-start = ((), (), s32[]{:S(2)}) async-start(), calls=%async_computation.24 | async-start | bytes 3932160 | tf_op jit(solution)/shard_map/reduce_scatter | solution.py:187
  1239.3 190.7 %reduce-scatter.29.cloned.1.call-start = ((), (), s32[]{:S(2)}) async-start(), calls=%async_computation.32 | async-start | bytes 4055040 | tf_op jit(solution)/shard_map/reduce_scatter | solution.py:282
  1245.9 212.0 %reduce-scatter.33.cloned.1.call-start = ((), (), s32[]{:S(2)}) async-start(), calls=%async_computation.34 | async-start | bytes 2785280 | tf_op jit(solution)/shard_map/reduce_scatter | solution.py:290
  1251.1 353.8 %reduce-scatter.31.cloned.1.call-start = ((), (), s32[]{:S(2)}) async-start(), calls=%async_computation.33 | async-start | bytes 6266880 | tf_op jit(solution)/shard_map/reduce_scatter | solution.py:289
  1258.5 474.9 %reduce-scatter.27.cloned.1.call-start = ((), (), s32[]{:S(2)}) async-start(), calls=%async_computation.31 | async-start | bytes 8110080 | tf_op jit(solution)/shard_map/reduce_scatter | solution.py:281
  1266.8 741.3 %reduce-scatter.35.cloned.1.call-start = ((), (), s32[]{:S(2)}) async-start(), calls=%async_computation.35 | async-start | bytes 13926400 | tf_op jit(solution)/shard_map/reduce_scatter | solution.py:291
  1277.4 1406.3 %reduce-scatter.37.cloned.1.call-start = ((), (), s32[]{:S(2)}) async-start(), calls=%async_computation.36 | async-start | bytes 34816000 | tf_op jit(solution)/shard_map/reduce_scatter | solution.py:292
  1296.1 2063.7 %reduce-scatter.39.cloned.1.call-start = ((), (), s32[]{:S(2)}) async-start(), calls=%async_computation.37 | async-start | bytes 34816000 | tf_op jit(solution)/shard_map/reduce_scatter | solution.py:293
  1313.9 2722.1 %reduce-scatter.41.cloned.1.call-start = ((), (), s32[]{:S(2)}) async-start(), calls=%async_computation.38 | async-start | bytes 34816000 | tf_op jit(solution)/shard_map/reduce_scatter | solution.py:294
  (56 other events, 857.8 us)
Sparse Core Ops, SparseCore 0:
  10.9 58.7 all-gather.15
  72.5 55.6 all-gather.17
  131.1 60.0 all-gather.11
  193.9 64.9 all-gather.13
  261.4 95.7 all-gather.19
  366.6 11.4 reduce-scatter.14
  383.3 12.5 all-gather.21
  399.0 189.0 all-gather.23
  591.2 186.1 all-gather.25
  778.8 9.5 all-gather.29
  791.5 189.0 all-gather.27
  1032.8 11.3 reduce-scatter.18
  1049.7 12.5 all-gather.31
  1214.0 8.6 reduce-scatter.24
  1225.3 9.0 reduce-scatter.22
  1237.2 10.2 reduce-scatter.20
  1249.6 11.3 reduce-scatter.16
  1267.7 105.1 reduce-scatter.28
  1375.9 81.8 reduce-scatter.32
  1464.4 140.4 reduce-scatter.30
  1612.1 121.2 reduce-scatter.26
  1736.3 271.8 reduce-scatter.34
  2011.1 672.5 reduce-scatter.36
  2686.6 673.1 reduce-scatter.38
  3362.8 673.1 reduce-scatter.40
where the time goes:
time: 4050 us; the launch traced here: 4040 us
  waiting for transfers between devices  3440 us (85%)
  matrix products  380 us (9%)
  blocking collectives  130 us (3%)
  other arithmetic  44 us (1%)
    reduce_scatter x1, waiting for transfers between devices, shards(): lax.psum_scatter(down_grad, 'fsdp', scatter_dimension=0, tiled=True)  676 us
    reduce_scatter x1, waiting for transfers between devices, shards(): lax.psum_scatter(up_grad, 'fsdp', scatter_dimension=0, tiled=True)  676 us
    reduce_scatter x1, waiting for transfers between devices, shards(): lax.psum_scatter(gate_grad, 'fsdp', scatter_dimension=0, tiled=True)  676 us
    reduce_scatter x1, waiting for transfers between devices, shards(): lax.psum_scatter(out_grad, 'fsdp', scatter_dimension=0, tiled=True)  275 us
    all_gather x1, waiting for transfers between devices, shards(): lax.all_gather(gate_proj, 'fsdp', axis=0, tiled=True)  192 us
    all_gather x1, waiting for transfers between devices, shards(): lax.all_gather(down_proj, 'fsdp', axis=0, tiled=True)  188 us
    all_gather x1, waiting for transfers between devices, shards(): lax.all_gather(up_proj, 'fsdp', axis=0, tiled=True)  174 us
    reduce_scatter x1, waiting for transfers between devices, shards(): lax.psum_scatter(q_up_grad, 'fsdp', scatter_dimension=0, tiled=True)  147 us
  transfers between devices with their start and end apart: 25, of which 19 were waited for; matrix products, arithmetic and copies ran while one was open for 6% of the time, Pallas kernels for 0%

commit v1 on v0

v1 whole, which is shorter than its diff:
```python
import functools
import math

import jax
import jax.numpy as jnp
from jax import lax
from jax.sharding import Mesh
from jax.sharding import PartitionSpec as P

NOPE = 64
ROPE = 32
VD = 64
KVR = 256


eps = 1e-05
resid_scale = 1.4 / math.sqrt(62.0)
rope_base = 10000.0
SWAP = [(0, 1), (1, 0)]
f32 = jnp.float32
bf16 = jnp.bfloat16


def rms_scale(value, gain):
    return value * lax.rsqrt(jnp.mean(value * value, axis=-1, keepdims=True) + eps) * gain


def rotate(value, cosine, sine):
    half = value.shape[-1] // 2
    first = value[..., :half]
    second = value[..., half:]
    return jnp.concatenate(
        [first * cosine - second * sine, second * cosine + first * sine], axis=-1
    )


def angles(seq_row, start, count):
    own_ids = lax.dynamic_slice_in_dim(seq_row, start, count)
    earlier = jnp.sum((seq_row[None, :] < own_ids[:, None]).astype(jnp.int32), axis=1)
    place = (start + jnp.arange(count, dtype=jnp.int32) - earlier).astype(f32)
    freq = jnp.power(rope_base, -jnp.arange(ROPE // 2, dtype=f32) * (2.0 / ROPE))
    turn = place[:, None] * freq[None, :]
    return (jnp.cos(turn), jnp.sin(turn))


def contract(left, right, left_dim, right_dim):
    return lax.dot_general(
        left, right, (((left_dim,), (right_dim,)), ((), ())), preferred_element_type=f32
    )


def attend(items, allowed, score_scale):
    query, key_rows, value_rows = items
    raw = jnp.einsum("hqd,hkd->hqk", query, key_rows, preferred_element_type=f32)
    masked = jnp.where(allowed[None], raw * score_scale, -1e30)
    top = jnp.max(masked, axis=-1, keepdims=True)
    weights = jnp.exp(masked - top)
    total = jnp.sum(weights, axis=-1, keepdims=True)
    mixed = jnp.einsum(
        "hqk,hkd->hqd",
        (weights / total).astype(bf16),
        value_rows,
        preferred_element_type=f32,
    )
    return (
        mixed.astype(bf16),
        top[..., 0] + jnp.log(total[..., 0]),
        jnp.max(top[..., 0], axis=-1),
    )


def attend_back(items, allowed, score_scale):
    query, key_rows, value_rows, d_mixed, log_total = items
    raw = jnp.einsum("hqd,hkd->hqk", query, key_rows, preferred_element_type=f32)
    masked = jnp.where(allowed[None], raw * score_scale, -1e30)
    chance = jnp.exp(masked - log_total[..., None])
    d_values = jnp.einsum("hqk,hqd->hkd", chance.astype(bf16), d_mixed, preferred_element_type=f32)
    d_chance = jnp.einsum("hqd,hkd->hqk", d_mixed, value_rows, preferred_element_type=f32)
    inner = jnp.sum(chance * d_chance, axis=-1, keepdims=True)
    d_raw = (chance * (d_chance - inner) * score_scale).astype(bf16)
    d_query = jnp.einsum("hqk,hkd->hqd", d_raw, key_rows, preferred_element_type=f32)
    d_key_rows = jnp.einsum("hqk,hqd->hkd", d_raw, query, preferred_element_type=f32)
    return (d_query, d_key_rows, d_values)


def swap(value, axis):
    return lax.ppermute(value, axis, SWAP)


def pick(value, at, dim):
    return lax.dynamic_index_in_dim(value, at, dim, keepdims=True)


def both(own, other, axis, dim):
    here = lax.axis_index(axis) == 0
    return jnp.concatenate([jnp.where(here, own, other), jnp.where(here, other, own)], axis=dim)


def gather(block, axes, order):
    held = block.reshape((1,) * len(axes) + block.shape)
    for axis in order:
        held = both(held, swap(held, axis), axis, axes.index(axis))
    return held.reshape((-1,) + block.shape[1:])


def scatter(total, axes, order, rows):
    held = total.reshape((2,) * len(axes) + (rows,) + total.shape[1:])
    for axis in order:
        at = lax.axis_index(axis)
        dim = axes.index(axis)
        sent = pick(held, 1 - at, dim).astype(bf16)
        held = pick(held, at, dim).astype(f32) + swap(sent, axis).astype(f32)
    return held.reshape((rows,) + total.shape[1:])


def shards(
    fsdp,
    hidden_in,
    seq_ids,
    block_ids,
    clip_limit,
    cotangent,
    q_down,
    kv_down,
    q_up,
    kv_up,
    out_proj,
    gate_proj,
    up_proj,
    down_proj,
    in_gain,
    q_gain,
    kv_gain,
    post_gain,
):
    tokens_here, width = hidden_in.shape
    seq_row = seq_ids[0]
    block_row = block_ids[0]
    group = seq_row.shape[0]
    heads = q_up.shape[1] // (NOPE + ROPE)
    stride = math.gcd(heads, 4)
    packs = heads // stride
    score_scale = 1.0 / math.sqrt(NOPE + ROPE)
    first_row = lax.axis_index("c") * tokens_here
    wide, near = fsdp[1], fsdp[-1]
    pair = (wide, near)
    spread = [axis for axis in fsdp if axis not in pair]
    at_wide, at_near = lax.axis_index(wide), lax.axis_index(near)
    diagonal = [(i, 3 - i) for i in range(4)]
    every = fsdp + ["c"]
    out_order = list(fsdp)
    back_order = list(reversed(fsdp))

    small_rows = q_down.shape[0]
    small_cols = q_down.shape[1] + kv_down.shape[1]

    def column(value):
        return jnp.pad(value, (0, small_rows - value.shape[0]))[:, None]

    small = jnp.concatenate(
        [q_down, kv_down, column(in_gain), column(post_gain), column(q_gain), column(kv_gain)],
        axis=1,
    )
    small = jnp.pad(small, ((0, 0), (0, -small.shape[1] % 128)))
    small_full = gather(small, every, every)
    devices = small_full.shape[0] // small_rows

    def gain(at, count):
        return (
            small_full[:, small_cols + at].reshape(devices, small_rows)[:, :count].reshape(-1)
        ).astype(f32)

    in_float = gain(0, in_gain.shape[0])
    post_float = gain(1, post_gain.shape[0])
    q_gain_float = gain(2, q_gain.shape[0])
    kv_gain_float = gain(3, kv_gain.shape[0])
    down_full = small_full[:, :small_cols]

    q_up_full = gather(q_up, fsdp, out_order)
    kv_up_full = gather(kv_up, fsdp, out_order)
    out_full = gather(out_proj, fsdp, out_order)

    def columns_of_chip(weight):
        rows, cols = weight.shape
        parts = weight.reshape(rows, 2, 2, cols // 4).transpose(1, 2, 0, 3)

        def part(w, n):
            return pick(pick(parts, w, 0), n, 1)

        own = part(at_wide, at_near)
        from_near = swap(part(at_wide, 1 - at_near), near)
        from_wide = swap(part(1 - at_wide, at_near), wide)
        from_far = lax.ppermute(part(1 - at_wide, 1 - at_near), pair, diagonal)
        held = both(both(own, from_near, near, 1), both(from_wide, from_far, near, 1), wide, 0)
        shape = [2 if axis in pair else 1 for axis in fsdp]
        held = held.reshape(shape + [rows, cols // 4])
        for axis in spread:
            held = both(held, swap(held, axis), axis, fsdp.index(axis))
        return held.reshape(-1, cols // 4)

    def rows_of_device(total):
        cols = total.shape[1]
        rows = total.shape[0] // 2 ** len(fsdp)
        held = total.reshape([2] * len(fsdp) + [rows, cols])
        for axis in reversed(spread):
            at = lax.axis_index(axis)
            dim = fsdp.index(axis)
            sent = pick(held, 1 - at, dim).astype(bf16)
            held = pick(held, at, dim).astype(f32) + swap(sent, axis).astype(f32)
        parts = held.reshape(2, 2, rows, cols)

        def part(w, n):
            return pick(pick(parts, w, 0), n, 1).astype(bf16)

        own = pick(pick(parts, at_wide, 0), at_near, 1)
        from_near = swap(part(at_wide, 1 - at_near), near).astype(f32)
        from_wide = swap(part(1 - at_wide, at_near), wide).astype(f32)
        from_far = lax.ppermute(part(1 - at_wide, 1 - at_near), pair, diagonal).astype(f32)
        held = both(both(own, from_near, near, 1), both(from_wide, from_far, near, 1), wide, 0)
        return held.transpose(2, 0, 1, 3).reshape(rows, 4 * cols)

    def tokens_of_chips(value):
        chips = [
            value,
            swap(value, near),
            swap(value, wide),
            lax.ppermute(value, pair, diagonal),
        ]
        return jnp.concatenate(chips + [swap(rows, "c") for rows in chips], axis=0)

    def sum_of_chips(value):
        half = value.shape[0] // 2
        other = swap(value[half:].astype(bf16), "c")
        held = (value[:half] + other.astype(f32)).reshape(4, tokens_here, -1)
        sent = held[1:].astype(bf16)
        return (
            held[0]
            + swap(sent[0], near).astype(f32)
            + swap(sent[1], wide).astype(f32)
            + lax.ppermute(sent[2], pair, diagonal).astype(f32)
        )

    def core_both(value):
        return both(value, swap(value, "c"), "c", 0)

    def core_sum(value):
        at = lax.axis_index("c")
        held = value.reshape(2, tokens_here, -1)
        return (pick(held, at, 0) + swap(pick(held, 1 - at, 0), "c"))[0]

    cot_float = cotangent.astype(f32)
    d_ffn = (resid_scale * cot_float).astype(bf16)

    gate_full = columns_of_chip(gate_proj)
    up_full = columns_of_chip(up_proj)
    down_proj_full = columns_of_chip(down_proj)
    d_ffn_all = tokens_of_chips(d_ffn)

    x_float = hidden_in.astype(f32)
    x_normed = rms_scale(x_float, in_float).astype(bf16)
    pre = jnp.dot(x_normed, down_full, preferred_element_type=f32)
    q_rank = q_down.shape[1]
    q_pre = pre[:, :q_rank]
    c_lat_pre = pre[:, q_rank : q_rank + KVR]
    c_rot_pre = pre[:, q_rank + KVR :]
    own_cos, own_sin = angles(seq_row, first_row, tokens_here)
    q_latent = rms_scale(q_pre, q_gain_float).astype(bf16)
    kv_latent = rms_scale(c_lat_pre, kv_gain_float).astype(bf16)
    key_rot = rotate(c_rot_pre, own_cos, own_sin).astype(bf16)
    latents = core_both(jnp.concatenate([q_latent, kv_latent, key_rot], axis=1))
    q_lat_all = latents[:, :q_rank]
    kv_lat_all = latents[:, q_rank : q_rank + KVR]
    key_rot_all = latents[:, q_rank + KVR :]
    all_cos, all_sin = angles(seq_row, 0, group)
    q_full = (
        jnp.dot(q_lat_all, q_up_full, preferred_element_type=f32)
        .reshape(group, heads, NOPE + ROPE)
        .transpose(1, 0, 2)
    )
    kv_full = (
        jnp.dot(kv_lat_all, kv_up_full, preferred_element_type=f32)
        .reshape(group, heads, NOPE + VD)
        .transpose(1, 0, 2)
    )
    queries = jnp.concatenate(
        [q_full[:, :, :NOPE], rotate(q_full[:, :, NOPE:], all_cos, all_sin)], axis=-1
    ).astype(bf16)
    key_rows = jnp.concatenate(
        [
            kv_full[:, :, :NOPE].astype(bf16),
            jnp.broadcast_to(key_rot_all[None], (heads, group, ROPE)),
        ],
        axis=-1,
    )
    value_rows = kv_full[:, :, NOPE:].astype(bf16)
    allowed = (seq_row[:, None] == seq_row[None, :]) & (block_row[None, :] <= block_row[:, None])
    query_packs = queries.reshape(packs, stride, group, NOPE + ROPE)
    key_packs = key_rows.reshape(packs, stride, group, NOPE + ROPE)
    value_packs = value_rows.reshape(packs, stride, group, VD)
    mixed, log_total, local_peak = lax.map(
        functools.partial(attend, allowed=allowed, score_scale=score_scale),
        (query_packs, key_packs, value_packs),
    )
    attn = mixed.reshape(heads, group, VD).transpose(1, 0, 2).reshape(group, heads * VD)
    branch = core_sum(contract(attn, out_full, 1, 1))
    mid = x_float + resid_scale * branch
    mid_normed = rms_scale(mid, post_float).astype(bf16)
    mid_all = tokens_of_chips(mid_normed)
    gate = jnp.dot(mid_all, gate_full, preferred_element_type=f32)
    up_value = jnp.dot(mid_all, up_full, preferred_element_type=f32)
    sigmoid = jax.nn.sigmoid(gate)
    silu_value = gate * sigmoid
    act = (silu_value * up_value).astype(bf16)
    ffn = sum_of_chips(contract(act, down_proj_full, 1, 1))
    layer_out = (mid + resid_scale * ffn).astype(bf16)

    peaks = local_peak.reshape(heads)
    for axis in fsdp:
        peaks = jnp.maximum(peaks, swap(peaks, axis))
    limit = clip_limit[0]
    factors = limit / jnp.maximum(peaks, limit)
    root = jnp.sqrt(factors)
    q_cols = jnp.concatenate(
        [
            jnp.broadcast_to(root[:, None], (heads, NOPE)),
            jnp.broadcast_to(factors[:, None], (heads, ROPE)),
        ],
        axis=1,
    ).reshape(heads * (NOPE + ROPE))
    kv_cols = jnp.concatenate(
        [jnp.broadcast_to(root[:, None], (heads, NOPE)), jnp.ones((heads, VD), f32)], axis=1
    ).reshape(heads * (NOPE + VD))
    q_clipped = (q_up.astype(f32) * q_cols[None, :]).astype(bf16)
    kv_clipped = (kv_up.astype(f32) * kv_cols[None, :]).astype(bf16)

    d_act = jnp.dot(d_ffn_all, down_proj_full, preferred_element_type=f32)
    d_gate = (d_act * up_value * (sigmoid * (1.0 + gate * (1.0 - sigmoid)))).astype(bf16)
    d_up = (d_act * silu_value).astype(bf16)
    d_mid_normed = sum_of_chips(contract(d_gate, gate_full, 1, 1) + contract(d_up, up_full, 1, 1))
    down_out = rows_of_device(contract(d_ffn_all, act, 0, 0))
    gate_out = rows_of_device(contract(mid_all, d_gate, 0, 0))
    up_out = rows_of_device(contract(mid_all, d_up, 0, 0))
    post_pull = jax.vjp(rms_scale, mid, post_float)[1]
    d_mid_norm, post_grad = post_pull(d_mid_normed)
    d_mid = cot_float + d_mid_norm
    d_branch = (resid_scale * d_mid).astype(bf16)
    d_branch_all = core_both(d_branch)
    out_grad = contract(d_branch_all, attn, 0, 0)
    out_out = scatter(out_grad, fsdp, back_order, out_proj.shape[0])
    d_attn = jnp.dot(d_branch_all, out_full, preferred_element_type=f32).astype(bf16)
    d_mixed = d_attn.reshape(group, heads, VD).transpose(1, 0, 2).reshape(packs, stride, group, VD)
    d_query, d_key_rows, d_values = lax.map(
        functools.partial(attend_back, allowed=allowed, score_scale=score_scale),
        (query_packs, key_packs, value_packs, d_mixed, log_total),
    )
    d_query = d_query.reshape(heads, group, NOPE + ROPE)
    d_key_rows = d_key_rows.reshape(heads, group, NOPE + ROPE)
    d_values = d_values.reshape(heads, group, VD)
    d_q_rot = rotate(d_query[:, :, NOPE:], all_cos, -all_sin)
    d_q = (
        jnp.concatenate([d_query[:, :, :NOPE], d_q_rot], axis=-1)
        .transpose(1, 0, 2)
        .reshape(group, heads * (NOPE + ROPE))
        .astype(bf16)
    )
    d_key_rot_part = jnp.sum(d_key_rows[:, :, NOPE:], axis=0)
    d_kv = (
        jnp.concatenate([d_key_rows[:, :, :NOPE], d_values], axis=-1)
        .transpose(1, 0, 2)
        .reshape(group, heads * (NOPE + VD))
        .astype(bf16)
    )
    q_up_grad = contract(q_lat_all, d_q, 0, 0)
    kv_up_grad = contract(kv_lat_all, d_kv, 0, 0)
    q_up_out = scatter(q_up_grad, fsdp, back_order, q_up.shape[0])
    kv_up_out = scatter(kv_up_grad, fsdp, back_order, kv_up.shape[0])
    d_q_lat_part = contract(d_q, q_up_full, 1, 1)
    d_kv_lat_part = contract(d_kv, kv_up_full, 1, 1)
    d_latents = core_sum(
        jnp.concatenate([d_q_lat_part, d_kv_lat_part, d_key_rot_part], axis=1)
    )
    q_pull = jax.vjp(rms_scale, q_pre, q_gain_float)[1]
    d_q_pre, q_gain_grad = q_pull(d_latents[:, :q_rank])
    kv_pull = jax.vjp(rms_scale, c_lat_pre, kv_gain_float)[1]
    d_c_lat, kv_gain_grad = kv_pull(d_latents[:, q_rank : q_rank + KVR])
    d_pre = jnp.concatenate(
        [d_q_pre, d_c_lat, rotate(d_latents[:, q_rank + KVR :], own_cos, -own_sin)], axis=-1
    ).astype(bf16)
    down_grads = contract(x_normed, d_pre, 0, 0)
    d_x_normed = contract(d_pre, down_full, 1, 1)
    in_pull = jax.vjp(rms_scale, x_float, in_float)[1]
    d_x_norm, in_grad = in_pull(d_x_normed)
    input_grad = d_mid + d_x_norm

    def spread_out(value):
        rows = value.reshape(devices, -1)
        return jnp.pad(rows, ((0, 0), (0, small_rows - rows.shape[1]))).reshape(-1, 1)

    small_grads = jnp.concatenate(
        [
            down_grads,
            spread_out(in_grad),
            spread_out(post_grad),
            spread_out(q_gain_grad),
            spread_out(kv_gain_grad),
        ],
        axis=1,
    )
    small_out = scatter(small_grads, every, ["c"] + back_order, small_rows)
    return (
        layer_out,
        input_grad,
        small_out[:, :q_rank],
        small_out[:, q_rank:small_cols],
        q_up_out,
        kv_up_out,
        out_out,
        gate_out,
        up_out,
        down_out,
        small_out[: in_gain.shape[0], small_cols],
        small_out[: q_gain.shape[0], small_cols + 2],
        small_out[: kv_gain.shape[0], small_cols + 3],
        small_out[: post_gain.shape[0], small_cols + 1],
        q_clipped,
        kv_clipped,
        peaks,
        factors,
    )


def solution(mesh):
    bits = mesh.shape["fsdp"].bit_length() - 1
    fsdp = [f"f{i}" for i in range(bits)]
    fine = Mesh(mesh.devices.reshape((2,) * (bits + 1)), tuple(fsdp) + ("c",))
    split = tuple(fsdp)
    whole = split + ("c",)
    return jax.shard_map(
        functools.partial(shards, fsdp),
        mesh=fine,
        in_specs=(
            P(whole, None),
            P(split, None),
            P(split, None),
            P(),
            P(whole, None),
            P(whole, None),
            P(whole, None),
            P(split, "c"),
            P(split, "c"),
            P(split, "c"),
            P(split, "c"),
            P(split, "c"),
            P(split, "c"),
            P(whole),
            P(whole),
            P(whole),
            P(whole),
        ),
        out_specs=(
            P(whole, None),
            P(whole, None),
            P(whole, None),
            P(whole, None),
            P(split, "c"),
            P(split, "c"),
            P(split, "c"),
            P(split, "c"),
            P(split, "c"),
            P(split, "c"),
            P(whole),
            P(whole),
            P(whole),
            P(whole),
            P(split, "c"),
            P(split, "c"),
            P("c"),
            P("c"),
        ),
        check_vma=False,
    )
```

time: 4050 us -> 1520 us (0.38)
  waiting for transfers between devices: 3440 us -> 669 us
  local copies, waits for them, and re-layouts: 34 us -> 216 us
  blocking collectives: 130 us -> 0 us
  other arithmetic: 44 us -> 172 us
  starting transfers between devices: 2.01 us -> 90.1 us
    reduce_scatter x14 -> x0, waiting for transfers between devices: 2630 us -> none  [the longest x1 676 us: shards(): lax.psum_scatter(down_grad, 'fsdp', scatter_dimension=0, tiled=True)]
    all_gather x11 -> x0, waiting for transfers between devices: 803 us -> none  [the longest x1 192 us: shards(): lax.all_gather(gate_proj, 'fsdp', axis=0, tiled=True)]
    ppermute x0 -> x94, waiting for transfers between devices: none -> 669 us  [the longest x84 619 us: swap(): return lax.ppermute(value, axis, SWAP)]
    ppermute x0 -> x94, starting transfers between devices: none -> 90.1 us  [the longest x84 74.1 us: swap(): return lax.ppermute(value, axis, SWAP)]
    unnamed x2 -> x0, blocking collectives: 81 us -> none
    unnamed x138 -> x349, local copies, waits for them, and re-layouts: 15.2 us -> 59.7 us
    pmax x1 -> x0, blocking collectives: 42.1 us -> none  [shards(): peaks = lax.pmax(local_peak.reshape(heads), 'fsdp')]
    dot_general x16 -> x14, matrix products: 146 us -> 134 us  [contract(): lax.dot_general(left, right, (((left_dim,), (right_dim,)), ((), ())), pre...]
  transfers between devices with their start and end apart: 25 -> 94, of which waited for: 19 -> 42; matrix products, arithmetic and copies ran while one was open for 6% -> 41% of each run, Pallas kernels for 0% -> 0%
where the time goes in v1:
time: 1520 us; the launch traced here: 1510 us
  waiting for transfers between devices  669 us (44%)
  matrix products  363 us (24%)
  local copies, waits for them, and re-layouts  216 us (14%)
  other arithmetic  172 us (11%)
  starting transfers between devices  90.1 us (6%)
    ppermute x84, waiting for transfers between devices, swap(): return lax.ppermute(value, axis, SWAP)  619 us
    dot_general x14, matrix products, contract(): lax.dot_general(left, right, (((left_dim,), (right_dim,)), ((), ())), pre...  134 us
    ppermute x84, starting transfers between devices, swap(): return lax.ppermute(value, axis, SWAP)  74.1 us
    unnamed x349, local copies, waits for them, and re-layouts  59.7 us
    dot_general x5, matrix products, attend_back(): jnp.einsum('hqk,hkd->hqd', d_raw, key_rows, preferred_element_type=f32)  40.9 us
    dot_general x5, matrix products, attend_back(): jnp.einsum('hqk,hqd->hkd', d_raw, query, preferred_element_type=f32)  40.8 us
  transfers between devices with their start and end apart: 94, of which 42 were waited for; matrix products, arithmetic and copies ran while one was open for 41% of the time, Pallas kernels for 0%

profile of v1, /device:TPU:0, one launch (start us, length us, event | category | flops | bytes accessed | tf_op | source)
XLA Modules:
  0.0 1514.5 jit_solution(10159352397066586865)
XLA Ops:
  138.9 49.2 %collective-permute-done.15 = bf16[2,1,1,1,160,1280]{5,4,3,2,1,0:T(8,128)(2,1)} collective-permute-done((bf16[2,1,1,1,160,1280]{5,4,3,2,1,0:T(8,128)(2,1)}, bf16[2,1,1,1,160,1280]{5,4,3,2,1,0:T(8,128)(2,1)}, u32[]{:S(2)}, u32[]{:S(2)}) %collective-permute-start.15) | collective-permute-done | bytes 819232 | tf_op jit(solution)/shard_map/ppermute | solution.py:87
  191.1 26.8 %collective-permute-done.34 = bf16[1,2,1,2,160,800]{5,4,3,1,2,0:T(8,128)(2,1)} collective-permute-done((bf16[1,2,1,2,160,800]{5,4,3,1,2,0:T(8,128)(2,1)}, bf16[1,2,1,2,160,800]{5,4,3,1,2,0:T(8,128)(2,1)}, u32[]{:S(2)}, u32[]{:S(2)}) %collective-permute-start.34) | collective-permute-done | bytes 1024032 | tf_op jit(solution)/shard_map/ppermute | solution.py:87
  218.4 24.1 %collective-permute-done.39 = bf16[1,2,1,2,160,800]{5,4,3,1,2,0:T(8,128)(2,1)} collective-permute-done((bf16[1,2,1,2,160,800]{5,4,3,1,2,0:T(8,128)(2,1)}, bf16[1,2,1,2,160,800]{5,4,3,1,2,0:T(8,128)(2,1)}, u32[]{:S(2)}, u32[]{:S(2)}) %collective-permute-start.39) | collective-permute-done | bytes 1024032 | tf_op jit(solution)/shard_map/ppermute | solution.py:87
  250.0 15.6 %collective-permute-done.29 = bf16[1,2,1,2,160,800]{5,4,3,1,2,0:T(8,128)(2,1)S(1)} collective-permute-done((bf16[1,2,1,2,160,800]{5,4,3,1,2,0:T(8,128)(2,1)}, bf16[1,2,1,2,160,800]{5,4,3,1,2,0:T(8,128)(2,1)S(1)}, u32[]{:S(2)}, u32[]{:S(2)}) %collective-permute-start.29) | collective-permute-done | bytes 1024032 | tf_op jit(solution)/shard_map/ppermute | solution.py:87
  269.5 17.2 %collective-permute-done.8 = bf16[2,2,1,1,48,1920]{5,4,3,2,1,0:T(8,128)(2,1)S(1)} collective-permute-done((bf16[2,2,1,1,48,1920]{5,4,3,2,1,0:T(8,128)(2,1)S(1)}, bf16[2,2,1,1,48,1920]{5,4,3,2,1,0:T(8,128)(2,1)S(1)}, u32[]{:S(2)}, u32[]{:S(2)}) %collective-permute-start.8) | collective-permute-done | bytes 737312 | tf_op jit(solution)/shard_map/ppermute | solution.py:87
  297.6 29.8 %collective-permute-done.3 = bf16[2,2,2,1,1,80,1152]{6,5,4,3,2,1,0:T(8,128)(2,1)S(1)} collective-permute-done((bf16[2,2,2,1,1,80,1152]{6,5,4,3,2,1,0:T(8,128)(2,1)S(1)}, bf16[2,2,2,1,1,80,1152]{6,5,4,3,2,1,0:T(8,128)(2,1)S(1)}, u32[]{:S(2)}, u32[]{:S(2)}) %collective-permute-start.3) | collective-permute-done | bytes 1474592 | tf_op jit(solution)/shard_map/ppermute | solution.py:87
  336.4 22.5 %collective-permute-done.9 = bf16[2,2,2,1,48,1920]{5,4,3,2,1,0:T(8,128)(2,1)S(1)} collective-permute-done((bf16[2,2,2,1,48,1920]{5,4,3,2,1,0:T(8,128)(2,1)S(1)}, bf16[2,2,2,1,48,1920]{5,4,3,2,1,0:T(8,128)(2,1)S(1)}, u32[]{:S(2)}, u32[]{:S(2)}) %collective-permute-start.9) | collective-permute-done | bytes 1474592 | tf_op jit(solution)/shard_map/ppermute | solution.py:87
  389.7 56.9 %collective-permute-done.17 = bf16[2,2,2,1,160,1280]{5,4,3,2,1,0:T(8,128)(2,1)} collective-permute-done((bf16[2,2,2,1,160,1280]{5,4,3,2,1,0:T(8,128)(2,1)}, bf16[2,2,2,1,160,1280]{5,4,3,2,1,0:T(8,128)(2,1)}, u32[]{:S(2)}, u32[]{:S(2)}) %collective-permute-start.17) | collective-permute-done | bytes 3276832 | tf_op jit(solution)/shard_map/ppermute | solution.py:87
  461.5 37.2 %while.30 = (s32[]{:T(128)}, bf16[5,4,512,64]{2,3,1,0:T(8,128)(2,1)}, f32[5,4,512]{2,1,0:T(4,128)}, f32[5,4]{1,0:T(8,128)S(1)}, bf16[5,4,512,96]{2,3,1,0:T(8,128...) while((s32[]{:T(128)}, ...), condition=%wide.region_9.10_spmd.clone, body=%wide.region_5.9_spmd.clone.sunk | while | flops 350091264 | bytes 15014561 | solution.py:300
  560.5 25.7 %collective-permute-done.19 = bf16[256,2560]{1,0:T(8,128)(2,1)S(1)} collective-permute-done((bf16[256,2560]{1,0:T(8,128)(2,1)}, bf16[256,2560]{1,0:T(8,128)(2,1)S(1)}, u32[]{:S(2)}, u32[]{:S(2)}) %collective-permute-start.19) | collective-permute-done | bytes 1310752 | tf_op jit(solution)/shard_map/ppermute | solution.py:87
  590.3 22.3 %collective-permute-done.21 = bf16[256,2560]{1,0:T(8,128)(2,1)S(1)} collective-permute-done((bf16[256,2560]{1,0:T(8,128)(2,1)}, bf16[256,2560]{1,0:T(8,128)(2,1)S(1)}, u32[]{:S(2)}, u32[]{:S(2)}) %collective-permute-start.21) | collective-permute-done | bytes 1310752 | tf_op jit(solution)/shard_map/ppermute | solution.py:227
  618.5 13.9 fusion.158
  632.4 13.2 fusion.157
  645.6 20.6 %multiply_convert_fusion.1 = (bf16[2048,800]{0,1:T(8,128)(2,1)}, bf16[2048,800]{0,1:T(8,128)(2,1)}, bf16[2048,800]{0,1:T(8,128)(2,1)S(1)}) fusion(f32[2048,800]{0,1:T(8,128)} %fusion.157, f32[2048,800]{0,1:T(8,128)} %fusion.158, bf16[2048,2560]{1,0:T(8,128)(2,1)} %constant_dynamic-update-slice_fusion.8, bf16[2560,800]{1,0:T(8,128)(2,1)} %bitcast.360), kind=kOutput, calls=%fused_computation.76 | convolution fusion | flops 8413184000 | bytes 37519360 | tf_op jit(solution)/shard_map/dot_general | solution.py:336
  666.2 16.3 %fusion.166 = f32[2560,800]{1,0:T(8,128)S(1)} fusion(bf16[2048,2560]{1,0:T(8,128)(2,1)} %constant_dynamic-update-slice_fusion, bf16[2048,800]{0,1:T(8,128)(2,1)} %get-tuple-element.239), kind=kOutput, calls=%fused_computation.470 | convolution fusion | flops 8388608000 | bytes 21954560 | tf_op jit(solution)/shard_map/dot_general | solution.py:47
  682.6 19.1 %fusion.160 = f32[2048,2560]{1,0:T(8,128)} fusion(bf16[2048,800]{0,1:T(8,128)(2,1)S(1)} %copy-done.145, bf16[2560,800]{1,0:T(8,128)(2,1)} %bitcast.368), kind=kOutput, calls=%fused_computation.464 | convolution fusion | flops 8388608000 | bytes 28344320 | tf_op jit(solution)/shard_map/dot_general | solution.py:47
  701.7 14.0 fusion.168
  719.2 15.4 %fusion.167 = f32[2560,800]{1,0:T(8,128)S(1)} fusion(bf16[2048,2560]{1,0:T(8,128)(2,1)} %constant_dynamic-update-slice_fusion, bf16[2048,800]{0,1:T(8,128)(2,1)} %get-tuple-element.238), kind=kOutput, calls=%fused_computation.471 | convolution fusion | flops 8388608000 | bytes 21954560 | tf_op jit(solution)/shard_map/dot_general | solution.py:47
  740.2 21.0 %convolution_add_fusion = f32[2048,2560]{1,0:T(8,128)} fusion(f32[2048,2560]{1,0:T(8,128)} %fusion.160, bf16[2048,800]{0,1:T(8,128)(2,1)} %get-tuple-element.238, bf16[2560,800]{1,0:T(8,128)(2,1)} %bitcast.364), kind=kOutput, calls=%fused_computation.68 | convolution fusion | flops 8393850880 | bytes 49315840 | tf_op jit(solution)/shard_map/dot_general | solution.py:47
  775.5 42.4 %collective-permute-done.80 = bf16[2,2,1,2,160,800]{5,4,3,2,1,0:T(8,128)(2,1)} collective-permute-done((bf16[2,2,1,2,160,800]{5,4,3,2,1,0:T(8,128)(2,1)}, bf16[2,2,1,2,160,800]{5,4,3,2,1,0:T(8,128)(2,1)}, u32[]{:S(2)}, u32[]{:S(2)}) %collective-permute-start.80) | collective-permute-done | bytes 2048032 | tf_op jit(solution)/shard_map/ppermute | solution.py:87
  824.5 42.2 %collective-permute-done.75 = bf16[2,2,1,2,160,800]{5,4,3,2,1,0:T(8,128)(2,1)} collective-permute-done((bf16[2,2,1,2,160,800]{5,4,3,2,1,0:T(8,128)(2,1)}, bf16[2,2,1,2,160,800]{5,4,3,2,1,0:T(8,128)(2,1)}, u32[]{:S(2)}, u32[]{:S(2)}) %collective-permute-start.75) | collective-permute-done | bytes 2048032 | tf_op jit(solution)/shard_map/ppermute | solution.py:87
  871.9 14.3 fusion.159
  901.9 22.7 %collective-permute-done.76 = bf16[1,2,1,2,160,800]{5,4,3,2,1,0:T(8,128)(2,1)} collective-permute-done((bf16[1,2,1,2,160,800]{5,4,3,2,1,0:T(8,128)(2,1)}, bf16[1,2,1,2,160,800]{5,4,3,2,1,0:T(8,128)(2,1)}, u32[]{:S(2)}, u32[]{:S(2)}) %collective-permute-start.76) | collective-permute-done | bytes 1024032 | tf_op jit(solution)/shard_map/ppermute | solution.py:87
  952.7 12.9 fusion.152
  984.6 49.6 %collective-permute-done.78 = bf16[1,1,160,800]{3,2,1,0:T(8,128)(2,1)} collective-permute-done((bf16[1,1,160,800]{3,2,1,0:T(8,128)(2,1)}, bf16[1,1,160,800]{3,2,1,0:T(8,128)(2,1)}, u32[]{:S(2)}, u32[]{:S(2)}) %collective-permute-start.78) | collective-permute-done | bytes 256032 | tf_op jit(solution)/shard_map/ppermute | solution.py:87
  1057.2 12.9 fusion.153
  1093.3 146.4 %while.31 = (s32[]{:T(128)}, f32[5,4,512,96]{2,3,1,0:T(8,128)}, f32[5,4,512,96]{2,3,1,0:T(8,128)}, bf16[5,4,512,64]{2,3,1,0:T(8,128)(2,1)}, bf16[5,4,512,96]{2,3...) while((s32[]{:T(128)}, f32[5,4,512,96]{2,3,1,0:T(8,128)}, ...), condition=%wide.region_14.15_spmd.clone, body=%wide.region_12.14_spmd.clone.sunk | while | flops 887886848 | bytes 51151992 | solution.py:352
  1319.5 15.0 concatenate.437
  1346.6 50.5 %collective-permute-done.63 = bf16[2,2,2,1,48,1920]{5,4,3,2,1,0:T(8,128)(2,1)} collective-permute-done((bf16[2,2,2,1,48,1920]{5,4,3,2,1,0:T(8,128)(2,1)}, bf16[2,2,2,1,48,1920]{5,4,3,2,1,0:T(8,128)(2,1)}, u32[]{:S(2)}, u32[]{:S(2)}) %collective-permute-start.63) | collective-permute-done | bytes 1474592 | tf_op jit(solution)/shard_map/ppermute | solution.py:87
  1402.7 13.5 collective-permute-done.64
  1436.3 21.6 %collective-permute-done.72 = bf16[2,2,1,1,160,1280]{5,4,3,2,1,0:T(8,128)(2,1)S(1)} collective-permute-done((bf16[2,2,1,1,160,1280]{5,4,3,2,1,0:T(8,128)(2,1)S(1)}, bf16[2,2,1,1,160,1280]{5,4,3,2,1,0:T(8,128)(2,1)S(1)}, u32[]{:S(2)}, u32[]{:S(2)}) %collective-permute-start.72) | collective-permute-done | bytes 1638432 | tf_op jit(solution)/shard_map/ppermute | solution.py:87
  1496.2 12.6 collective-permute-done.74
  (852 shorter events, 775.7 us)
Async XLA Ops:
  3.6 286.2 %collective-permute-start.45 = (bf16[256,2560]{1,0:T(8,128)(2,1)}, bf16[256,2560]{1,0:T(8,128)(2,1)}, u32[]{:S(2)}, u32[]{:S(2)}) collective-permute-start(bf16[256,2560]{1,0:T(8,128)(2,1)} %fusion.87), channel_id=1, source_target_pairs={{0,2},{2,0},{1,3},{3,1},{4,6},{6,4},{5,7},{7,5},{8,10},{10,8},{9,1... | collective-permute-start | bytes 3932168 | tf_op jit(solution)/shard_map/ppermute | solution.py:87
  6.5 287.3 %collective-permute-start.46 = (bf16[256,2560]{1,0:T(8,128)(2,1)}, bf16[256,2560]{1,0:T(8,128)(2,1)}, u32[]{:S(2)}, u32[]{:S(2)}) collective-permute-start(bf16[256,2560]{1,0:T(8,128)(2,1)} %fusion.87), channel_id=1, source_target_pairs={{0,8},{8,0},{1,9},{9,1},{2,10},{10,2},{3,11},{11,3},{4,12},{12,4},... | collective-permute-start | bytes 3932168 | tf_op jit(solution)/shard_map/ppermute | solution.py:87
  120.5 97.3 %collective-permute-start.34 = (bf16[1,2,1,2,160,800]{5,4,3,1,2,0:T(8,128)(2,1)}, bf16[1,2,1,2,160,800]{5,4,3,1,2,0:T(8,128)(2,1)}, u32[]{:S(2)}, u32[]{:S(2)}) collective-permute-start(bf16[1,2,1,2,160,800]{5,4,3,1,2,0:T(8,128)(2,1)} %maximum_bitcast_fusion.4), channel_id=1, source_target_pairs={{0,16},{16,0},{1,17},{17,1},{2,18},{18,2},{3,19},{19,3},{4,20},{20... | collective-permute-start | bytes 3072008 | tf_op jit(solution)/shard_map/ppermute | solution.py:87
  122.6 120.0 %collective-permute-start.39 = (bf16[1,2,1,2,160,800]{5,4,3,1,2,0:T(8,128)(2,1)}, bf16[1,2,1,2,160,800]{5,4,3,1,2,0:T(8,128)(2,1)}, u32[]{:S(2)}, u32[]{:S(2)}) collective-permute-start(bf16[1,2,1,2,160,800]{5,4,3,1,2,0:T(8,128)(2,1)} %maximum_bitcast_fusion.5), channel_id=1, source_target_pairs={{0,16},{16,0},{1,17},{17,1},{2,18},{18,2},{3,19},{19,3},{4,20},{20... | collective-permute-start | bytes 3072008 | tf_op jit(solution)/shard_map/ppermute | solution.py:87
  188.1 77.6 %collective-permute-start.29 = (bf16[1,2,1,2,160,800]{5,4,3,1,2,0:T(8,128)(2,1)}, bf16[1,2,1,2,160,800]{5,4,3,1,2,0:T(8,128)(2,1)S(1)}, u32[]{:S(2)}, u32[]{:S(2)}) collective-permute-start(bf16[1,2,1,2,160,800]{5,4,3,1,2,0:T(8,128)(2,1)} %maximum_bitcast_fusion.3), channel_id=1, source_target_pairs={{0,16},{16,0},{1,17},{17,1},{2,18},{18,2},{3,19},{19,3},{4,20},{20... | collective-permute-start | bytes 3072008 | tf_op jit(solution)/shard_map/ppermute | solution.py:87
  217.8 78.4 %collective-permute-start.47 = (bf16[256,2560]{1,0:T(8,128)(2,1)}, bf16[256,2560]{1,0:T(8,128)(2,1)S(1)}, u32[]{:S(2)}, u32[]{:S(2)}) collective-permute-start(bf16[256,2560]{1,0:T(8,128)(2,1)} %fusion.87), channel_id=1, source_target_pairs={{0,10},{2,8},{8,2},{10,0},{1,11},{3,9},{9,3},{11,1},{4,14},{6,12},... | collective-permute-start | bytes 3932168 | tf_op jit(solution)/shard_map/ppermute | solution.py:227
  265.6 64.7 %collective-permute-start.48 = (bf16[256,2560]{1,0:T(8,128)(2,1)}, bf16[256,2560]{1,0:T(8,128)(2,1)S(1)}, u32[]{:S(2)}, u32[]{:S(2)}) collective-permute-start(bf16[256,2560]{1,0:T(8,128)(2,1)} %fusion.87), channel_id=1, source_target_pairs={{0,1},{1,0},{2,3},{3,2},{4,5},{5,4},{6,7},{7,6},{8,9},{9,8},{10,11... | collective-permute-start | bytes 3932168 | tf_op jit(solution)/shard_map/ppermute | solution.py:87
  289.7 77.5 %collective-permute-start.16 = (bf16[2,2,1,1,160,1280]{5,4,3,2,1,0:T(8,128)(2,1)}, bf16[2,2,1,1,160,1280]{5,4,3,2,1,0:T(8,128)(2,1)S(1)}, u32[]{:S(2)}, u32[]{:S(2)}) collective-permute-start(bf16[2,2,1,1,160,1280]{5,4,3,2,1,0:T(8,128)(2,1)} %pad_maximum_fusion.18), channel_id=1, source_target_pairs={{0,4},{4,0},{1,5},{5,1},{2,6},{6,2},{3,7},{7,3},{8,12},{12,8},{9,1... | collective-permute-start | bytes 4915208 | tf_op jit(solution)/shard_map/ppermute | solution.py:87
  293.8 65.1 %collective-permute-start.9 = (bf16[2,2,2,1,48,1920]{5,4,3,2,1,0:T(8,128)(2,1)S(1)}, bf16[2,2,2,1,48,1920]{5,4,3,2,1,0:T(8,128)(2,1)S(1)}, u32[]{:S(2)}, u32[]{:S(2)}) collective-permute-start(bf16[2,2,2,1,48,1920]{5,4,3,2,1,0:T(8,128)(2,1)S(1)} %pad_maximum_fusion.20), channel_id=1, source_target_pairs={{0,2},{2,0},{1,3},{3,1},{4,6},{6,4},{5,7},{7,5},{8,10},{10,8},{9,1... | collective-permute-start | bytes 4423688 | tf_op jit(solution)/shard_map/ppermute | solution.py:87
  332.0 183.7 %collective-permute-start.40 = (bf16[2,2,1,2,160,800]{5,4,3,1,2,0:T(8,128)(2,1)}, bf16[2,2,1,2,160,800]{5,4,3,1,2,0:T(8,128)(2,1)}, u32[]{:S(2)}, u32[]{:S(2)}) collective-permute-start(bf16[2,2,1,2,160,800]{5,4,3,1,2,0:T(8,128)(2,1)} %pad_maximum_fusion.13), channel_id=1, source_target_pairs={{0,4},{4,0},{1,5},{5,1},{2,6},{6,2},{3,7},{7,3},{8,12},{12,8},{9,1... | collective-permute-start | bytes 6144008 | tf_op jit(solution)/shard_map/ppermute | solution.py:87
  334.7 186.6 %collective-permute-start.35 = (bf16[2,2,1,2,160,800]{5,4,3,1,2,0:T(8,128)(2,1)}, bf16[2,2,1,2,160,800]{5,4,3,1,2,0:T(8,128)(2,1)}, u32[]{:S(2)}, u32[]{:S(2)}) collective-permute-start(bf16[2,2,1,2,160,800]{5,4,3,1,2,0:T(8,128)(2,1)} %pad_maximum_fusion.12), channel_id=1, source_target_pairs={{0,4},{4,0},{1,5},{5,1},{2,6},{6,2},{3,7},{7,3},{8,12},{12,8},{9,1... | collective-permute-start | bytes 6144008 | tf_op jit(solution)/shard_map/ppermute | solution.py:87
  358.9 167.3 %collective-permute-start.30 = (bf16[2,2,1,2,160,800]{5,4,3,1,2,0:T(8,128)(2,1)}, bf16[2,2,1,2,160,800]{5,4,3,1,2,0:T(8,128)(2,1)}, u32[]{:S(2)}, u32[]{:S(2)}) collective-permute-start(bf16[2,2,1,2,160,800]{5,4,3,1,2,0:T(8,128)(2,1)} %pad_maximum_fusion.11), channel_id=1, source_target_pairs={{0,4},{4,0},{1,5},{5,1},{2,6},{6,2},{3,7},{7,3},{8,12},{12,8},{9,1... | collective-permute-start | bytes 6144008 | tf_op jit(solution)/shard_map/ppermute | solution.py:87
  368.4 144.7 %collective-permute-start.51 = (bf16[256,2560]{1,0:T(8,128)(2,1)}, bf16[256,2560]{1,0:T(8,128)(2,1)}, u32[]{:S(2)}, u32[]{:S(2)}) collective-permute-start(bf16[256,2560]{1,0:T(8,128)(2,1)} %copy-done.82), channel_id=1, source_target_pairs={{0,1},{1,0},{2,3},{3,2},{4,5},{5,4},{6,7},{7,6},{8,9},{9,8},{10,11... | collective-permute-start | bytes 3932168 | tf_op jit(solution)/shard_map/ppermute | solution.py:87
  373.0 73.6 %collective-permute-start.17 = (bf16[2,2,2,1,160,1280]{5,4,3,2,1,0:T(8,128)(2,1)}, bf16[2,2,2,1,160,1280]{5,4,3,2,1,0:T(8,128)(2,1)}, u32[]{:S(2)}, u32[]{:S(2)}) collective-permute-start(bf16[2,2,2,1,160,1280]{5,4,3,2,1,0:T(8,128)(2,1)} %pad_maximum_fusion.5), channel_id=1, source_target_pairs={{0,2},{2,0},{1,3},{3,1},{4,6},{6,4},{5,7},{7,5},{8,10},{10,8},{9,1... | collective-permute-start | bytes 9830408 | tf_op jit(solution)/shard_map/ppermute | solution.py:87
  557.1 55.5 %collective-permute-start.21 = (bf16[256,2560]{1,0:T(8,128)(2,1)}, bf16[256,2560]{1,0:T(8,128)(2,1)S(1)}, u32[]{:S(2)}, u32[]{:S(2)}) collective-permute-start(bf16[256,2560]{1,0:T(8,128)(2,1)} %get-tuple-element.233), channel_id=1, source_target_pairs={{0,10},{2,8},{8,2},{10,0},{1,11},{3,9},{9,3},{11,1},{4,14},{6,12},... | collective-permute-start | bytes 3932168 | tf_op jit(solution)/shard_map/ppermute | solution.py:227
  736.5 81.3 %collective-permute-start.80 = (bf16[2,2,1,2,160,800]{5,4,3,2,1,0:T(8,128)(2,1)}, bf16[2,2,1,2,160,800]{5,4,3,2,1,0:T(8,128)(2,1)}, u32[]{:S(2)}, u32[]{:S(2)}) collective-permute-start(bf16[2,2,1,2,160,800]{5,4,3,2,1,0:T(8,128)(2,1)} %dynamic-slice_convert_fusion.3), channel_id=1, source_target_pairs={{0,4},{4,0},{1,5},{5,1},{2,6},{6,2},{3,7},{7,3},{8,12},{12,8},{9,1... | collective-permute-start | bytes 6144008 | tf_op jit(solution)/shard_map/ppermute | solution.py:87
  739.5 127.2 %collective-permute-start.75 = (bf16[2,2,1,2,160,800]{5,4,3,2,1,0:T(8,128)(2,1)}, bf16[2,2,1,2,160,800]{5,4,3,2,1,0:T(8,128)(2,1)}, u32[]{:S(2)}, u32[]{:S(2)}) collective-permute-start(bf16[2,2,1,2,160,800]{5,4,3,2,1,0:T(8,128)(2,1)} %dynamic-slice_convert_fusion.4), channel_id=1, source_target_pairs={{0,4},{4,0},{1,5},{5,1},{2,6},{6,2},{3,7},{7,3},{8,12},{12,8},{9,1... | collective-permute-start | bytes 6144008 | tf_op jit(solution)/shard_map/ppermute | solution.py:87
  768.0 184.7 %collective-permute-start.52 = (bf16[1024,2560]{1,0:T(8,128)(2,1)}, bf16[1024,2560]{1,0:T(8,128)(2,1)}, u32[]{:S(2)}, u32[]{:S(2)}) collective-permute-start(bf16[1024,2560]{1,0:T(8,128)(2,1)} %slice.356), channel_id=1, source_target_pairs={{0,1},{1,0},{2,3},{3,2},{4,5},{5,4},{6,7},{7,6},{8,9},{9,8},{10,11... | collective-permute-start | bytes 15728648 | tf_op jit(solution)/shard_map/ppermute | solution.py:87
  773.4 119.9 %collective-permute-start.86 = (bf16[1,2,1,2,160,800]{5,4,3,2,1,0:T(8,128)(2,1)}, bf16[1,2,1,2,160,800]{5,4,3,2,1,0:T(8,128)(2,1)}, u32[]{:S(2)}, u32[]{:S(2)}) collective-permute-start(bf16[1,2,1,2,160,800]{5,4,3,2,1,0:T(8,128)(2,1)} %dynamic-slice_convert_fusion.8), channel_id=1, source_target_pairs={{0,16},{16,0},{1,17},{17,1},{2,18},{18,2},{3,19},{19,3},{4,20},{20... | collective-permute-start | bytes 3072008 | tf_op jit(solution)/shard_map/ppermute | solution.py:87
  822.4 78.0 %collective-permute-start.81 = (bf16[1,2,1,2,160,800]{5,4,3,2,1,0:T(8,128)(2,1)}, bf16[1,2,1,2,160,800]{5,4,3,2,1,0:T(8,128)(2,1)}, u32[]{:S(2)}, u32[]{:S(2)}) collective-permute-start(bf16[1,2,1,2,160,800]{5,4,3,2,1,0:T(8,128)(2,1)} %dynamic-slice_convert_fusion.9), channel_id=1, source_target_pairs={{0,16},{16,0},{1,17},{17,1},{2,18},{18,2},{3,19},{19,3},{4,20},{20... | collective-permute-start | bytes 3072008 | tf_op jit(solution)/shard_map/ppermute | solution.py:87
  893.3 163.8 %collective-permute-start.41 = (bf16[1024,2560]{1,0:T(8,128)(2,1)}, bf16[1024,2560]{1,0:T(8,128)(2,1)}, u32[]{:S(2)}, u32[]{:S(2)}) collective-permute-start(bf16[1024,2560]{1,0:T(8,128)(2,1)} %slice.357), channel_id=1, source_target_pairs={{0,1},{1,0},{2,3},{3,2},{4,5},{5,4},{6,7},{7,6},{8,9},{9,8},{10,11... | collective-permute-start | bytes 15728648 | tf_op jit(solution)/shard_map/ppermute | solution.py:87
  969.7 80.7 %collective-permute-start.53 = (bf16[256,2560]{1,0:T(8,128)(2,1)}, bf16[256,2560]{1,0:T(8,128)(2,1)}, u32[]{:S(2)}, u32[]{:S(2)}) collective-permute-start(bf16[256,2560]{1,0:T(8,128)(2,1)} %get-tuple-element.247), channel_id=1, source_target_pairs={{0,2},{2,0},{1,3},{3,1},{4,6},{6,4},{5,7},{7,5},{8,10},{10,8},{9,1... | collective-permute-start | bytes 3932168 | tf_op jit(solution)/shard_map/ppermute | solution.py:87
  970.2 80.2 %collective-permute-start.54 = (bf16[256,2560]{1,0:T(8,128)(2,1)}, bf16[256,2560]{1,0:T(8,128)(2,1)}, u32[]{:S(2)}, u32[]{:S(2)}) collective-permute-start(bf16[256,2560]{1,0:T(8,128)(2,1)} %get-tuple-element.249), channel_id=1, source_target_pairs={{0,8},{8,0},{1,9},{9,1},{2,10},{10,2},{3,11},{11,3},{4,12},{12,4},... | collective-permute-start | bytes 3932168 | tf_op jit(solution)/shard_map/ppermute | solution.py:87
  970.4 79.9 %collective-permute-start.55 = (bf16[256,2560]{1,0:T(8,128)(2,1)}, bf16[256,2560]{1,0:T(8,128)(2,1)}, u32[]{:S(2)}, u32[]{:S(2)}) collective-permute-start(bf16[256,2560]{1,0:T(8,128)(2,1)} %get-tuple-element.248), channel_id=1, source_target_pairs={{0,10},{2,8},{8,2},{10,0},{1,11},{3,9},{9,3},{11,1},{4,14},{6,12},... | collective-permute-start | bytes 3932168 | tf_op jit(solution)/shard_map/ppermute | solution.py:240
  977.9 56.3 %collective-permute-start.78 = (bf16[1,1,160,800]{3,2,1,0:T(8,128)(2,1)}, bf16[1,1,160,800]{3,2,1,0:T(8,128)(2,1)}, u32[]{:S(2)}, u32[]{:S(2)}) collective-permute-start(bf16[1,1,160,800]{3,2,1,0:T(8,128)(2,1)} %get-tuple-element.297), channel_id=1, source_target_pairs={{0,8},{8,0},{1,9},{9,1},{2,10},{10,2},{3,11},{11,3},{4,12},{12,4},... | collective-permute-start | bytes 768008 | tf_op jit(solution)/shard_map/ppermute | solution.py:87
  1074.1 265.2 %collective-permute-start.42 = (bf16[256,2560]{1,0:T(8,128)(2,1)}, bf16[256,2560]{1,0:T(8,128)(2,1)}, u32[]{:S(2)}, u32[]{:S(2)}) collective-permute-start(bf16[256,2560]{1,0:T(8,128)(2,1)} %get-tuple-element.250), channel_id=1, source_target_pairs={{0,2},{2,0},{1,3},{3,1},{4,6},{6,4},{5,7},{7,5},{8,10},{10,8},{9,1... | collective-permute-start | bytes 3932168 | tf_op jit(solution)/shard_map/ppermute | solution.py:87
  1075.7 264.6 %collective-permute-start.43 = (bf16[256,2560]{1,0:T(8,128)(2,1)}, bf16[256,2560]{1,0:T(8,128)(2,1)}, u32[]{:S(2)}, u32[]{:S(2)}) collective-permute-start(bf16[256,2560]{1,0:T(8,128)(2,1)} %get-tuple-element.252), channel_id=1, source_target_pairs={{0,8},{8,0},{1,9},{9,1},{2,10},{10,2},{3,11},{11,3},{4,12},{12,4},... | collective-permute-start | bytes 3932168 | tf_op jit(solution)/shard_map/ppermute | solution.py:87
  1076.6 263.7 %collective-permute-start.44 = (bf16[256,2560]{1,0:T(8,128)(2,1)}, bf16[256,2560]{1,0:T(8,128)(2,1)}, u32[]{:S(2)}, u32[]{:S(2)}) collective-permute-start(bf16[256,2560]{1,0:T(8,128)(2,1)} %get-tuple-element.251), channel_id=1, source_target_pairs={{0,10},{2,8},{8,2},{10,0},{1,11},{3,9},{9,3},{11,1},{4,14},{6,12},... | collective-permute-start | bytes 3932168 | tf_op jit(solution)/shard_map/ppermute | solution.py:240
  1292.7 124.7 %collective-permute-start.71 = (bf16[2,2,2,1,160,1280]{5,4,3,2,1,0:T(8,128)(2,1)}, bf16[2,2,2,1,160,1280]{5,4,3,2,1,0:T(8,128)(2,1)}, u32[]{:S(2)}, u32[]{:S(2)}) collective-permute-start(bf16[2,2,2,1,160,1280]{5,4,3,2,1,0:T(8,128)(2,1)} %dynamic-slice_convert_fusion), channel_id=1, source_target_pairs={{0,2},{2,0},{1,3},{3,1},{4,6},{6,4},{5,7},{7,5},{8,10},{10,8},{9,1... | collective-permute-start | bytes 9830408 | tf_op jit(solution)/shard_map/ppermute | solution.py:87
  1296.2 100.9 %collective-permute-start.63 = (bf16[2,2,2,1,48,1920]{5,4,3,2,1,0:T(8,128)(2,1)}, bf16[2,2,2,1,48,1920]{5,4,3,2,1,0:T(8,128)(2,1)}, u32[]{:S(2)}, u32[]{:S(2)}) collective-permute-start(bf16[2,2,2,1,48,1920]{5,4,3,2,1,0:T(8,128)(2,1)} %dynamic-slice_convert_fusion.6), channel_id=1, source_target_pairs={{0,2},{2,0},{1,3},{3,1},{4,6},{6,4},{5,7},{7,5},{8,10},{10,8},{9,1... | collective-permute-start | bytes 4423688 | tf_op jit(solution)/shard_map/ppermute | solution.py:87
  1339.4 60.8 %collective-permute-start.69 = (bf16[2,1,1,1,16,2560]{5,4,3,2,1,0:T(8,128)(2,1)}, bf16[2,1,1,1,16,2560]{5,4,3,2,1,0:T(8,128)(2,1)S(1)}, u32[]{:S(2)}, u32[]{:S(2)}) collective-permute-start(bf16[2,1,1,1,16,2560]{5,4,3,2,1,0:T(8,128)(2,1)} %dynamic-slice_convert_fusion.30), channel_id=1, source_target_pairs={{0,8},{8,0},{1,9},{9,1},{2,10},{10,2},{3,11},{11,3},{4,12},{12,4},... | collective-permute-start | bytes 491528 | tf_op jit(solution)/shard_map/ppermute | solution.py:87
  1340.3 83.5 %collective-permute-start.58 = (bf16[2,2,2,2,1,80,1060]{6,5,4,3,2,1,0:T(8,128)(2,1)}, bf16[2,2,2,2,1,80,1060]{6,5,4,3,2,1,0:T(8,128)(2,1)}, u32[]{:S(2)}, u32[]{:S(2)}) collective-permute-start(bf16[2,2,2,2,1,80,1060]{6,5,4,3,2,1,0:T(8,128)(2,1)} %dynamic-slice_convert_fusion.1), channel_id=1, source_target_pairs={{0,1},{1,0},{2,3},{3,2},{4,5},{5,4},{6,7},{7,6},{8,9},{9,8},{10,11... | collective-permute-start | bytes 8140808 | tf_op jit(solution)/shard_map/ppermute | solution.py:87
  (224 other events, 5010.8 us)

commit v2 on v1

v2 whole, which is shorter than its diff:
```python
import functools
import math

import jax
import jax.numpy as jnp
from jax import lax
from jax.experimental import pallas as pl
from jax.experimental.pallas import tpu as pltpu
from jax.experimental.layout import Layout, with_layout_constraint
from jax.sharding import Mesh
from jax.sharding import PartitionSpec as P

NOPE = 64
ROPE = 32
VD = 64
KVR = 256
TILE = 128


eps = 1e-05
resid_scale = 1.4 / math.sqrt(62.0)
rope_base = 10000.0
SWAP = [(0, 1), (1, 0)]
f32 = jnp.float32
bf16 = jnp.bfloat16


def rms_scale(value, gain):
    return value * lax.rsqrt(jnp.mean(value * value, axis=-1, keepdims=True) + eps) * gain


def rotate(value, cosine, sine):
    half = value.shape[-1] // 2
    first = value[..., :half]
    second = value[..., half:]
    return jnp.concatenate(
        [first * cosine - second * sine, second * cosine + first * sine], axis=-1
    )


def angles(seq_row, start, count):
    own_ids = lax.dynamic_slice_in_dim(seq_row, start, count)
    earlier = jnp.sum((seq_row[None, :] < own_ids[:, None]).astype(jnp.int32), axis=1)
    place = (start + jnp.arange(count, dtype=jnp.int32) - earlier).astype(f32)
    freq = jnp.power(rope_base, -jnp.arange(ROPE // 2, dtype=f32) * (2.0 / ROPE))
    turn = place[:, None] * freq[None, :]
    return (jnp.cos(turn), jnp.sin(turn))


def contract(left, right, left_dim, right_dim):
    return lax.dot_general(
        left, right, (((left_dim,), (right_dim,)), ((), ())), preferred_element_type=f32
    )


def turn(value, plain, first, second):
    return (
        value * plain
        + pltpu.roll(value, TILE - ROPE // 2, 1) * first
        + pltpu.roll(value, ROPE // 2, 1) * second
    )


def tables(cosine, sine):
    rows = cosine.shape[0]
    half = ROPE // 2

    def zeros(count):
        return jnp.zeros((rows, count), f32)

    plain = jnp.concatenate([jnp.ones((rows, NOPE), f32), cosine, cosine, zeros(TILE - NOPE - ROPE)], axis=1)
    first = jnp.concatenate([zeros(NOPE), -sine, zeros(TILE - NOPE - half)], axis=1)
    second = jnp.concatenate([zeros(NOPE + half), sine, zeros(TILE - NOPE - ROPE)], axis=1)
    return plain, first, second


def attend_kernel(
    scale,
    q_ref,
    kv_ref,
    rot_ref,
    plain_ref,
    first_ref,
    second_ref,
    bias_ref,
    mixed_ref,
    query_ref,
    total_ref,
    peak_ref,
):
    step = pl.program_id(0)
    lane = lax.broadcasted_iota(jnp.int32, (q_ref.shape[0], TILE), 1)
    spot = lax.broadcasted_iota(jnp.int32, peak_ref.shape, 1)

    @pl.when(step == 0)
    def _():
        peak_ref[...] = jnp.zeros_like(peak_ref)

    outs = []
    for one in range(2):
        cols = slice(one * TILE, (one + 1) * TILE)
        query = turn(q_ref[:, cols], plain_ref[...], first_ref[...], second_ref[...]).astype(bf16)
        query_ref[:, cols] = query
        kv = kv_ref[:, cols]
        keys = jnp.where(lane < NOPE, kv, rot_ref[...])
        masked = contract(keys, query, 1, 1) * scale + bias_ref[...]
        top = jnp.max(masked, axis=0, keepdims=True)
        weights = jnp.exp(masked - top)
        total = jnp.sum(weights, axis=0, keepdims=True)
        chance = (weights * (1.0 / total)).astype(bf16)
        outs.append(contract(chance, kv, 0, 0))
        total_ref[0, one : one + 1, :] = top + jnp.log(total)
        peak_ref[...] = jnp.where(spot == step * 2 + one, jnp.max(top), peak_ref[...])
    mixed_ref[...] = jnp.where(lane < VD, pltpu.roll(outs[0], VD, 1), outs[1]).astype(bf16)


def attend(q, kv, rot, turns, bias, scale):
    group, cols = q.shape
    heads = cols // TILE
    whole = pl.BlockSpec((group, TILE), lambda i: (0, 0))
    two = pl.BlockSpec((group, 2 * TILE), lambda i: (0, i))
    return pl.pallas_call(
        functools.partial(attend_kernel, scale),
        grid=(heads // 2,),
        out_shape=(
            jax.ShapeDtypeStruct((group, heads * VD), bf16),
            jax.ShapeDtypeStruct((group, cols), bf16),
            jax.ShapeDtypeStruct((heads // 2, 2, group), f32),
            jax.ShapeDtypeStruct((8, TILE), f32),
        ),
        in_specs=[two, two, whole, whole, whole, whole, pl.BlockSpec((group, group), lambda i: (0, 0))],
        out_specs=(
            pl.BlockSpec((group, TILE), lambda i: (0, i)),
            two,
            pl.BlockSpec((1, 2, group), lambda i: (i, 0, 0)),
            pl.BlockSpec((8, TILE), lambda i: (0, 0)),
        ),
        compiler_params=pltpu.CompilerParams(
            dimension_semantics=("arbitrary",), vmem_limit_bytes=40 << 20
        ),
        cost_estimate=pl.CostEstimate(
            flops=4 * heads * group * group * TILE,
            transcendentals=heads * group * group,
            bytes_accessed=12 * group * cols,
        ),
    )(q, kv, rot, *turns, bias)


def attend_back_kernel(
    scale,
    query_ref,
    kv_ref,
    d_mixed_ref,
    total_ref,
    rot_ref,
    plain_ref,
    first_ref,
    second_ref,
    bias_ref,
    d_q_ref,
    d_kv_ref,
    d_rot_ref,
):
    step = pl.program_id(0)
    lane = lax.broadcasted_iota(jnp.int32, (query_ref.shape[0], TILE), 1)

    @pl.when(step == 0)
    def _():
        d_rot_ref[...] = jnp.zeros_like(d_rot_ref)

    pair = d_mixed_ref[...].astype(f32)
    for one in range(2):
        cols = slice(one * TILE, (one + 1) * TILE)
        query = query_ref[:, cols]
        kv = kv_ref[:, cols]
        keys = jnp.where(lane < NOPE, kv, rot_ref[...])
        own = pair if one else pltpu.roll(pair, VD, 1)
        d_mixed = jnp.where(lane < VD, 0.0, own).astype(bf16)
        masked = contract(keys, query, 1, 1) * scale + bias_ref[...]
        chance = jnp.exp(masked - total_ref[0, one : one + 1, :])
        d_values = contract(chance.astype(bf16), d_mixed, 1, 0)
        d_chance = contract(kv, d_mixed, 1, 1)
        inner = jnp.sum(chance * d_chance, axis=0, keepdims=True)
        d_raw = (chance * (d_chance - inner) * scale).astype(bf16)
        d_keys = contract(d_raw, query, 1, 0)
        d_query = contract(d_raw, keys, 0, 0)
        d_q_ref[:, cols] = turn(
            d_query, plain_ref[...], first_ref[...], second_ref[...]
        ).astype(bf16)
        d_kv_ref[:, cols] = jnp.where(lane < NOPE, d_keys, d_values).astype(bf16)
        d_rot_ref[...] += d_keys


def attend_back(query, kv, d_mixed, total, rot, turns, bias, scale):
    group, cols = query.shape
    heads = cols // TILE
    whole = pl.BlockSpec((group, TILE), lambda i: (0, 0))
    two = pl.BlockSpec((group, 2 * TILE), lambda i: (0, i))
    return pl.pallas_call(
        functools.partial(attend_back_kernel, scale),
        grid=(heads // 2,),
        out_shape=(
            jax.ShapeDtypeStruct((group, cols), bf16),
            jax.ShapeDtypeStruct((group, cols), bf16),
            jax.ShapeDtypeStruct((group, TILE), f32),
        ),
        in_specs=[
            two,
            two,
            pl.BlockSpec((group, TILE), lambda i: (0, i)),
            pl.BlockSpec((1, 2, group), lambda i: (i, 0, 0)),
            whole,
            whole,
            whole,
            whole,
            pl.BlockSpec((group, group), lambda i: (0, 0)),
        ],
        out_specs=(two, two, whole),
        compiler_params=pltpu.CompilerParams(
            dimension_semantics=("arbitrary",), vmem_limit_bytes=40 << 20
        ),
        cost_estimate=pl.CostEstimate(
            flops=10 * heads * group * group * TILE,
            transcendentals=heads * group * group,
            bytes_accessed=8 * group * cols,
        ),
    )(query, kv, d_mixed, total, rot, *turns, bias)


def swap(value, axis):
    return lax.ppermute(value, axis, SWAP)


def far(value, pair):
    return lax.ppermute(value, pair, [(i, 3 - i) for i in range(4)])


def after(value, *others):
    return lax.optimization_barrier((value,) + others)[0]


def pick(value, at, dim):
    return lax.dynamic_index_in_dim(value, at, dim, keepdims=True)


def both(own, other, axis, dim):
    here = lax.axis_index(axis) == 0
    return jnp.concatenate([jnp.where(here, own, other), jnp.where(here, other, own)], axis=dim)


def heads_grad_kernel(latent_ref, d_ref, out_ref):
    total = contract(latent_ref[...], d_ref[...], 0, 0)
    parts = [total[:, i * TILE : i * TILE + NOPE + ROPE] for i in range(4)]
    out_ref[...] = jnp.concatenate(parts, axis=1).astype(bf16)


def heads_grad(latent, d_heads):
    group, rank = latent.shape
    packs = d_heads.shape[1] // (4 * TILE)
    cols = 4 * (NOPE + ROPE)
    return pl.pallas_call(
        heads_grad_kernel,
        grid=(packs,),
        out_shape=jax.ShapeDtypeStruct((rank, packs * cols), bf16),
        in_specs=[
            pl.BlockSpec((group, rank), lambda i: (0, 0)),
            pl.BlockSpec((group, 4 * TILE), lambda i: (0, i)),
        ],
        out_specs=pl.BlockSpec((rank, cols), lambda i: (0, i)),
        compiler_params=pltpu.CompilerParams(vmem_limit_bytes=32 << 20),
        cost_estimate=pl.CostEstimate(
            flops=2 * group * rank * packs * 4 * TILE,
            transcendentals=0,
            bytes_accessed=2 * (group * packs * 4 * TILE + rank * packs * cols),
        ),
    )(latent, d_heads)


def rows_first(value):
    return with_layout_constraint(value, Layout(major_to_minor=(0, 1)))


def square_scatter(held, first, second, dim):
    here, there = lax.axis_index(first), lax.axis_index(second)

    def part(w, n):
        return pick(pick(held, w, dim), n, dim + 1)

    near = swap(part(here, 1 - there).astype(bf16), second)
    wide = swap(part(1 - here, there).astype(bf16), first)
    corner = far(part(1 - here, 1 - there).astype(bf16), (first, second))
    own = part(here, there).astype(f32)
    return own + near.astype(f32) + wide.astype(f32) + corner.astype(f32)


def place_of(first, second):
    return lax.axis_index(first) * 2 + lax.axis_index(second)


def other_of(axes):
    return {axis: 1 - lax.axis_index(axis) for axis in axes}


def meet(partners):
    barrier = pltpu.get_barrier_semaphore()
    for axes in partners:
        pl.semaphore_signal(
            barrier, inc=1, device_id=other_of(axes), device_id_type=pl.DeviceIdType.MESH
        )
    pl.semaphore_wait(barrier, len(partners))


class Sender:
    def __init__(self, send_sems, recv_sems):
        self.send_sems, self.recv_sems, self.all, self.left = send_sems, recv_sems, [], []

    def start(self, source, target, axes):
        copy = pltpu.make_async_remote_copy(
            src_ref=source,
            dst_ref=target,
            send_sem=self.send_sems.at[len(self.all)],
            recv_sem=self.recv_sems.at[len(self.all)],
            device_id=other_of(axes),
            device_id_type=pl.DeviceIdType.MESH,
        )
        copy.start()
        self.all.append(copy)
        return copy

    def finish(self):
        for copy in self.all:
            if all(copy is not other for other in self.left):
                copy.wait_send()


def first_kernel(
    squares,
    pair,
    spread,
    small_ref,
    gains_ref,
    q_ref,
    kv_ref,
    gate_ref,
    up_ref,
    down_ref,
    small_out,
    gains_out,
    q_out,
    kv_out,
    gate_out,
    others_out,
    staged,
    send_sems,
    recv_sems,
):
    core = lax.axis_index("c")
    places = [place_of(*square) for square in squares]
    me = place_of(*pair)
    sender = Sender(send_sems, recv_sems)
    cols = staged.shape[3]

    small_out[(*places, core)] = small_ref[...]
    gains_out[(*places, core)] = gains_ref[...]
    q_out[tuple(places)] = q_ref[...]
    kv_out[tuple(places)] = kv_ref[...]
    partners = [axes for one, two in squares for axes in ((two,), (one,), (one, two))]
    meet(partners + [pair, ("c",)])

    def blocks(ref, stage, place, tail, lead=()):
        index = lead + (slice(None),) * (stage - len(lead)) + (place,) + tuple(places[stage + 1 :])
        return ref.at[index + tail]

    early = [(small_out, (core,)), (gains_out, (core,))]
    later = [(q_out, ()), (kv_out, ())]

    def send_first(ref, tail):
        mine = blocks(ref, 0, places[0], tail)
        return [sender.start(mine, mine, axes) for axes in partners[:3]]

    def send_square(ref, tail, stage):
        one, two = squares[stage]
        mine = blocks(ref, stage, places[stage], tail)
        return [sender.start(mine, mine, (two,)), sender.start(mine, mine, (one,))]

    def pass_on(ref, tail, stage, copies):
        one, two = squares[stage]
        copies[0].wait_recv()
        half = blocks(ref, stage, places[stage] ^ 1, tail, (slice(0, 2),))
        first = sender.start(half, half, (one,))
        copies[1].wait_recv()
        half = blocks(ref, stage, places[stage] ^ 2, tail, (slice(2, 4),))
        return [first, sender.start(half, half, (two,))]

    def wait(copies):
        for copy in copies:
            copy.wait_recv()

    targets = (gate_out.at[0], others_out.at[0], others_out.at[1])

    def send_columns(away, axes):
        return [
            sender.start(staged.at[which, me ^ away], target.at[me], axes)
            for which, target in enumerate(targets)
        ]

    first = [send_first(*item) for item in early]
    for which, weight_ref in enumerate((gate_ref, up_ref, down_ref)):
        for quarter in range(4):
            staged[which, quarter] = weight_ref[:, quarter * cols : (quarter + 1) * cols]
    columns = [send_columns(1, (pair[1],))]
    for which, target in enumerate(targets):
        target[me] = staged[which, me]
    for copies in first:
        wait(copies)
    sent = [send_square(*item, 1) for item in early]
    first_later = [send_first(*item) for item in later]
    columns.append(send_columns(2, (pair[0],)))
    for stage in range(1, len(squares)):
        if stage > 1:
            sent = [send_square(*item, stage) for item in early]
        passed = [pass_on(*item, stage, copies) for item, copies in zip(early, sent)]
        if stage == 1:
            for copies in first_later:
                wait(copies)
            sent_later = [send_square(*item, 1) for item in later]
            columns.append(send_columns(3, pair))
        for copies in passed:
            wait(copies)
    mine = (slice(None),) * len(squares) + (core,)
    core_sent = [sender.start(ref.at[mine], ref.at[mine], ("c",)) for ref, _ in early]
    for copies in columns:
        copies[0].wait_recv()
    gate_over = [sender.start(gate_out.at[0], gate_out.at[1], (spread[0],))]
    for stage in range(1, len(squares)):
        if stage > 1:
            sent_later = [send_square(*item, stage) for item in later]
        passed = [pass_on(*item, stage, copies) for item, copies in zip(later, sent_later)]
        for copies in passed:
            wait(copies)
    wait(core_sent)
    for copies in columns:
        wait(copies[1:])
    wait(gate_over)
    sender.finish()


def first_gather(squares, pair, spread, small, gains, q_up, kv_up, gate, up, down):
    vmem = pl.BlockSpec(memory_space=pltpu.VMEM)
    rows, cols = gate.shape
    lead = (4,) * len(squares)
    copies = 12 + 16 * (len(squares) - 1) + 2 + 9 + 1
    return pl.pallas_call(
        functools.partial(first_kernel, squares, pair, spread),
        out_shape=(
            jax.ShapeDtypeStruct(lead + (2,) + small.shape, bf16),
            jax.ShapeDtypeStruct(lead + (2,) + gains.shape, bf16),
            jax.ShapeDtypeStruct(lead + q_up.shape, bf16),
            jax.ShapeDtypeStruct(lead + kv_up.shape, bf16),
            jax.ShapeDtypeStruct((2, 4, rows, cols // 4), bf16),
            jax.ShapeDtypeStruct((2, 4, rows, cols // 4), bf16),
        ),
        in_specs=[vmem] * 7,
        out_specs=(vmem,) * 6,
        scratch_shapes=[
            pltpu.VMEM((3, 4, rows, cols // 4), bf16),
            pltpu.SemaphoreType.DMA((copies,)),
            pltpu.SemaphoreType.DMA((copies,)),
        ],
        compiler_params=pltpu.CompilerParams(
            collective_id=0, has_side_effects=True, vmem_limit_bytes=48 << 20
        ),
    )(small, gains, q_up, kv_up, gate, up, down)


def lay_copies(fsdp, pair, spread, pieces, target, sems):
    copies = []
    for number, piece in enumerate(pieces):
        for block in range(4):
            place = 0
            for axis in fsdp:
                if axis == pair[0]:
                    bit = block >> 1
                elif axis == pair[1]:
                    bit = block & 1
                else:
                    bit = lax.axis_index(axis) ^ ((number >> spread.index(axis)) & 1)
                place = place * 2 + bit
            copies.append(pltpu.make_async_copy(piece.at[block], target.at[place], sems.at[len(copies)]))
    for copy in copies:
        copy.start()
    return copies


def lay_kernel(fsdp, pair, spread, *refs):
    count = 2 ** len(spread)
    target, sems = refs[count:]
    for copy in lay_copies(fsdp, pair, spread, refs[:count], target, sems):
        copy.wait()


def lay(pieces, fsdp, pair, spread):
    rows, cols = pieces[0].shape[1:]
    blocks = 4 * len(pieces)
    out = pl.pallas_call(
        functools.partial(lay_kernel, fsdp, pair, spread),
        out_shape=jax.ShapeDtypeStruct((blocks, rows, cols), bf16),
        in_specs=[pl.BlockSpec(memory_space=pltpu.HBM)] * len(pieces),
        out_specs=pl.BlockSpec(memory_space=pltpu.VMEM),
        scratch_shapes=[pltpu.SemaphoreType.DMA((blocks,))],
        compiler_params=pltpu.CompilerParams(vmem_limit_bytes=32 << 20),
        cost_estimate=pl.CostEstimate(
            flops=0, transcendentals=0, bytes_accessed=4 * blocks * rows * cols
        ),
    )(*pieces)
    return out.reshape(blocks * rows, cols)


def tokens_kernel(pair, value_ref, out_ref, send_sems, recv_sems):
    core = lax.axis_index("c")
    me = place_of(*pair)
    one, two = pair
    half = value_ref.shape[0] // 2
    sender = Sender(send_sems, recv_sems)
    out_ref[me, core] = value_ref[...]
    meet([(two,), (one,), ("c",)])

    def send(place, axes, rows=slice(None)):
        mine = out_ref.at[place, core, rows]
        return sender.start(mine, mine, axes)

    near = send(me, (two,))
    wide = send(me, (one,))
    got = [send(me, ("c",))]
    near.wait_recv()
    far = [send(me ^ 1, (one,), slice(0, half))]
    got.append(send(me ^ 1, ("c",)))
    wide.wait_recv()
    far.append(send(me ^ 2, (two,), slice(half, 2 * half)))
    got.append(send(me ^ 2, ("c",)))
    for copy in far:
        copy.wait_recv()
    got.append(send(me ^ 3, ("c",)))
    for copy in got:
        copy.wait_recv()
    sender.finish()


def tokens_of_chips(value, pair):
    rows, cols = value.shape
    vmem = pl.BlockSpec(memory_space=pltpu.VMEM)
    out = pl.pallas_call(
        functools.partial(tokens_kernel, pair),
        out_shape=jax.ShapeDtypeStruct((4, 2, rows, cols), bf16),
        in_specs=[vmem],
        out_specs=vmem,
        scratch_shapes=[pltpu.SemaphoreType.DMA((8,)), pltpu.SemaphoreType.DMA((8,))],
        compiler_params=pltpu.CompilerParams(
            collective_id=1, has_side_effects=True, vmem_limit_bytes=24 << 20
        ),
    )(value)
    return out.reshape(8 * rows, cols)


def merge_kernel(which, parts_ref, out_ref):
    cols = out_ref.shape[1] // 4
    for quarter in range(4):
        out_ref[:, quarter * cols : (quarter + 1) * cols] = parts_ref[0, quarter].astype(f32)


def merge(parts, which):
    rows, cols = parts.shape[2:]
    return pl.pallas_call(
        functools.partial(merge_kernel, which),
        grid=(1,),
        out_shape=jax.ShapeDtypeStruct((rows, 4 * cols), f32),
        in_specs=[pl.BlockSpec((1, 4, rows, cols), lambda i: (which, 0, 0, 0))],
        out_specs=pl.BlockSpec((rows, 4 * cols), lambda i: (0, 0)),
        cost_estimate=pl.CostEstimate(
            flops=0, transcendentals=0, bytes_accessed=24 * rows * cols
        ),
    )(parts)


class Reduction:
    def __init__(self, sender, held, dims, order, buffers, out):
        self.sender, self.held, self.dims, self.order = sender, held, list(dims), list(order)
        self.buffers, self.out = list(buffers), out

    def half(self, at):
        return (slice(None),) * self.dims.index(self.order[0]) + (at,)

    def begin(self):
        axis = self.order[0]
        source = self.held.at[self.half(1 - lax.axis_index(axis))]
        self.copy = self.sender.start(source, self.buffers[0], (axis,))

    def end(self):
        self.copy.wait_recv()
        axis = self.order[0]
        own = self.held[self.half(lax.axis_index(axis))]
        total = own.astype(f32) + self.buffers[0][...].astype(f32)
        self.held = self.buffers.pop(0)
        self.dims.remove(axis)
        self.order.pop(0)
        if self.order:
            self.held[...] = total.astype(bf16)
            self.begin()
        else:
            self.out[...] = total

    def finish(self):
        while self.order:
            self.end()


def halves_of(rows):
    half = rows // 2 // 16 * 16
    return pl.ds(0, half), pl.ds(half, rows - half)


def last_kernel(
    fsdp,
    pair,
    peak_ref,
    small_ref,
    gains_ref,
    q_ref,
    kv_ref,
    out_ref,
    down_ref,
    gate_ref,
    up_ref,
    small_sum,
    gains_sum,
    q_sum,
    kv_sum,
    out_sum,
    ffn_out,
    peak_out,
    *scratch,
):
    scratch = list(scratch)
    stages = len(fsdp)
    sender = Sender(scratch.pop(), scratch.pop())

    def buffers(count):
        taken = scratch[:count]
        del scratch[:count]
        return taken

    down = list(reversed(fsdp))
    turned = [down[1], down[0]] + down[2:]
    with_core = fsdp + ["c"]
    small = Reduction(sender, small_ref, with_core, ["c"] + turned, buffers(stages + 1), small_sum)
    gains = Reduction(sender, gains_ref, with_core, ["c"] + down, buffers(stages + 1), gains_sum)
    q = Reduction(sender, q_ref, fsdp, down, buffers(stages), q_sum)
    kv = Reduction(sender, kv_ref, fsdp, down, buffers(stages), kv_sum)
    outs = []
    for rows in halves_of(out_sum.shape[0]):
        part = out_ref.at[(slice(None),) * stages + (rows,)]
        outs.append(Reduction(sender, part, fsdp, turned, buffers(stages), out_sum.at[rows]))
    over = buffers(1)[0]
    peaks = buffers(stages)
    me = place_of(*pair)
    row = lax.axis_index(fsdp[0])
    meet([(axis,) for axis in with_core] + [pair])

    def send_columns(which, held):
        ffn_out[which, me] = held[me]
        return [
            sender.start(held.at[me ^ away], ffn_out.at[which, me], axes)
            for away, axes in ((1, (pair[1],)), (2, (pair[0],)), (3, pair))
        ]

    peak_out[...] = peak_ref[...]

    def send_peaks(stage):
        return sender.start(peak_out, peaks[stage], (fsdp[stage],))

    def next_peaks(stage, sent):
        sent.wait()
        sender.left.append(sent)
        peak_out[...] = jnp.maximum(peak_out[...], peaks[stage][...])
        return send_peaks(stage + 1) if stage < stages - 1 else None

    for part in (small, gains, q, outs[0], kv):
        part.begin()
    peak_sent = send_peaks(0)
    crossing = sender.start(up_ref.at[1 - row], over, (fsdp[0],))
    outs[1].begin()
    columns = send_columns(0, down_ref)
    small.end()
    gains.end()
    columns += send_columns(1, gate_ref)
    peak_sent = next_peaks(0, peak_sent)
    for part in (q, kv, outs[0]):
        part.end()
    crossing.wait_recv()
    over[...] = (up_ref[row].astype(f32) + over[...].astype(f32)).astype(bf16)
    columns += send_columns(2, over)
    for stage in range(1, stages):
        peak_sent = next_peaks(stage, peak_sent)
        for part in (outs[1], small, gains, q, kv, outs[0]):
            part.end()
    for reduction in (q, kv, outs[0], small, gains, outs[1]):
        reduction.finish()
    for copy in columns:
        copy.wait_recv()
    sender.finish()


def last_scatter(fsdp, pair, peak, small, gains, q, kv, out, down, gate, up):
    vmem = pl.BlockSpec(memory_space=pltpu.VMEM)
    stages = len(fsdp)

    def buffers(array, count, rows=None):
        lead = array.ndim - 2
        block = (rows or array.shape[-2], array.shape[-1])
        return [pltpu.VMEM((2,) * (lead - 1 - i) + block, bf16) for i in range(count)]

    scratch = (
        buffers(small, stages + 1)
        + buffers(gains, stages + 1)
        + buffers(q, stages)
        + buffers(kv, stages)
        + [buf for rows in halves_of(out.shape[-2]) for buf in buffers(out, stages, rows.size)]
        + [pltpu.VMEM(down.shape, bf16)]
        + [pltpu.VMEM(peak.shape, f32)] * stages
    )
    copies = 2 * (stages + 1) + 4 * stages + 1 + 9 + stages
    return pl.pallas_call(
        functools.partial(last_kernel, fsdp, pair),
        out_shape=tuple(jax.ShapeDtypeStruct(x.shape[-2:], f32) for x in (small, gains, q, kv, out))
        + (
            jax.ShapeDtypeStruct((3,) + down.shape, bf16),
            jax.ShapeDtypeStruct(peak.shape, f32),
        ),
        in_specs=[vmem] * 9,
        out_specs=(vmem,) * 7,
        scratch_shapes=scratch
        + [pltpu.SemaphoreType.DMA((copies,)), pltpu.SemaphoreType.DMA((copies,))],
        compiler_params=pltpu.CompilerParams(
            collective_id=2, has_side_effects=True, vmem_limit_bytes=60 << 20
        ),
    )(peak, small, gains, q, kv, out, down, gate, up)


def shards(
    fsdp,
    hidden_in,
    seq_ids,
    block_ids,
    clip_limit,
    cotangent,
    q_down,
    kv_down,
    q_up,
    kv_up,
    out_proj,
    gate_proj,
    up_proj,
    down_proj,
    in_gain,
    q_gain,
    kv_gain,
    post_gain,
):
    tokens_here, width = hidden_in.shape
    seq_row = seq_ids[0]
    block_row = block_ids[0]
    group = seq_row.shape[0]
    heads = q_up.shape[1] // (NOPE + ROPE)
    score_scale = 1.0 / math.sqrt(NOPE + ROPE)
    core = lax.axis_index("c")
    first_row = core * tokens_here
    wide, near = fsdp[1], fsdp[-1]
    pair = (wide, near)
    spread = [axis for axis in fsdp if axis not in pair]
    squares = [(fsdp[i], fsdp[i + 1]) for i in range(0, len(fsdp), 2)]
    at_wide, at_near = lax.axis_index(wide), lax.axis_index(near)
    chips = tuple(fsdp)
    count = 2 ** len(fsdp)

    small_rows = q_down.shape[0]
    q_rank = q_down.shape[1]
    small_cols = q_rank + kv_down.shape[1]

    def row(value):
        return jnp.pad(value, ((0, 0), (0, TILE - value.shape[1])))[:, None, :]

    def rows_of(*values):
        held = jnp.concatenate([row(value) for value in values], axis=1)
        return jnp.pad(held, ((0, 0), (0, 8 - len(values)), (0, 0)))

    small = jnp.concatenate([q_down, kv_down], axis=1)
    gains = rows_of(in_gain[None], post_gain[None], q_gain[None], kv_gain[None])[0]
    q_up_wide = jnp.pad(
        q_up.reshape(-1, heads, NOPE + ROPE), ((0, 0), (0, 0), (0, TILE - NOPE - ROPE))
    ).reshape(-1, heads * TILE)
    small_all, gains_all, q_up_all, kv_up_all, gate_held, others_held = first_gather(
        squares, pair, spread, small, gains, q_up_wide, kv_up, gate_proj, up_proj, down_proj
    )
    down_full = small_all.reshape(-1, small_cols)
    q_up_full = q_up_all.reshape(-1, heads * TILE)
    kv_up_full = kv_up_all.reshape(-1, kv_up.shape[1])
    devices = 2 * count

    def gain(at, size):
        return gains_all.reshape(devices, 8, TILE)[:, at, :size].reshape(-1).astype(f32)

    in_float = gain(0, in_gain.shape[0])
    post_float = gain(1, post_gain.shape[0])
    q_gain_float = gain(2, q_gain.shape[0])
    kv_gain_float = gain(3, kv_gain.shape[0])

    out_full = lax.all_gather(after(out_proj, gains_all), chips, axis=0, tiled=True)
    cot_float = cotangent.astype(f32)

    def over(pieces, axis, *ready):
        return [swap(after(piece, *ready), axis) for piece in pieces]

    def exchange(held, dims, axis):
        at, dim = lax.axis_index(axis), dims.index(axis)
        return swap(pick(held, 1 - at, dim), axis), pick(held, at, dim)

    def sum_of_cores(value):
        held = value.reshape(2, 2, 2, tokens_here, width)
        other = swap(pick(held, 1 - core, 2), "c")
        return (pick(held, core, 2).astype(f32) + other.astype(f32)).astype(bf16)

    def sum_of_chips(held):
        return square_scatter(held, wide, near, 0).reshape(tokens_here, width)

    def core_both(value):
        return both(value, swap(value, "c"), "c", 0)

    def core_sum(value):
        def rows(at):
            return lax.dynamic_slice_in_dim(value, at * tokens_here, tokens_here)

        return rows(core) + swap(rows(1 - core), "c")

    x_float = hidden_in.astype(f32)
    x_normed = rms_scale(x_float, in_float).astype(bf16)
    pre = jnp.dot(x_normed, down_full, preferred_element_type=f32)
    q_pre = pre[:, :q_rank]
    c_lat_pre = pre[:, q_rank : q_rank + KVR]
    c_rot_pre = pre[:, q_rank + KVR :]
    own_cos, own_sin = angles(seq_row, first_row, tokens_here)
    q_latent = rms_scale(q_pre, q_gain_float).astype(bf16)
    kv_latent = rms_scale(c_lat_pre, kv_gain_float).astype(bf16)
    key_rot = rotate(c_rot_pre, own_cos, own_sin).astype(bf16)
    key_rot = jnp.pad(key_rot, ((0, 0), (NOPE, TILE - NOPE - ROPE)))
    latents = core_both(jnp.concatenate([q_latent, kv_latent, key_rot], axis=1))
    q_lat_all = latents[:, :q_rank]
    kv_lat_all = latents[:, q_rank : q_rank + KVR]
    key_rot_all = latents[:, q_rank + KVR :]
    all_cos, all_sin = angles(seq_row, 0, group)
    q_full = jnp.dot(q_lat_all, q_up_full, preferred_element_type=f32)
    kv_full = jnp.dot(kv_lat_all, kv_up_full, preferred_element_type=f32).astype(bf16)
    allowed = (seq_row[None, :] == seq_row[:, None]) & (block_row[:, None] <= block_row[None, :])
    bias = jnp.where(allowed, 0.0, -1e30).astype(f32)
    axes = list(spread)
    gate_pieces = [gate_held[0], gate_held[1]]
    up_pieces = [others_held[0]]
    down_pieces = [others_held[1]]
    up_pieces += over(up_pieces, axes[0])
    for axis in axes[1:]:
        gate_pieces += over(gate_pieces, axis)
    q_full, *early = lax.optimization_barrier((q_full, *gate_pieces, *up_pieces))
    gate_pieces, up_pieces = early[: len(gate_pieces)], early[len(gate_pieces) :]
    attn, queries, log_total, local_peak = attend(
        q_full, kv_full, key_rot_all, tables(all_cos, all_sin), bias, score_scale
    )
    down_pieces += over(down_pieces, axes[0], q_full)
    for axis in axes[1:]:
        up_pieces += over(up_pieces, axis)
    d_ffn = (resid_scale * cot_float).astype(bf16)
    d_ffn_all = lax.all_gather(after(d_ffn, attn), (wide, near, "c"), axis=0, tiled=True)
    branch = core_sum(contract(attn, out_full, 1, 1))
    mid = x_float + resid_scale * branch
    mid_normed = rms_scale(mid, post_float).astype(bf16)
    gate_full = lay([after(piece, attn) for piece in gate_pieces], fsdp, pair, spread)
    mid_all = tokens_of_chips(after(mid_normed, gate_full, *down_pieces), pair)
    for axis in axes[1:]:
        down_pieces += over(down_pieces, axis, mid_all)
    gate = jnp.dot(mid_all, gate_full, preferred_element_type=f32)
    up_full = lay([after(piece, gate) for piece in up_pieces], fsdp, pair, spread)
    up_value = jnp.dot(mid_all, up_full, preferred_element_type=f32)
    down_proj_full = lay([after(piece, up_value) for piece in down_pieces], fsdp, pair, spread)
    sigmoid = jax.nn.sigmoid(gate)
    silu_value = gate * sigmoid
    act = (silu_value * up_value).astype(bf16)

    d_act = jnp.dot(d_ffn_all, down_proj_full, preferred_element_type=f32)
    d_gate = (d_act * up_value * (sigmoid * (1.0 + gate * (1.0 - sigmoid)))).astype(bf16)
    d_up = (d_act * silu_value).astype(bf16)
    dims = list(fsdp)
    first, last = spread[0], spread[-1]
    held_shape = [2] * len(fsdp) + [width // count, -1]

    def added(parts):
        return (parts[0].astype(f32) + parts[1].astype(f32)).astype(bf16)

    def inner(held):
        left = [axis for axis in dims if axis != last]
        for axis in reversed(spread[1:-1]):
            held = added(exchange(held, left, axis))
            left.remove(axis)
        return held

    def begin(grad):
        return exchange(grad.reshape(held_shape), dims, last)

    def cross(held):
        return exchange(held, [first, *pair], first)

    down_grad = rows_first(contract(d_ffn_all, act, 0, 0).astype(bf16))
    down_parts = begin(down_grad)
    d_gate_late, d_up_late, _ = lax.optimization_barrier((d_gate, d_up, down_grad))
    d_mid_part = (
        contract(d_gate_late, gate_full, 1, 1) + contract(d_up_late, up_full, 1, 1)
    ).astype(bf16)
    d_mid_held = sum_of_cores(d_mid_part)
    d_mid_normed = sum_of_chips(d_mid_held)
    mid_late, down_got, down_kept, _ = lax.optimization_barrier(
        (mid_all, *down_parts, d_mid_held)
    )
    gate_grad = rows_first(contract(mid_late, d_gate, 0, 0).astype(bf16))
    gate_parts = begin(gate_grad)
    down_parts = cross(inner(added((down_got, down_kept))))
    up_grad = rows_first(contract(after(mid_late, gate_grad), d_up, 0, 0).astype(bf16))
    up_parts = begin(up_grad)
    ffn_part = contract(after(act, up_grad), down_proj_full, 1, 1).astype(bf16)
    post_pull = jax.vjp(rms_scale, mid, post_float)[1]
    d_mid_norm, post_grad = post_pull(after(d_mid_normed, up_grad, ffn_part))
    ffn = lax.psum_scatter(
        after(ffn_part, d_mid_norm), (wide, near, "c"), scatter_dimension=0, tiled=True
    )
    layer_out = (mid + resid_scale * ffn.astype(f32)).astype(bf16)
    d_mid = cot_float + d_mid_norm
    d_branch = (resid_scale * d_mid).astype(bf16)
    d_branch_all = core_both(d_branch)
    d_attn = jnp.dot(d_branch_all, out_full, preferred_element_type=f32).astype(bf16)
    d_attn_late, gate_got, gate_kept, *down_parts = lax.optimization_barrier(
        (d_attn, *gate_parts, *down_parts)
    )
    gate_parts = cross(inner(added((gate_got, gate_kept))))
    d_q, d_kv, d_rot_part = attend_back(
        queries,
        kv_full,
        d_attn_late,
        log_total,
        key_rot_all,
        tables(all_cos, -all_sin),
        bias,
        score_scale,
    )
    out_grad = rows_first(contract(after(d_branch_all, d_q), attn, 0, 0).astype(bf16))
    q_lat_late, *up_parts = lax.optimization_barrier((q_lat_all, *up_parts))
    q_up_grad = heads_grad(q_lat_late, d_q)
    kv_up_grad = rows_first(contract(kv_lat_all, d_kv, 0, 0).astype(bf16))
    d_q_lat_part = contract(d_q, q_up_full, 1, 1)
    d_kv_lat_part = contract(d_kv, kv_up_full, 1, 1)
    d_latents = core_sum(jnp.concatenate([d_q_lat_part, d_kv_lat_part, d_rot_part], axis=1))
    q_pull = jax.vjp(rms_scale, q_pre, q_gain_float)[1]
    d_q_pre, q_gain_grad = q_pull(d_latents[:, :q_rank])
    kv_pull = jax.vjp(rms_scale, c_lat_pre, kv_gain_float)[1]
    d_c_lat, kv_gain_grad = kv_pull(d_latents[:, q_rank : q_rank + KVR])
    d_key_rot = d_latents[:, q_rank + KVR + NOPE : q_rank + KVR + NOPE + ROPE]
    d_pre = jnp.concatenate(
        [d_q_pre, d_c_lat, rotate(d_key_rot, own_cos, -own_sin)], axis=-1
    ).astype(bf16)
    down_grads = rows_first(contract(x_normed, d_pre, 0, 0).astype(bf16))
    d_x_normed = contract(d_pre, down_full, 1, 1)
    in_pull = jax.vjp(rms_scale, x_float, in_float)[1]
    d_x_norm, in_grad = in_pull(d_x_normed)
    input_grad = d_mid + d_x_norm

    rows_here = width // count
    ffn_held = [
        added(down_parts).reshape(4, rows_here, -1),
        added(gate_parts).reshape(4, rows_here, -1),
        inner(added(up_parts)).reshape(2, 4, rows_here, -1),
    ]
    gain_grads = rows_of(
        *(grad.reshape(devices, -1) for grad in (in_grad, post_grad, q_gain_grad, kv_gain_grad))
    ).astype(bf16)

    def blocks(grad, lead):
        return grad.reshape([2] * lead + [grad.shape[0] // 2**lead, -1])

    small_out, gain_out, q_up_out, kv_up_out, out_out, ffn_cols, peak_all = last_scatter(
        fsdp,
        pair,
        local_peak,
        blocks(down_grads, len(fsdp) + 1),
        gain_grads.reshape([2] * (len(fsdp) + 1) + [8, TILE]),
        blocks(q_up_grad, len(fsdp)),
        blocks(kv_up_grad, len(fsdp)),
        blocks(out_grad, len(fsdp)),
        *ffn_held,
    )
    down_out, gate_out, up_out = (merge(ffn_cols, which) for which in range(3))
    peaks = peak_all[0, :heads]
    limit = clip_limit[0]
    factors = limit / jnp.maximum(peaks, limit)
    root = jnp.sqrt(factors)
    q_cols = jnp.concatenate(
        [
            jnp.broadcast_to(root[:, None], (heads, NOPE)),
            jnp.broadcast_to(factors[:, None], (heads, ROPE)),
        ],
        axis=1,
    ).reshape(heads * (NOPE + ROPE))
    kv_cols = jnp.concatenate(
        [jnp.broadcast_to(root[:, None], (heads, NOPE)), jnp.ones((heads, VD), f32)], axis=1
    ).reshape(heads * (NOPE + VD))
    q_clipped = (q_up.astype(f32) * q_cols[None, :]).astype(bf16)
    kv_clipped = (kv_up.astype(f32) * kv_cols[None, :]).astype(bf16)
    return (
        layer_out,
        input_grad,
        small_out[:, :q_rank],
        small_out[:, q_rank:],
        q_up_out,
        kv_up_out,
        out_out,
        gate_out,
        up_out,
        down_out,
        gain_out[0, : in_gain.shape[0]],
        gain_out[2, : q_gain.shape[0]],
        gain_out[3, : kv_gain.shape[0]],
        gain_out[1, : post_gain.shape[0]],
        q_clipped,
        kv_clipped,
        peaks,
        factors,
    )


def solution(mesh):
    bits = mesh.shape["fsdp"].bit_length() - 1
    fsdp = [f"f{i}" for i in range(bits)]
    fine = Mesh(mesh.devices.reshape((2,) * (bits + 1)), tuple(fsdp) + ("c",))
    split = tuple(fsdp)
    whole = split + ("c",)
    return jax.shard_map(
        functools.partial(shards, fsdp),
        mesh=fine,
        in_specs=(
            P(whole, None),
            P(split, None),
            P(split, None),
            P(),
            P(whole, None),
            P(whole, None),
            P(whole, None),
            P(split, "c"),
            P(split, "c"),
            P(split, "c"),
            P(split, "c"),
            P(split, "c"),
            P(split, "c"),
            P(whole),
            P(whole),
            P(whole),
            P(whole),
        ),
        out_specs=(
            P(whole, None),
            P(whole, None),
            P(whole, None),
            P(whole, None),
            P(split, "c"),
            P(split, "c"),
            P(split, "c"),
            P(split, "c"),
            P(split, "c"),
            P(split, "c"),
            P(whole),
            P(whole),
            P(whole),
            P(whole),
            P(split, "c"),
            P(split, "c"),
            P("c"),
            P("c"),
        ),
        check_vma=False,
    )
```

time: 1520 us -> 1130 us (0.74)
  Pallas kernels: 0 us -> 438 us
  waiting for transfers between devices: 669 us -> 323 us
  matrix products: 363 us -> 192 us
  local copies, waits for them, and re-layouts: 216 us -> 63.7 us
  other arithmetic: 172 us -> 63.4 us
  starting transfers between devices: 90.1 us -> 19.2 us
    pallas_call x0 -> x12, Pallas kernels: none -> 438 us  [the longest x1 193 us: last_scatter(): pl.pallas_call(functools.partial(last_kernel, fsdp, pair), out_shape=tupl...]
    ppermute x84 -> x20, waiting for transfers between devices: 619 us -> 269 us  [swap(): return lax.ppermute(value, axis, SWAP)]
    dot_general x37 -> x2, matrix products: 169 us -> 3.04 us  [the longest x1 2.2 us: shards(): q_full = jnp.dot(q_lat_all, q_up_full, preferred_element_type=f32)]
    ppermute x84 -> x20, starting transfers between devices: 74.1 us -> 16.6 us  [swap(): return lax.ppermute(value, axis, SWAP)]
    concatenate x11 -> x7, local copies, waits for them, and re-layouts: 38.7 us -> 1.7 us  [the longest x1 1.4 us: shards(): jnp.concatenate([d_q_pre, d_c_lat, rotate(d_key_rot, own_cos, -own_sin)],...]
    add x19 -> x1, other arithmetic: 31.3 us -> 0.12 us  [core_sum(): return rows(core) + swap(rows(1 - core), 'c')]
    slice x13 -> x3, local copies, waits for them, and re-layouts: 31.5 us -> 0.7 us  [the longest x1 0.66 us: shards(): small_out[:, q_rank:]]
    select_n x41 -> x1, other arithmetic: 29.8 us -> 1.88 us  [both(): jnp.where(here, own, other)]
  transfers between devices with their start and end apart: 94 -> 24, of which waited for: 42 -> 16; matrix products, arithmetic and copies ran while one was open for 41% -> 15% of each run, Pallas kernels for 0% -> 28%
where the time goes in v2:
time: 1130 us; the launch traced here: 1120 us
  Pallas kernels  438 us (39%)
  waiting for transfers between devices  323 us (29%)
  matrix products  192 us (17%)
  local copies, waits for them, and re-layouts  63.7 us (6%)
  other arithmetic  63.4 us (6%)
  starting transfers between devices  19.2 us (2%)
  between operations  16.3 us (1%)
    ppermute x20, waiting for transfers between devices, swap(): return lax.ppermute(value, axis, SWAP)  269 us
    pallas_call x1, Pallas kernels, last_scatter(): pl.pallas_call(functools.partial(last_kernel, fsdp, pair), out_shape=tupl...  193 us
    dot_general x13, matrix products, contract(): lax.dot_general(left, right, (((left_dim,), (right_dim,)), ((), ())), pre...  128 us
    pallas_call x1, Pallas kernels, first_gather(): pl.pallas_call(functools.partial(first_kernel, squares, pair, spread), ou...  125 us
    pallas_call x1, Pallas kernels, tokens_of_chips(): pl.pallas_call(functools.partial(tokens_kernel, pair), out_shape=jax.Shap...  62.9 us
    unnamed x218, local copies, waits for them, and re-layouts  41.2 us
    ppermute x1, waiting for transfers between devices, far(): return lax.ppermute(value, pair, [(i, 3 - i) for i in range(4)])  28 us
    all_gather x1, waiting for transfers between devices, shards(): lax.all_gather(after(out_proj, gains_all), chips, axis=0, tiled=True)  26.1 us
  transfers between devices with their start and end apart: 24, of which 16 were waited for; matrix products, arithmetic and copies ran while one was open for 15% of the time, Pallas kernels for 28%

profile of v2, /device:TPU:0, one launch (start us, length us, event | category | flops | bytes accessed | tf_op | source)
XLA Modules:
  0.0 1115.4 jit_solution(8930398513686778369)
XLA Ops:
  14.4 125.2 %shard_map.304 = (bf16[4,4,2,80,1056]{4,3,2,1,0:T(8,128)(2,1)}, bf16[4,4,2,8,128]{4,3,2,1,0:T(8,128)(2,1)S(1)}, bf16[4,4,48,2560]{3,2,1,0:T(8,128)(2,1)}, bf16[4...) custom-call(bf16[80,1056]{1,0:T(8,128)(2,1)S(1)} %pad_maximum_fusion.2.small_ref, ...), custom_call_target="tpu_custom_call" | custom-call | tf_op jit(solution)/shard_map/pallas_call | solution.py:453
  171.9 13.0 %collective-permute-done.1.refs_2_ = bf16[4,160,800]{2,1,0:T(8,128)(2,1)} collective-permute-done((bf16[4,160,800]{2,1,0:T(8,128)(2,1)}, bf16[4,160,800]{2,1,0:T(8,128)(2,1)}, u32[]{:S(2)}, u32[]{:S(2)}) %collective-permute-start.1) | collective-permute-done | bytes 1024032 | tf_op jit(solution)/shard_map/ppermute | solution.py:231
  184.8 30.1 %collective-permute-done.2.refs_3_ = bf16[4,160,800]{2,1,0:T(8,128)(2,1)} collective-permute-done((bf16[4,160,800]{2,1,0:T(8,128)(2,1)S(1)}, bf16[4,160,800]{2,1,0:T(8,128)(2,1)}, u32[]{:S(2)}, u32[]{:S(2)}) %collective-permute-start.2) | collective-permute-done | bytes 1024032 | tf_op jit(solution)/shard_map/ppermute | solution.py:231
  214.9 14.6 %collective-permute-done.3.refs_1_ = bf16[4,160,800]{2,1,0:T(8,128)(2,1)} collective-permute-done((bf16[4,160,800]{2,1,0:T(8,128)(2,1)S(1)}, bf16[4,160,800]{2,1,0:T(8,128)(2,1)}, u32[]{:S(2)}, u32[]{:S(2)}) %collective-permute-start.3) | collective-permute-done | bytes 1024032 | tf_op jit(solution)/shard_map/ppermute | solution.py:231
  229.5 16.5 %shard_map.305 = (bf16[512,1280]{1,0:T(8,128)(2,1)S(1)}, bf16[512,2560]{1,0:T(8,128)(2,1)S(1)}, f32[10,2,512]{2,1,0:T(2,128)S(1)}, f32[8,128]{1,0:T(8,128)S(1)}) custom-call(f32[512,2560]{1,0:T(8,128)S(1)} %fusion.51.q_ref, bf16[512,2560]{1,0:T(8,128)(2,1)S(1)} %convolution_convert_fusion.6.kv_ref, bf16[512,128]{1,0:T(8,128)(2,1)S(1)} %pad_maximum_fusion.3.rot_ref, ...), custom_call_target="tpu_custom_call" | custom-call | flops 2684354560 | bytes 15728640 | tf_op jit(solution)/shard_map/pallas_call | solution.py:122
  249.3 26.1 %all-gather.3.cloned.1.call-done = bf16[2560,1280]{1,0:T(8,128)(2,1)} async-done(((bf16[160,1280]{1,0:T(8,128)(2,1)}), bf16[2560,1280]{1,0:T(8,128)(2,1)}) %all-gather.3.cloned.1.call-update) | async-done | bytes 6553616 | tf_op jit(solution)/shard_map/all_gather | solution.py:817
  275.4 6.5 fusion.52
  295.4 43.4 %collective-permute-done.5.refs_1_ = bf16[4,160,800]{2,1,0:T(8,128)(2,1)S(1)} collective-permute-done((bf16[4,160,800]{2,1,0:T(8,128)(2,1)S(1)}, bf16[4,160,800]{2,1,0:T(8,128)(2,1)S(1)}, u32[]{:S(2)}, u32[]{:S(2)}) %collective-permute-start.5) | collective-permute-done | bytes 1024032 | tf_op jit(solution)/shard_map/ppermute | solution.py:231
  338.7 62.9 %shard_map.307 = bf16[4,2,256,2560]{3,2,1,0:T(8,128)(2,1)S(1)} custom-call(bf16[256,2560]{1,0:T(8,128)(2,1)S(1)} %multiply_convert_fusion.4.value_ref), custom_call_target="tpu_custom_call" | custom-call | tf_op jit(solution)/shard_map/pallas_call | solution.py:552
  401.7 16.5 %fusion.53 = f32[2048,800]{0,1:T(8,128)} fusion(bf16[2048,2560]{1,0:T(8,128)(2,1)S(1)} %bitcast.125, bf16[2560,800]{1,0:T(8,128)(2,1)} %bitcast.135), kind=kOutput, calls=%fused_computation.180 | convolution fusion | flops 8388608000 | bytes 21135360 | tf_op jit(solution)/shard_map/dot_general | solution.py:888
  424.7 13.0 %fusion.54 = f32[2048,800]{0,1:T(8,128)} fusion(bf16[2048,2560]{1,0:T(8,128)(2,1)S(1)} %bitcast.126, bf16[2560,800]{1,0:T(8,128)(2,1)} %bitcast.137), kind=kOutput, calls=%fused_computation.181 | convolution fusion | flops 8388608000 | bytes 21135360 | tf_op jit(solution)/shard_map/dot_general | solution.py:890
  437.6 8.8 collective-permute-done.10.refs_3_
  446.5 24.0 %collective-permute-done.9.refs_2_ = bf16[4,160,800]{2,1,0:T(8,128)(2,1)} collective-permute-done((bf16[4,160,800]{2,1,0:T(8,128)(2,1)S(1)}, bf16[4,160,800]{2,1,0:T(8,128)(2,1)}, u32[]{:S(2)}, u32[]{:S(2)}) %collective-permute-start.9) | collective-permute-done | bytes 1024032 | tf_op jit(solution)/shard_map/ppermute | solution.py:231
  474.9 20.1 %multiply_convert_fusion = (bf16[2048,800]{0,1:T(8,128)(2,1)S(1)}, bf16[2048,800]{0,1:T(8,128)(2,1)}, bf16[2048,800]{0,1:T(8,128)(2,1)}) fusion(f32[2048,800]{0,1:T(8,128)} %fusion.53, f32[2048,800]{0,1:T(8,128)} %fusion.54, bf16[2048,2560]{1,0:T(8,128)(2,1)} %all-gather.5.cloned.1.call-done, bf16[2560,800]{1,0:T(8,128)(2,1)} %bitcast.131), kind=kOutput, calls=%fused_computation.5 | convolution fusion | flops 8413184000 | bytes 37519360 | tf_op jit(solution)/shard_map/dot_general | solution.py:896
  495.0 17.4 %convolution_convert_fusion.5 = bf16[2560,800]{1,0:T(8,128)(2,1)} fusion(bf16[2048,2560]{1,0:T(8,128)(2,1)} %all-gather.5.cloned.1.call-done, bf16[2048,800]{0,1:T(8,128)(2,1)} %get-tuple-element.117), kind=kOutput, calls=%fused_computation.12 | convolution fusion | flops 8390656000 | bytes 17858560 | tf_op jit(solution)/shard_map/dot_general | solution.py:51
  512.4 17.4 %fusion.55 = f32[2048,2560]{1,0:T(8,128)} fusion(bf16[2048,800]{0,1:T(8,128)(2,1)S(1)} %copy-done.96, bf16[2560,800]{1,0:T(8,128)(2,1)} %bitcast.136), kind=kOutput, calls=%fused_computation.182 | convolution fusion | flops 8388608000 | bytes 28344320 | tf_op jit(solution)/shard_map/dot_general | solution.py:51
  529.8 17.9 %add_convert_fusion = bf16[2048,2560]{1,0:T(8,128)(2,1)} fusion(f32[2048,2560]{1,0:T(8,128)} %fusion.55, bf16[2048,800]{0,1:T(8,128)(2,1)S(1)} %get-tuple-element.114, bf16[2560,800]{1,0:T(8,128)(2,1)} %bitcast.138), kind=kOutput, calls=%fused_computation | convolution fusion | flops 8399093760 | bytes 38830080 | tf_op jit(solution)/shard_map/dot_general | solution.py:51
  561.9 7.9 add_convert_fusion.1
  569.8 39.5 %collective-permute-done.8 = bf16[2,2,1,2,160,800]{5,4,3,1,2,0:T(8,128)(2,1)} collective-permute-done((bf16[2,2,1,2,160,800]{5,4,3,1,2,0:T(8,128)(2,1)S(1)}, bf16[2,2,1,2,160,800]{5,4,3,1,2,0:T(8,128)(2,1)}, u32[]{:S(2)}, u32[]{:S(2)}) %collective-permute-start.8) | collective-permute-done | bytes 2048032 | tf_op jit(solution)/shard_map/ppermute | solution.py:231
  609.3 16.8 %convolution_convert_fusion.4 = bf16[2560,800]{1,0:T(8,128)(2,1)} fusion(bf16[2048,2560]{1,0:T(8,128)(2,1)} %bitcast.127, bf16[2048,800]{0,1:T(8,128)(2,1)} %get-tuple-element.113), kind=kOutput, calls=%fused_computation.11 | convolution fusion | flops 8390656000 | bytes 17858560 | tf_op jit(solution)/shard_map/dot_general | solution.py:51
  626.2 15.2 %convolution_convert_fusion.3 = bf16[2560,800]{1,0:T(8,128)(2,1)} fusion(bf16[2048,2560]{1,0:T(8,128)(2,1)S(1)} %bitcast.130, bf16[2048,800]{0,1:T(8,128)(2,1)} %copy-done.95), kind=kOutput, calls=%fused_computation.10 | convolution fusion | flops 8390656000 | bytes 17858560 | tf_op jit(solution)/shard_map/dot_general | solution.py:51
  647.0 13.6 %convolution_convert_fusion.2 = bf16[2048,2560]{1,0:T(8,128)(2,1)} fusion(bf16[2048,800]{0,1:T(8,128)(2,1)S(1)} %copy-done.97, bf16[2560,800]{1,0:T(8,128)(2,1)S(1)} %bitcast.134), kind=kOutput, calls=%fused_computation.3 | convolution fusion | flops 8393850880 | bytes 17858560 | tf_op jit(solution)/shard_map/dot_general | solution.py:51
  660.6 14.0 %collective-permute-done.12 = bf16[1,1,1,256,2560]{4,3,2,1,0:T(8,128)(2,1)} collective-permute-done((bf16[1,1,1,256,2560]{4,3,2,1,0:T(8,128)(2,1)}, bf16[1,1,1,256,2560]{4,3,2,1,0:T(8,128)(2,1)}, u32[]{:S(2)}, u32[]{:S(2)}) %collective-permute-start.12) | collective-permute-done | bytes 1310752 | tf_op jit(solution)/shard_map/ppermute | solution.py:231
  675.5 28.0 %collective-permute-done.14 = bf16[1,1,1,256,2560]{4,3,2,1,0:T(8,128)(2,1)} collective-permute-done((bf16[1,1,1,256,2560]{4,3,2,1,0:T(8,128)(2,1)}, bf16[1,1,1,256,2560]{4,3,2,1,0:T(8,128)(2,1)}, u32[]{:S(2)}, u32[]{:S(2)}) %collective-permute-start.14) | collective-permute-done | bytes 1310752 | tf_op jit(solution)/shard_map/ppermute | solution.py:235
  730.4 38.5 %collective-permute-done.19 = bf16[2,2,1,2,160,800]{5,4,3,1,0,2:T(8,128)(2,1)} collective-permute-done((bf16[2,2,1,2,160,800]{5,4,3,1,0,2:T(8,128)(2,1)}, bf16[2,2,1,2,160,800]{5,4,3,1,0,2:T(8,128)(2,1)}, u32[]{:S(2)}, u32[]{:S(2)}) %collective-permute-start.19) | collective-permute-done | bytes 2048032 | tf_op jit(solution)/shard_map/ppermute | solution.py:231
  775.2 7.0 convolution_convert_fusion.8.d_mixed_ref
  782.2 33.3 %collective-permute-done.16 = bf16[2,2,1,2,160,800]{5,4,3,1,2,0:T(8,128)(2,1)} collective-permute-done((bf16[2,2,1,2,160,800]{5,4,3,1,2,0:T(8,128)(2,1)}, bf16[2,2,1,2,160,800]{5,4,3,1,2,0:T(8,128)(2,1)}, u32[]{:S(2)}, u32[]{:S(2)}) %collective-permute-start.16) | collective-permute-done | bytes 2048032 | tf_op jit(solution)/shard_map/ppermute | solution.py:231
  821.2 21.1 %shard_map.310 = (bf16[512,2560]{1,0:T(8,128)(2,1)S(1)}, bf16[512,2560]{1,0:T(8,128)(2,1)S(1)}, f32[512,128]{1,0:T(8,128)S(1)}) custom-call(bf16[512,2560]{1,0:T(8,128)(2,1)S(1)} %copy-done.31, bf16[512,2560]{1,0:T(8,128)(2,1)S(1)} %copy-done.2, bf16[512,1280]{1,0:T(8,128)(2,1)S(1)} %convolution_convert_fusion.8.d_mixed_ref, ...), custom_call_target="tpu_custom_call" | custom-call | flops 6710886400 | bytes 10485760 | tf_op jit(solution)/shard_map/pallas_call | solution.py:199
  877.0 6.6 fusion.4
  884.6 5.8 convolution_convert_fusion.1
  890.5 192.7 %shard_map.312 = (f32[80,1056]{1,0:T(8,128)}, f32[8,128]{1,0:T(8,128)}, f32[48,1920]{1,0:T(8,128)}, f32[16,2560]{1,0:T(8,128)}, f32[160,1280]{1,0:T(8,128)}, /*i...) custom-call(f32[8,128]{1,0:T(8,128)} %copy-done.29, bf16[2,2,2,2,2,80,1056]{6,5,4,3,2,1,0:T(8,128)(2,1)} %bitcast.146, ...), custom_call_target="tpu_custom_call" | custom-call | tf_op jit(solution)/shard_map/pallas_call | solution.py:732
  1097.6 5.7 fusion.6
  (383 shorter events, 180.0 us)
Async XLA Ops:
  7.2 268.2 %all-gather.3.cloned.1.call-start = ((), (), s32[]{:S(2)}) async-start(), calls=%async_computation.1 | async-start | bytes 6963200 | tf_op jit(solution)/shard_map/all_gather | solution.py:817
  8.7 132.3 %copy-start.69 = (s32[1,512]{1,0:T(1,128)S(1)}, s32[1,512]{1,0:T(1,128)}, u32[]{:S(2)}) copy-start(s32[1,512]{1,0:T(1,128)} %param.18) | copy-start | bytes 6148
  14.4 126.9 %copy-start.36 = (bf16[256,2560]{1,0:T(8,128)(2,1)S(1)}, bf16[256,2560]{1,0:T(8,128)(2,1)}, u32[]{:S(2)}) copy-start(bf16[256,2560]{1,0:T(8,128)(2,1)} %param.17) | copy-start | bytes 3932164
  140.7 334.2 %all-gather.5.cloned.1.call-start = ((), (), s32[]{:S(2)}) async-start(), calls=%async_computation.2 | async-start | bytes 11796480 | tf_op jit(solution)/shard_map/all_gather | solution.py:880
  155.2 9.1 collective-permute-start
  156.5 28.4 %collective-permute-start.1 = (bf16[4,160,800]{2,1,0:T(8,128)(2,1)}, bf16[4,160,800]{2,1,0:T(8,128)(2,1)}, u32[]{:S(2)}, u32[]{:S(2)}) collective-permute-start(bf16[4,160,800]{2,1,0:T(8,128)(2,1)} %get-tuple-element.91.refs_0_), channel_id=1, source_target_pairs={{0,4},{4,0},{1,5},{5,1},{2,6},{6,2},{3,7},{7,3},{8,12},{12,8},{9,1... | collective-permute-start | bytes 3072008 | tf_op jit(solution)/shard_map/ppermute | solution.py:231
  158.0 56.9 %collective-permute-start.2 = (bf16[4,160,800]{2,1,0:T(8,128)(2,1)S(1)}, bf16[4,160,800]{2,1,0:T(8,128)(2,1)}, u32[]{:S(2)}, u32[]{:S(2)}) collective-permute-start(bf16[4,160,800]{2,1,0:T(8,128)(2,1)S(1)} %get-tuple-element.93.refs_1_), channel_id=1, source_target_pairs={{0,4},{4,0},{1,5},{5,1},{2,6},{6,2},{3,7},{7,3},{8,12},{12,8},{9,1... | collective-permute-start | bytes 3072008 | tf_op jit(solution)/shard_map/ppermute | solution.py:231
  158.7 70.8 %collective-permute-start.3 = (bf16[4,160,800]{2,1,0:T(8,128)(2,1)S(1)}, bf16[4,160,800]{2,1,0:T(8,128)(2,1)}, u32[]{:S(2)}, u32[]{:S(2)}) collective-permute-start(bf16[4,160,800]{2,1,0:T(8,128)(2,1)S(1)} %get-tuple-element.101.refs_0_), channel_id=1, source_target_pairs={{0,16},{16,0},{1,17},{17,1},{2,18},{18,2},{3,19},{19,3},{4,20},{20... | collective-permute-start | bytes 3072008 | tf_op jit(solution)/shard_map/ppermute | solution.py:231
  165.9 63.6 %copy-start.27 = (bf16[512,128]{1,0:T(8,128)(2,1)}, bf16[512,128]{1,0:T(8,128)(2,1)S(1)}, u32[]{:S(2)}) copy-start(bf16[512,128]{1,0:T(8,128)(2,1)S(1)} %pad_maximum_fusion.3.rot_ref) | copy-start | bytes 393220
  249.3 854.0 %reduce-scatter.2.cloned.1.call-start = ((), (), s32[]{:S(2)}) async-start(), calls=%async_computation.3 | async-start | bytes 11796480 | tf_op jit(solution)/shard_map/reduce_scatter | solution.py:938
  285.4 6.4 collective-permute-start.4
  285.5 53.2 %collective-permute-start.5 = (bf16[4,160,800]{2,1,0:T(8,128)(2,1)S(1)}, bf16[4,160,800]{2,1,0:T(8,128)(2,1)S(1)}, u32[]{:S(2)}, u32[]{:S(2)}) collective-permute-start(bf16[4,160,800]{2,1,0:T(8,128)(2,1)S(1)} %get-tuple-element.109.refs_0_), channel_id=1, source_target_pairs={{0,16},{16,0},{1,17},{17,1},{2,18},{18,2},{3,19},{19,3},{4,20},{20... | collective-permute-start | bytes 3072008 | tf_op jit(solution)/shard_map/ppermute | solution.py:231
  286.9 132.9 %collective-permute-start.7 = (bf16[4,160,800]{2,1,0:T(8,128)(2,1)}, bf16[4,160,800]{2,1,0:T(8,128)(2,1)}, u32[]{:S(2)}, u32[]{:S(2)}) collective-permute-start(bf16[4,160,800]{2,1,0:T(8,128)(2,1)} %collective-permute-done.3.refs_1_), channel_id=1, source_target_pairs={{0,4},{4,0},{1,5},{5,1},{2,6},{6,2},{3,7},{7,3},{8,12},{12,8},{9,1... | collective-permute-start | bytes 3072008 | tf_op jit(solution)/shard_map/ppermute | solution.py:231
  288.3 131.4 %collective-permute-start.6 = (bf16[4,160,800]{2,1,0:T(8,128)(2,1)S(1)}, bf16[4,160,800]{2,1,0:T(8,128)(2,1)}, u32[]{:S(2)}, u32[]{:S(2)}) collective-permute-start(bf16[4,160,800]{2,1,0:T(8,128)(2,1)S(1)} %get-tuple-element.101.refs_0_), channel_id=1, source_target_pairs={{0,4},{4,0},{1,5},{5,1},{2,6},{6,2},{3,7},{7,3},{8,12},{12,8},{9,1... | collective-permute-start | bytes 3072008 | tf_op jit(solution)/shard_map/ppermute | solution.py:231
  295.0 106.7 %copy-start.34 = (f32[256,2560]{1,0:T(8,128)}, f32[256,2560]{1,0:T(8,128)S(1)}, u32[]{:S(2)}) copy-start(f32[256,2560]{1,0:T(8,128)S(1)} %get-tuple-element.160) | copy-start | bytes 7864324
  295.0 106.6 %copy-start.86 = (f32[256]{0:T(256)}, f32[256]{0:T(256)S(1)}, u32[]{:S(2)}) copy-start(f32[256]{0:T(256)S(1)} %get-tuple-element.159) | copy-start | bytes 3076
  295.0 106.6 %copy-start.74 = (f32[256]{0:T(256)}, f32[256]{0:T(256)S(1)}, u32[]{:S(2)}) copy-start(f32[256]{0:T(256)S(1)} %fusion.47) | copy-start | bytes 3076
  338.7 63.0 %copy-start.12 = (bf16[4,160,800]{2,1,0:T(8,128)(2,1)}, bf16[4,160,800]{2,1,0:T(8,128)(2,1)S(1)}, u32[]{:S(2)}) copy-start(bf16[4,160,800]{2,1,0:T(8,128)(2,1)S(1)} %collective-permute-done.5.refs_1_) | copy-start | bytes 3072004
  418.3 28.2 %collective-permute-start.10 = (bf16[4,160,800]{2,1,0:T(8,128)(2,1)S(1)}, bf16[4,160,800]{2,1,0:T(8,128)(2,1)}, u32[]{:S(2)}, u32[]{:S(2)}) collective-permute-start(bf16[4,160,800]{2,1,0:T(8,128)(2,1)S(1)} %copy-done.13), channel_id=1, source_target_pairs={{0,4},{4,0},{1,5},{5,1},{2,6},{6,2},{3,7},{7,3},{8,12},{12,8},{9,1... | collective-permute-start | bytes 3072008 | tf_op jit(solution)/shard_map/ppermute | solution.py:231
  419.7 50.7 %collective-permute-start.9 = (bf16[4,160,800]{2,1,0:T(8,128)(2,1)S(1)}, bf16[4,160,800]{2,1,0:T(8,128)(2,1)}, u32[]{:S(2)}, u32[]{:S(2)}) collective-permute-start(bf16[4,160,800]{2,1,0:T(8,128)(2,1)S(1)} %get-tuple-element.109.refs_0_), channel_id=1, source_target_pairs={{0,4},{4,0},{1,5},{5,1},{2,6},{6,2},{3,7},{7,3},{8,12},{12,8},{9,1... | collective-permute-start | bytes 3072008 | tf_op jit(solution)/shard_map/ppermute | solution.py:231
  552.9 9.0 collective-permute-start.11
  557.0 52.4 %collective-permute-start.8 = (bf16[2,2,1,2,160,800]{5,4,3,1,2,0:T(8,128)(2,1)S(1)}, bf16[2,2,1,2,160,800]{5,4,3,1,2,0:T(8,128)(2,1)}, u32[]{:S(2)}, u32[]{:S(2)}) collective-permute-start(bf16[2,2,1,2,160,800]{5,4,3,1,2,0:T(8,128)(2,1)S(1)} %get-tuple-element.172), channel_id=1, source_target_pairs={{0,4},{4,0},{1,5},{5,1},{2,6},{6,2},{3,7},{7,3},{8,12},{12,8},{9,1... | collective-permute-start | bytes 6144008 | tf_op jit(solution)/shard_map/ppermute | solution.py:231
  561.9 64.3 %slice-start = ((s8[10485760]{0:T(1024)(128)(4,1)}), s8[2097152]{0:T(1024)(128)(4,1)S(1)}, s32[]{:S(2)}) async-start(s8[10485760]{0:T(1024)(128)(4,1)} %bitcast.128), calls=%async_computation.4 | async-start | bytes 4194304
  643.5 31.1 %collective-permute-start.12 = (bf16[1,1,1,256,2560]{4,3,2,1,0:T(8,128)(2,1)}, bf16[1,1,1,256,2560]{4,3,2,1,0:T(8,128)(2,1)}, u32[]{:S(2)}, u32[]{:S(2)}) collective-permute-start(bf16[1,1,1,256,2560]{4,3,2,1,0:T(8,128)(2,1)} %get-tuple-element.164), channel_id=1, source_target_pairs={{0,2},{2,0},{1,3},{3,1},{4,6},{6,4},{5,7},{7,5},{8,10},{10,8},{9,1... | collective-permute-start | bytes 3932168 | tf_op jit(solution)/shard_map/ppermute | solution.py:231
  643.5 32.0 %collective-permute-start.13 = (bf16[1,1,1,256,2560]{4,3,2,1,0:T(8,128)(2,1)}, bf16[1,1,1,256,2560]{4,3,2,1,0:T(8,128)(2,1)}, u32[]{:S(2)}, u32[]{:S(2)}) collective-permute-start(bf16[1,1,1,256,2560]{4,3,2,1,0:T(8,128)(2,1)} %get-tuple-element.166), channel_id=1, source_target_pairs={{0,8},{8,0},{1,9},{9,1},{2,10},{10,2},{3,11},{11,3},{4,12},{12,4},... | collective-permute-start | bytes 3932168 | tf_op jit(solution)/shard_map/ppermute | solution.py:231
  644.5 59.0 %collective-permute-start.14 = (bf16[1,1,1,256,2560]{4,3,2,1,0:T(8,128)(2,1)}, bf16[1,1,1,256,2560]{4,3,2,1,0:T(8,128)(2,1)}, u32[]{:S(2)}, u32[]{:S(2)}) collective-permute-start(bf16[1,1,1,256,2560]{4,3,2,1,0:T(8,128)(2,1)} %get-tuple-element.165), channel_id=1, source_target_pairs={{0,10},{2,8},{8,2},{10,0},{1,11},{3,9},{9,3},{11,1},{4,14},{6,12},... | collective-permute-start | bytes 3932168 | tf_op jit(solution)/shard_map/ppermute | solution.py:235
  715.8 53.1 %collective-permute-start.19 = (bf16[2,2,1,2,160,800]{5,4,3,1,0,2:T(8,128)(2,1)}, bf16[2,2,1,2,160,800]{5,4,3,1,0,2:T(8,128)(2,1)}, u32[]{:S(2)}, u32[]{:S(2)}) collective-permute-start(bf16[2,2,1,2,160,800]{5,4,3,1,0,2:T(8,128)(2,1)} %get-tuple-element.168), channel_id=1, source_target_pairs={{0,4},{4,0},{1,5},{5,1},{2,6},{6,2},{3,7},{7,3},{8,12},{12,8},{9,1... | collective-permute-start | bytes 6144008 | tf_op jit(solution)/shard_map/ppermute | solution.py:231
  717.2 56.1 %collective-permute-start.15 = (bf16[256,2560]{1,0:T(8,128)(2,1)}, bf16[256,2560]{1,0:T(8,128)(2,1)}, u32[]{:S(2)}, u32[]{:S(2)}) collective-permute-start(bf16[256,2560]{1,0:T(8,128)(2,1)} %get-tuple-element.157), channel_id=1, source_target_pairs={{0,1},{1,0},{2,3},{3,2},{4,5},{5,4},{6,7},{7,6},{8,9},{9,8},{10,11... | collective-permute-start | bytes 3932168 | tf_op jit(solution)/shard_map/ppermute | solution.py:231
  722.4 59.8 %collective-permute-start.17 = (bf16[1,2,1,2,160,800]{5,4,3,1,2,0:T(8,128)(2,1)}, bf16[1,2,1,2,160,800]{5,4,3,1,2,0:T(8,128)(2,1)}, u32[]{:S(2)}, u32[]{:S(2)}) collective-permute-start(bf16[1,2,1,2,160,800]{5,4,3,1,2,0:T(8,128)(2,1)} %get-tuple-element.176), channel_id=1, source_target_pairs={{0,16},{16,0},{1,17},{17,1},{2,18},{18,2},{3,19},{19,3},{4,20},{20... | collective-permute-start | bytes 3072008 | tf_op jit(solution)/shard_map/ppermute | solution.py:231
  728.7 86.8 %collective-permute-start.16 = (bf16[2,2,1,2,160,800]{5,4,3,1,2,0:T(8,128)(2,1)}, bf16[2,2,1,2,160,800]{5,4,3,1,2,0:T(8,128)(2,1)}, u32[]{:S(2)}, u32[]{:S(2)}) collective-permute-start(bf16[2,2,1,2,160,800]{5,4,3,1,2,0:T(8,128)(2,1)} %get-tuple-element.170), channel_id=1, source_target_pairs={{0,4},{4,0},{1,5},{5,1},{2,6},{6,2},{3,7},{7,3},{8,12},{12,8},{9,1... | collective-permute-start | bytes 6144008 | tf_op jit(solution)/shard_map/ppermute | solution.py:231
  819.1 50.6 %collective-permute-start.20 = (bf16[1,2,1,2,160,800]{5,4,3,1,2,0:T(8,128)(2,1)}, bf16[1,2,1,2,160,800]{5,4,3,1,2,0:T(8,128)(2,1)}, u32[]{:S(2)}, u32[]{:S(2)}) collective-permute-start(bf16[1,2,1,2,160,800]{5,4,3,1,2,0:T(8,128)(2,1)} %constant_dynamic-slice_fusion), channel_id=1, source_target_pairs={{0,16},{16,0},{1,17},{17,1},{2,18},{18,2},{3,19},{19,3},{4,20},{20... | collective-permute-start | bytes 3072008 | tf_op jit(solution)/shard_map/ppermute | solution.py:231
  846.9 25.3 %collective-permute-start.18 = (f32[256,1152]{1,0:T(8,128)S(1)}, f32[256,1152]{1,0:T(8,128)S(1)}, u32[]{:S(2)}, u32[]{:S(2)}) collective-permute-start(f32[256,1152]{1,0:T(8,128)S(1)} %constant_dynamic-slice_fusion.1), channel_id=1, source_target_pairs={{0,1},{1,0},{2,3},{3,2},{4,5},{5,4},{6,7},{7,6},{8,9},{9,8},{10,11... | collective-permute-start | bytes 3538952 | tf_op jit(solution)/shard_map/ppermute | solution.py:231
  (97 other events, 1000.8 us)
Sparse Core Ops, SparseCore 0:
  140.8 134.5 all-gather.2
  277.6 90.6 all-gather.4
  711.1 101.8 reduce-scatter.1

commit v3 on v2

--- a/solution.py
+++ b/solution.py
@@ -138,11 +138,7 @@
         compiler_params=pltpu.CompilerParams(
             dimension_semantics=("arbitrary",), vmem_limit_bytes=40 << 20
         ),
-        cost_estimate=pl.CostEstimate(
-            flops=4 * heads * group * group * TILE,
-            transcendentals=heads * group * group,
-            bytes_accessed=12 * group * cols,
-        ),
+        cost_estimate=pl.CostEstimate(flops=1, transcendentals=0, bytes_accessed=1),
     )(q, kv, rot, *turns, bias)
 
 
@@ -219,11 +215,7 @@
         compiler_params=pltpu.CompilerParams(
             dimension_semantics=("arbitrary",), vmem_limit_bytes=40 << 20
         ),
-        cost_estimate=pl.CostEstimate(
-            flops=10 * heads * group * group * TILE,
-            transcendentals=heads * group * group,
-            bytes_accessed=8 * group * cols,
-        ),
+        cost_estimate=pl.CostEstimate(flops=1, transcendentals=0, bytes_accessed=1),
     )(query, kv, d_mixed, total, rot, *turns, bias)
 
 
@@ -268,12 +260,69 @@
         ],
         out_specs=pl.BlockSpec((rank, cols), lambda i: (0, i)),
         compiler_params=pltpu.CompilerParams(vmem_limit_bytes=32 << 20),
-        cost_estimate=pl.CostEstimate(
-            flops=2 * group * rank * packs * 4 * TILE,
-            transcendentals=0,
-            bytes_accessed=2 * (group * packs * 4 * TILE + rank * packs * cols),
-        ),
+        cost_estimate=pl.CostEstimate(flops=1, transcendentals=0, bytes_accessed=1),
     )(latent, d_heads)
+
+
+def features_kernel(*refs):
+    out_ref = refs[-1]
+    total = contract(refs[0][...], refs[1][...], 1, 1)
+    for i in range(2, len(refs) - 1, 2):
+        total += contract(refs[i][...], refs[i + 1][...], 1, 1)
+    out_ref[...] = total.astype(bf16)
+
+
+def features(*pairs):
+    rows, cols = pairs[0][0].shape
+    width = pairs[0][1].shape[0]
+    tile = min(rows, 512)
+    return pl.pallas_call(
+        features_kernel,
+        grid=(rows // tile,),
+        out_shape=jax.ShapeDtypeStruct((rows, width), bf16),
+        in_specs=[
+            pl.BlockSpec((tile, cols), lambda i: (i, 0)),
+            pl.BlockSpec((width, cols), lambda i: (0, 0)),
+        ]
+        * len(pairs),
+        out_specs=pl.BlockSpec((tile, width), lambda i: (i, 0)),
+        compiler_params=pltpu.CompilerParams(vmem_limit_bytes=56 << 20),
+        cost_estimate=pl.CostEstimate(flops=1, transcendentals=0, bytes_accessed=1),
+    )(*(array for pair in pairs for array in pair))
+
+
+def grad_kernel(axis, left_ref, right_ref, keep_ref, send_ref, total):
+    half = total.shape[1]
+    value = contract(left_ref[...], right_ref[...], 0, 0).astype(bf16)
+    total[0] = value[:half]
+    total[1] = value[half:]
+    at = lax.axis_index(axis)
+    keep_ref[0] = total[at]
+    send_ref[0] = total[1 - at]
+
+
+def grad_halves(left, right, rows, axis):
+    tokens, width = left.shape
+    cols = right.shape[1]
+    tile = 4 * rows
+    if tile % TILE:
+        held = rows_first(contract(left, right, 0, 0).astype(bf16)).reshape(-1, 2, 2 * rows, cols)
+        at = lax.axis_index(axis)
+        return tuple(pick(held, i, 1)[:, 0] for i in (at, 1 - at))
+    out = jax.ShapeDtypeStruct((width // tile, 2 * rows, cols), bf16)
+    return pl.pallas_call(
+        functools.partial(grad_kernel, axis),
+        grid=(width // tile,),
+        out_shape=(out, out),
+        in_specs=[
+            pl.BlockSpec((tokens, tile), lambda i: (0, i)),
+            pl.BlockSpec((tokens, cols), lambda i: (0, 0)),
+        ],
+        out_specs=(pl.BlockSpec((1, 2 * rows, cols), lambda i: (i, 0, 0)),) * 2,
+        scratch_shapes=[pltpu.VMEM((2, 2 * rows, cols), bf16)],
+        compiler_params=pltpu.CompilerParams(vmem_limit_bytes=56 << 20),
+        cost_estimate=pl.CostEstimate(flops=1, transcendentals=0, bytes_accessed=1),
+    )(left, right)
 
 
 def rows_first(value):
@@ -349,7 +398,10 @@
     q_out,
     kv_out,
     gate_out,
-    others_out,
+    gate_over,
+    gate_last,
+    up_out,
+    down_out,
     staged,
     send_sems,
     recv_sems,
@@ -396,7 +448,7 @@
         for copy in copies:
             copy.wait_recv()
 
-    targets = (gate_out.at[0], others_out.at[0], others_out.at[1])
+    targets = (gate_out, up_out, down_out)
 
     def send_columns(away, axes):
         return [
@@ -431,7 +483,10 @@
     core_sent = [sender.start(ref.at[mine], ref.at[mine], ("c",)) for ref, _ in early]
     for copies in columns:
         copies[0].wait_recv()
-    gate_over = [sender.start(gate_out.at[0], gate_out.at[1], (spread[0],))]
+    over = [
+        sender.start(gate_out, gate_over, (spread[0],)),
+        sender.start(gate_out, gate_last, (spread[1],)),
+    ]
     for stage in range(1, len(squares)):
         if stage > 1:
             sent_later = [send_square(*item, stage) for item in later]
@@ -441,7 +496,7 @@
     wait(core_sent)
     for copies in columns:
         wait(copies[1:])
-    wait(gate_over)
+    wait(over)
     sender.finish()
 
 
@@ -449,7 +504,7 @@
     vmem = pl.BlockSpec(memory_space=pltpu.VMEM)
     rows, cols = gate.shape
     lead = (4,) * len(squares)
-    copies = 12 + 16 * (len(squares) - 1) + 2 + 9 + 1
+    copies = 12 + 16 * (len(squares) - 1) + 2 + 9 + 2
     return pl.pallas_call(
         functools.partial(first_kernel, squares, pair, spread),
         out_shape=(
@@ -457,11 +512,10 @@
             jax.ShapeDtypeStruct(lead + (2,) + gains.shape, bf16),
             jax.ShapeDtypeStruct(lead + q_up.shape, bf16),
             jax.ShapeDtypeStruct(lead + kv_up.shape, bf16),
-            jax.ShapeDtypeStruct((2, 4, rows, cols // 4), bf16),
-            jax.ShapeDtypeStruct((2, 4, rows, cols // 4), bf16),
-        ),
+        )
+        + (jax.ShapeDtypeStruct((4, rows, cols // 4), bf16),) * 5,
         in_specs=[vmem] * 7,
-        out_specs=(vmem,) * 6,
+        out_specs=(vmem,) * 9,
         scratch_shapes=[
             pltpu.VMEM((3, 4, rows, cols // 4), bf16),
             pltpu.SemaphoreType.DMA((copies,)),
@@ -546,7 +600,7 @@
     sender.finish()
 
 
-def tokens_of_chips(value, pair):
+def tokens_of_chips(value, pair, number):
     rows, cols = value.shape
     vmem = pl.BlockSpec(memory_space=pltpu.VMEM)
     out = pl.pallas_call(
@@ -556,8 +610,9 @@
         out_specs=vmem,
         scratch_shapes=[pltpu.SemaphoreType.DMA((8,)), pltpu.SemaphoreType.DMA((8,))],
         compiler_params=pltpu.CompilerParams(
-            collective_id=1, has_side_effects=True, vmem_limit_bytes=24 << 20
-        ),
+            collective_id=number, has_side_effects=True, vmem_limit_bytes=24 << 20
+        ),
+        cost_estimate=pl.CostEstimate(flops=1, transcendentals=0, bytes_accessed=1),
     )(value)
     return out.reshape(8 * rows, cols)
 
@@ -655,11 +710,12 @@
     small = Reduction(sender, small_ref, with_core, ["c"] + turned, buffers(stages + 1), small_sum)
     gains = Reduction(sender, gains_ref, with_core, ["c"] + down, buffers(stages + 1), gains_sum)
     q = Reduction(sender, q_ref, fsdp, down, buffers(stages), q_sum)
-    kv = Reduction(sender, kv_ref, fsdp, down, buffers(stages), kv_sum)
+    kv = Reduction(sender, kv_ref, fsdp, turned, buffers(stages), kv_sum)
+    upward = [down[-2]] + turned[:-2] + [down[-1]]
     outs = []
-    for rows in halves_of(out_sum.shape[0]):
+    for rows, order in zip(halves_of(out_sum.shape[0]), (turned, upward)):
         part = out_ref.at[(slice(None),) * stages + (rows,)]
-        outs.append(Reduction(sender, part, fsdp, turned, buffers(stages), out_sum.at[rows]))
+        outs.append(Reduction(sender, part, fsdp, order, buffers(stages), out_sum.at[rows]))
     over = buffers(1)[0]
     peaks = buffers(stages)
     me = place_of(*pair)
@@ -798,7 +854,7 @@
     q_up_wide = jnp.pad(
         q_up.reshape(-1, heads, NOPE + ROPE), ((0, 0), (0, 0), (0, TILE - NOPE - ROPE))
     ).reshape(-1, heads * TILE)
-    small_all, gains_all, q_up_all, kv_up_all, gate_held, others_held = first_gather(
+    small_all, gains_all, q_up_all, kv_up_all, *pieces = first_gather(
         squares, pair, spread, small, gains, q_up_wide, kv_up, gate_proj, up_proj, down_proj
     )
     down_full = small_all.reshape(-1, small_cols)
@@ -862,33 +918,36 @@
     allowed = (seq_row[None, :] == seq_row[:, None]) & (block_row[:, None] <= block_row[None, :])
     bias = jnp.where(allowed, 0.0, -1e30).astype(f32)
     axes = list(spread)
-    gate_pieces = [gate_held[0], gate_held[1]]
-    up_pieces = [others_held[0]]
-    down_pieces = [others_held[1]]
-    up_pieces += over(up_pieces, axes[0])
-    for axis in axes[1:]:
+    gate_held, gate_over, gate_last, up_held, down_held = pieces
+    gate_pieces = [gate_held, gate_over, gate_last, swap(gate_over, axes[1])]
+    for axis in axes[2:]:
         gate_pieces += over(gate_pieces, axis)
-    q_full, *early = lax.optimization_barrier((q_full, *gate_pieces, *up_pieces))
-    gate_pieces, up_pieces = early[: len(gate_pieces)], early[len(gate_pieces) :]
+    other_pieces = []
+    for piece in (up_held, down_held):
+        other_pieces += [swap(piece, axes[0]), swap(piece, axes[1])]
     attn, queries, log_total, local_peak = attend(
         q_full, kv_full, key_rot_all, tables(all_cos, all_sin), bias, score_scale
     )
-    down_pieces += over(down_pieces, axes[0], q_full)
-    for axis in axes[1:]:
-        up_pieces += over(up_pieces, axis)
+    attn, *early = lax.optimization_barrier((attn, *other_pieces, *gate_pieces))
+    other_pieces, gate_pieces = early[:4], early[4:]
     d_ffn = (resid_scale * cot_float).astype(bf16)
     d_ffn_all = lax.all_gather(after(d_ffn, attn), (wide, near, "c"), axis=0, tiled=True)
     branch = core_sum(contract(attn, out_full, 1, 1))
     mid = x_float + resid_scale * branch
     mid_normed = rms_scale(mid, post_float).astype(bf16)
-    gate_full = lay([after(piece, attn) for piece in gate_pieces], fsdp, pair, spread)
-    mid_all = tokens_of_chips(after(mid_normed, gate_full, *down_pieces), pair)
-    for axis in axes[1:]:
-        down_pieces += over(down_pieces, axis, mid_all)
+    gate_full = lay(gate_pieces, fsdp, pair, spread)
+    mid_all = tokens_of_chips(after(mid_normed, gate_full), pair, 1)
+    up_pieces = [up_held, *other_pieces[:2], swap(after(other_pieces[0], attn), axes[1])]
+    down_pieces = [down_held, *other_pieces[2:], swap(after(other_pieces[2], attn), axes[1])]
+    for axis in axes[2:]:
+        up_pieces += over(up_pieces, axis)
+        down_pieces += over(down_pieces, axis)
+    mid_all, *late = lax.optimization_barrier((mid_all, *up_pieces, *down_pieces))
+    up_pieces, down_pieces = late[: len(up_pieces)], late[len(up_pieces) :]
+    up_full = lay(up_pieces, fsdp, pair, spread)
     gate = jnp.dot(mid_all, gate_full, preferred_element_type=f32)
-    up_full = lay([after(piece, gate) for piece in up_pieces], fsdp, pair, spread)
     up_value = jnp.dot(mid_all, up_full, preferred_element_type=f32)
-    down_proj_full = lay([after(piece, up_value) for piece in down_pieces], fsdp, pair, spread)
+    down_proj_full = lay(down_pieces, fsdp, pair, spread)
     sigmoid = jax.nn.sigmoid(gate)
     silu_value = gate * sigmoid
     act = (silu_value * up_value).astype(bf16)
@@ -898,7 +957,6 @@
     d_up = (d_act * silu_value).astype(bf16)
     dims = list(fsdp)
     first, last = spread[0], spread[-1]
-    held_shape = [2] * len(fsdp) + [width // count, -1]
 
     def added(parts):
         return (parts[0].astype(f32) + parts[1].astype(f32)).astype(bf16)
@@ -910,31 +968,34 @@
             left.remove(axis)
         return held
 
-    def begin(grad):
-        return exchange(grad.reshape(held_shape), dims, last)
+    def begin(left, right, *ready):
+        keep, send = grad_halves(left, right, width // count, last)
+        shape = [2] * (len(fsdp) - 1) + [width // count, -1]
+        return swap(after(send, *ready), last).reshape(shape), keep.reshape(shape), keep
 
     def cross(held):
         return exchange(held, [first, *pair], first)
 
-    down_grad = rows_first(contract(d_ffn_all, act, 0, 0).astype(bf16))
-    down_parts = begin(down_grad)
-    d_gate_late, d_up_late, _ = lax.optimization_barrier((d_gate, d_up, down_grad))
-    d_mid_part = (
-        contract(d_gate_late, gate_full, 1, 1) + contract(d_up_late, up_full, 1, 1)
-    ).astype(bf16)
+    *down_parts, down_grad = begin(d_ffn_all, act)
+    d_gate_late, _ = lax.optimization_barrier((d_gate, down_grad))
+    gate_keep, gate_send = grad_halves(mid_all, d_gate_late, width // count, last)
+    d_up_late, d_gate_late, _ = lax.optimization_barrier((d_up, d_gate, gate_keep))
+    d_mid_part = features((d_gate_late, gate_full), (d_up_late, up_full))
+    d_mid_part, *down_parts = lax.optimization_barrier((d_mid_part, *down_parts))
     d_mid_held = sum_of_cores(d_mid_part)
     d_mid_normed = sum_of_chips(d_mid_held)
-    mid_late, down_got, down_kept, _ = lax.optimization_barrier(
-        (mid_all, *down_parts, d_mid_held)
-    )
-    gate_grad = rows_first(contract(mid_late, d_gate, 0, 0).astype(bf16))
-    gate_parts = begin(gate_grad)
-    down_parts = cross(inner(added((down_got, down_kept))))
-    up_grad = rows_first(contract(after(mid_late, gate_grad), d_up, 0, 0).astype(bf16))
-    up_parts = begin(up_grad)
-    ffn_part = contract(after(act, up_grad), down_proj_full, 1, 1).astype(bf16)
+    mid_late, gate_send, _ = lax.optimization_barrier((mid_all, gate_send, d_mid_held))
+    shape = [2] * (len(fsdp) - 1) + [width // count, -1]
+    gate_parts = (swap(gate_send, last).reshape(shape), gate_keep.reshape(shape))
+    down_parts = cross(inner(added(down_parts)))
+    *up_parts, up_grad = begin(mid_late, d_up, gate_parts[0])
+    ffn_part = features((after(act, up_grad), down_proj_full))
     post_pull = jax.vjp(rms_scale, mid, post_float)[1]
-    d_mid_norm, post_grad = post_pull(after(d_mid_normed, up_grad, ffn_part))
+    d_mid_normed, *early = lax.optimization_barrier(
+        (d_mid_normed, *down_parts, *gate_parts, ffn_part)
+    )
+    down_parts, gate_parts, ffn_part = early[:2], early[2:4], early[4]
+    d_mid_norm, post_grad = post_pull(d_mid_normed)
     ffn = lax.psum_scatter(
         after(ffn_part, d_mid_norm), (wide, near, "c"), scatter_dimension=0, tiled=True
     )
@@ -943,23 +1004,23 @@
     d_branch = (resid_scale * d_mid).astype(bf16)
     d_branch_all = core_both(d_branch)
     d_attn = jnp.dot(d_branch_all, out_full, preferred_element_type=f32).astype(bf16)
-    d_attn_late, gate_got, gate_kept, *down_parts = lax.optimization_barrier(
-        (d_attn, *gate_parts, *down_parts)
-    )
-    gate_parts = cross(inner(added((gate_got, gate_kept))))
+    gate_parts = cross(inner(added(gate_parts)))
     d_q, d_kv, d_rot_part = attend_back(
         queries,
         kv_full,
-        d_attn_late,
+        d_attn,
         log_total,
         key_rot_all,
         tables(all_cos, -all_sin),
         bias,
         score_scale,
     )
+    q_up_grad = heads_grad(q_lat_all, d_q)
+    d_q, d_kv, q_up_grad, *early = lax.optimization_barrier(
+        (d_q, d_kv, q_up_grad, *gate_parts, *up_parts)
+    )
+    gate_parts, up_parts = early[:2], early[2:]
     out_grad = rows_first(contract(after(d_branch_all, d_q), attn, 0, 0).astype(bf16))
-    q_lat_late, *up_parts = lax.optimization_barrier((q_lat_all, *up_parts))
-    q_up_grad = heads_grad(q_lat_late, d_q)
     kv_up_grad = rows_first(contract(kv_lat_all, d_kv, 0, 0).astype(bf16))
     d_q_lat_part = contract(d_q, q_up_full, 1, 1)
     d_kv_lat_part = contract(d_kv, kv_up_full, 1, 1)

time: 1130 us -> 957 us (0.85)
  waiting for transfers between devices: 323 us -> 193 us
  matrix products: 192 us -> 92.8 us
  Pallas kernels: 438 us -> 518 us
    ppermute x20 -> x19, waiting for transfers between devices: 269 us -> 122 us  [swap(): return lax.ppermute(value, axis, SWAP)]
    dot_general x13 -> x7, matrix products: 128 us -> 27.6 us  [contract(): lax.dot_general(left, right, (((left_dim,), (right_dim,)), ((), ())), pre...]
    pallas_call x0 -> x5, Pallas kernels: none -> 92.9 us  [the longest x3 48.9 us: grad_halves(): pl.pallas_call(functools.partial(grad_kernel, axis), grid=(width // tile,...]
    pallas_call x1, Pallas kernels: 193 us -> 166 us  [last_scatter(): pl.pallas_call(functools.partial(last_kernel, fsdp, pair), out_shape=tupl...]
    all_gather x1, waiting for transfers between devices: 26.1 us -> 43 us  [shards(): lax.all_gather(after(out_proj, gains_all), chips, axis=0, tiled=True)]
    pallas_call x1, Pallas kernels: 62.9 us -> 77.7 us  [tokens_of_chips(): pl.pallas_call(functools.partial(tokens_kernel, pair), out_shape=jax.Shap...]
    unnamed x218 -> x181, local copies, waits for them, and re-layouts: 41.2 us -> 35.6 us
  transfers between devices with their start and end apart: 24 -> 23, of which waited for: 16 -> 8; matrix products, arithmetic and copies ran while one was open for 15% -> 11% of each run, Pallas kernels for 28% -> 40%
where the time goes in v3:
time: 957 us; the launch traced here: 948 us
  Pallas kernels  518 us (54%)
  waiting for transfers between devices  193 us (20%)
  matrix products  92.8 us (10%)
  local copies, waits for them, and re-layouts  56.1 us (6%)
  other arithmetic  54.2 us (6%)
  starting transfers between devices  16.7 us (2%)
  between operations  16.2 us (2%)
    pallas_call x1, Pallas kernels, last_scatter(): pl.pallas_call(functools.partial(last_kernel, fsdp, pair), out_shape=tupl...  166 us
    pallas_call x1, Pallas kernels, first_gather(): pl.pallas_call(functools.partial(first_kernel, squares, pair, spread), ou...  125 us
    ppermute x19, waiting for transfers between devices, swap(): return lax.ppermute(value, axis, SWAP)  122 us
    pallas_call x1, Pallas kernels, tokens_of_chips(): pl.pallas_call(functools.partial(tokens_kernel, pair), out_shape=jax.Shap...  77.7 us
    pallas_call x3, Pallas kernels, grad_halves(): pl.pallas_call(functools.partial(grad_kernel, axis), grid=(width // tile,...  48.9 us
    pallas_call x2, Pallas kernels, features(): pl.pallas_call(features_kernel, grid=(rows // tile,), out_shape=jax.Shape...  44 us
    all_gather x1, waiting for transfers between devices, shards(): lax.all_gather(after(out_proj, gains_all), chips, axis=0, tiled=True)  43 us
    unnamed x181, local copies, waits for them, and re-layouts  35.6 us
  transfers between devices with their start and end apart: 23, of which 8 were waited for; matrix products, arithmetic and copies ran while one was open for 11% of the time, Pallas kernels for 40%

profile of v3, /device:TPU:0, one launch (start us, length us, event | category | flops | bytes accessed | tf_op | source)
XLA Modules:
  0.0 947.8 jit_solution(2104187904819914788)
XLA Ops:
  14.4 125.2 %shard_map.304 = (bf16[4,4,2,80,1056]{4,3,2,1,0:T(8,128)(2,1)}, bf16[4,4,2,8,128]{4,3,2,1,0:T(8,128)(2,1)S(1)}, bf16[4,4,48,2560]{3,2,1,0:T(8,128)(2,1)}, bf16[4...) custom-call(bf16[80,1056]{1,0:T(8,128)(2,1)S(1)} %pad_maximum_fusion, ...), custom_call_target="tpu_custom_call" | custom-call | tf_op jit(solution)/shard_map/pallas_call | solution.py:508
  149.6 5.1 fusion.14
  170.5 16.8 %shard_map.305 = (bf16[512,1280]{1,0:T(8,128)(2,1)S(1)}, bf16[512,2560]{1,0:T(8,128)(2,1)S(1)}, f32[10,2,512]{2,1,0:T(2,128)S(1)}, f32[8,128]{1,0:T(8,128)S(1)}) custom-call(f32[512,2560]{1,0:T(8,128)S(1)} %fusion.51.q_ref, bf16[512,2560]{1,0:T(8,128)(2,1)S(1)} %convolution_convert_fusion.2.kv_ref, bf16[512,128]{1,0:T(8,128)(2,1)S(1)} %pad_maximum_fusion.3.rot_ref, ...), custom_call_target="tpu_custom_call" | custom-call | flops 1 | bytes 1 | tf_op jit(solution)/shard_map/pallas_call | solution.py:122
  190.5 52.5 %collective-permute-done.1.refs_1_ = bf16[4,160,800]{2,1,0:T(8,128)(2,1)S(1)} collective-permute-done((bf16[4,160,800]{2,1,0:T(8,128)(2,1)}, bf16[4,160,800]{2,1,0:T(8,128)(2,1)S(1)}, u32[]{:S(2)}, u32[]{:S(2)}) %collective-permute-start.1) | collective-permute-done | bytes 1024032 | tf_op jit(solution)/shard_map/ppermute | solution.py:223
  243.0 23.6 %collective-permute-done.3.refs_1_ = bf16[4,160,800]{2,1,0:T(8,128)(2,1)} collective-permute-done((bf16[4,160,800]{2,1,0:T(8,128)(2,1)}, bf16[4,160,800]{2,1,0:T(8,128)(2,1)}, u32[]{:S(2)}, u32[]{:S(2)}) %collective-permute-start.3) | collective-permute-done | bytes 1024032 | tf_op jit(solution)/shard_map/ppermute | solution.py:223
  268.0 43.0 %all-gather.3.cloned.1.call-done = bf16[2560,1280]{1,0:T(8,128)(2,1)} async-done(((bf16[160,1280]{1,0:T(8,128)(2,1)}), bf16[2560,1280]{1,0:T(8,128)(2,1)}) %all-gather.3.cloned.1.call-update) | async-done | bytes 6553616 | tf_op jit(solution)/shard_map/all_gather | solution.py:873
  311.0 6.1 fusion.52
  335.1 77.7 %shard_map.307 = bf16[4,2,256,2560]{3,2,1,0:T(8,128)(2,1)S(1)} custom-call(bf16[256,2560]{1,0:T(8,128)(2,1)S(1)} %multiply_convert_fusion.4.value_ref), custom_call_target="tpu_custom_call" | custom-call | flops 1 | bytes 1 | tf_op jit(solution)/shard_map/pallas_call | solution.py:606
  422.5 12.9 %fusion.54 = f32[2048,800]{1,0:T(8,128)} fusion(bf16[2048,2560]{1,0:T(8,128)(2,1)S(1)} %bitcast.96, bf16[2560,800]{1,0:T(8,128)(2,1)S(1)} %bitcast.100), kind=kOutput, calls=%fused_computation.167 | convolution fusion | flops 8388608000 | bytes 21135360 | tf_op jit(solution)/shard_map/dot_general | solution.py:948
  435.4 16.3 %fusion.53 = f32[2048,800]{1,0:T(8,128)} fusion(bf16[2048,2560]{1,0:T(8,128)(2,1)} %all-gather.5.cloned.1.call-done.left_ref, bf16[2560,800]{1,0:T(8,128)(2,1)} %bitcast.104), kind=kOutput, calls=%fused_computation.166 | convolution fusion | flops 8388608000 | bytes 21135360 | tf_op jit(solution)/shard_map/dot_general | solution.py:955
  451.7 21.2 %multiply_convert_fusion = (bf16[2048,800]{1,0:T(8,128)(2,1)}, bf16[2048,800]{1,0:T(8,128)(2,1)}, bf16[2048,800]{1,0:T(8,128)(2,1)}) fusion(f32[2048,800]{1,0:T(8,128)} %fusion.54, f32[2048,800]{1,0:T(8,128)} %fusion.53, bf16[2048,2560]{1,0:T(8,128)(2,1)} %bitcast.97, bf16[2560,800]{1,0:T(8,128)(2,1)S(1)} %bitcast.103), kind=kOutput, calls=%fused_computation.3 | convolution fusion | flops 8413184000 | bytes 37519360 | tf_op jit(solution)/shard_map/dot_general | solution.py:949
  472.9 16.5 %shard_map.310 = (bf16[4,320,800]{2,1,0:T(8,128)(2,1)}, bf16[4,320,800]{2,1,0:T(8,128)(2,1)}) custom-call(bf16[2048,2560]{1,0:T(8,128)(2,1)} %all-gather.5.cloned.1.call-done.left_ref, bf16[2048,800]{1,0:T(8,128)(2,1)} %get-tuple-element.141.right_ref.refs_0_), custom_call_target="tpu_custom_call" | custom-call | flops 1 | bytes 1 | tf_op jit(solution)/shard_map/pallas_call | solution.py:313
  490.4 16.1 %shard_map.311 = (bf16[4,320,800]{2,1,0:T(8,128)(2,1)}, bf16[4,320,800]{2,1,0:T(8,128)(2,1)}) custom-call(bf16[2048,2560]{1,0:T(8,128)(2,1)} %bitcast.98, bf16[2048,800]{1,0:T(8,128)(2,1)} %get-tuple-element.131.right_ref.refs_0_), custom_call_target="tpu_custom_call" | custom-call | flops 1 | bytes 1 | tf_op jit(solution)/shard_map/pallas_call | solution.py:313
  506.4 28.2 %shard_map.312 = bf16[2048,2560]{1,0:T(8,128)(2,1)} custom-call(bf16[2048,800]{1,0:T(8,128)(2,1)} %get-tuple-element.131.right_ref.refs_0_, bf16[2560,800]{1,0:T(8,128)(2,1)} %bitcast.101, bf16[2048,800]{1,0:T(8,128)(2,1)} %get-tuple-element.132.refs_2_.right_ref, bf16[2560,800]{1,0:T(8,128)(2,1)} %bitcast.102), custom_call_target="tpu_custom_call" | custom-call | flops 1 | bytes 1 | tf_op jit(solution)/shard_map/pallas_call | solution.py:279
  534.7 7.2 collective-permute-done.9
  541.9 5.1 constant_dynamic-slice_fusion.8
  547.0 9.0 collective-permute-done.10
  556.0 5.5 add_convert_fusion
  575.3 16.3 %shard_map.313 = (bf16[4,320,800]{2,1,0:T(8,128)(2,1)}, bf16[4,320,800]{2,1,0:T(8,128)(2,1)}) custom-call(bf16[2048,2560]{1,0:T(8,128)(2,1)} %bitcast.99, bf16[2048,800]{1,0:T(8,128)(2,1)} %get-tuple-element.132.refs_2_.right_ref), custom_call_target="tpu_custom_call" | custom-call | flops 1 | bytes 1 | tf_op jit(solution)/shard_map/pallas_call | solution.py:313
  591.6 15.7 %shard_map.314 = bf16[2048,2560]{1,0:T(8,128)(2,1)} custom-call(bf16[2048,800]{1,0:T(8,128)(2,1)} %get-tuple-element.141.right_ref.refs_0_, bf16[2560,800]{1,0:T(8,128)(2,1)} %bitcast.105), custom_call_target="tpu_custom_call" | custom-call | flops 1 | bytes 1 | tf_op jit(solution)/shard_map/pallas_call | solution.py:279
  607.3 14.8 %collective-permute-done.12 = bf16[1,1,1,256,2560]{4,3,2,1,0:T(8,128)(2,1)} collective-permute-done((bf16[1,1,1,256,2560]{4,3,2,1,0:T(8,128)(2,1)}, bf16[1,1,1,256,2560]{4,3,2,1,0:T(8,128)(2,1)}, u32[]{:S(2)}, u32[]{:S(2)}) %collective-permute-start.12) | collective-permute-done | bytes 1310752 | tf_op jit(solution)/shard_map/ppermute | solution.py:223
  622.1 27.9 %collective-permute-done.13 = bf16[1,1,1,256,2560]{4,3,2,1,0:T(8,128)(2,1)} collective-permute-done((bf16[1,1,1,256,2560]{4,3,2,1,0:T(8,128)(2,1)}, bf16[1,1,1,256,2560]{4,3,2,1,0:T(8,128)(2,1)}, u32[]{:S(2)}, u32[]{:S(2)}) %collective-permute-start.13) | collective-permute-done | bytes 1310752 | tf_op jit(solution)/shard_map/ppermute | solution.py:227
  667.3 6.7 convolution_convert_fusion.4.d_mixed_ref
  674.0 21.1 %shard_map.315 = (bf16[512,2560]{1,0:T(8,128)(2,1)S(1)}, bf16[512,2560]{1,0:T(8,128)(2,1)S(1)}, f32[512,128]{1,0:T(8,128)S(1)}) custom-call(bf16[512,2560]{1,0:T(8,128)(2,1)S(1)} %copy-done.11, bf16[512,2560]{1,0:T(8,128)(2,1)S(1)} %copy-done.2, bf16[512,1280]{1,0:T(8,128)(2,1)S(1)} %convolution_convert_fusion.4.d_mixed_ref, ...), custom_call_target="tpu_custom_call" | custom-call | flops 1 | bytes 1 | tf_op jit(solution)/shard_map/pallas_call | solution.py:195
  695.1 3.9 shard_map.316
  700.7 15.1 %collective-permute-done.17 = bf16[1,2,2,160,800]{4,3,2,1,0:T(8,128)(2,1)} collective-permute-done((bf16[1,2,2,160,800]{4,3,2,1,0:T(8,128)(2,1)}, bf16[1,2,2,160,800]{4,3,2,1,0:T(8,128)(2,1)}, u32[]{:S(2)}, u32[]{:S(2)}) %collective-permute-start.17) | collective-permute-done | bytes 1024032 | tf_op jit(solution)/shard_map/ppermute | solution.py:223
  724.9 3.7 add_convert_fusion.1
  728.6 5.6 convolution_convert_fusion
  737.5 6.3 fusion.4
  744.8 4.6 convolution_convert_fusion.1
  749.4 166.0 %shard_map.317 = (f32[80,1056]{1,0:T(8,128)}, f32[8,128]{1,0:T(8,128)}, f32[48,1920]{1,0:T(8,128)}, f32[16,2560]{1,0:T(8,128)}, f32[160,1280]{1,0:T(8,128)}, /*i...) custom-call(f32[8,128]{1,0:T(8,128)} %copy-done.28, bf16[2,2,2,2,2,80,1056]{6,5,4,3,2,1,0:T(8,128)(2,1)} %bitcast.113, ...), custom_call_target="tpu_custom_call" | custom-call | tf_op jit(solution)/shard_map/pallas_call | solution.py:788
  929.8 5.8 fusion.6
  (338 shorter events, 129.9 us)
Async XLA Ops:
  7.2 303.8 %all-gather.3.cloned.1.call-start = ((), (), s32[]{:S(2)}) async-start(), calls=%async_computation.1 | async-start | bytes 6963200 | tf_op jit(solution)/shard_map/all_gather | solution.py:873
  8.7 138.9 %copy-start.66 = (s32[1,512]{1,0:T(1,128)S(1)}, s32[1,512]{1,0:T(1,128)}, u32[]{:S(2)}) copy-start(s32[1,512]{1,0:T(1,128)} %param.18) | copy-start | bytes 6148
  141.7 293.7 %all-gather.5.cloned.1.call-start = ((), (), s32[]{:S(2)}) async-start(), calls=%async_computation.2 | async-start | bytes 11796480 | tf_op jit(solution)/shard_map/all_gather | solution.py:934
  141.7 101.3 %collective-permute-start.1 = (bf16[4,160,800]{2,1,0:T(8,128)(2,1)}, bf16[4,160,800]{2,1,0:T(8,128)(2,1)S(1)}, u32[]{:S(2)}, u32[]{:S(2)}) collective-permute-start(bf16[4,160,800]{2,1,0:T(8,128)(2,1)} %get-tuple-element.124.refs_0_), channel_id=1, source_target_pairs={{0,16},{16,0},{1,17},{17,1},{2,18},{18,2},{3,19},{19,3},{4,20},{20... | collective-permute-start | bytes 3072008 | tf_op jit(solution)/shard_map/ppermute | solution.py:223
  143.1 99.9 %collective-permute-start.2 = (bf16[4,160,800]{2,1,0:T(8,128)(2,1)}, bf16[4,160,800]{2,1,0:T(8,128)(2,1)}, u32[]{:S(2)}, u32[]{:S(2)}) collective-permute-start(bf16[4,160,800]{2,1,0:T(8,128)(2,1)} %get-tuple-element.124.refs_0_), channel_id=1, source_target_pairs={{0,4},{4,0},{1,5},{5,1},{2,6},{6,2},{3,7},{7,3},{8,12},{12,8},{9,1... | collective-permute-start | bytes 3072008 | tf_op jit(solution)/shard_map/ppermute | solution.py:223
  143.6 123.0 %collective-permute-start.3 = (bf16[4,160,800]{2,1,0:T(8,128)(2,1)}, bf16[4,160,800]{2,1,0:T(8,128)(2,1)}, u32[]{:S(2)}, u32[]{:S(2)}) collective-permute-start(bf16[4,160,800]{2,1,0:T(8,128)(2,1)} %get-tuple-element.119.refs_0_), channel_id=1, source_target_pairs={{0,16},{16,0},{1,17},{17,1},{2,18},{18,2},{3,19},{19,3},{4,20},{20... | collective-permute-start | bytes 3072008 | tf_op jit(solution)/shard_map/ppermute | solution.py:223
  146.2 120.4 %collective-permute-start.4 = (bf16[4,160,800]{2,1,0:T(8,128)(2,1)}, bf16[4,160,800]{2,1,0:T(8,128)(2,1)}, u32[]{:S(2)}, u32[]{:S(2)}) collective-permute-start(bf16[4,160,800]{2,1,0:T(8,128)(2,1)} %get-tuple-element.119.refs_0_), channel_id=1, source_target_pairs={{0,4},{4,0},{1,5},{5,1},{2,6},{6,2},{3,7},{7,3},{8,12},{12,8},{9,1... | collective-permute-start | bytes 3072008 | tf_op jit(solution)/shard_map/ppermute | solution.py:223
  157.9 3.6 collective-permute-start
  161.4 105.2 %collective-permute-start.5 = (bf16[4,160,800]{2,1,0:T(8,128)(2,1)}, bf16[4,160,800]{2,1,0:T(8,128)(2,1)S(1)}, u32[]{:S(2)}, u32[]{:S(2)}) collective-permute-start(bf16[4,160,800]{2,1,0:T(8,128)(2,1)} %copy-done.18), channel_id=1, source_target_pairs={{0,4},{4,0},{1,5},{5,1},{2,6},{6,2},{3,7},{7,3},{8,12},{12,8},{9,1... | collective-permute-start | bytes 3072008 | tf_op jit(solution)/shard_map/ppermute | solution.py:223
  267.7 668.0 %reduce-scatter.2.cloned.1.call-start = ((), (), s32[]{:S(2)}) async-start(), calls=%async_computation.3 | async-start | bytes 11796480 | tf_op jit(solution)/shard_map/reduce_scatter | solution.py:999
  320.6 8.1 collective-permute-start.6
  320.6 92.2 %collective-permute-start.8 = (bf16[4,160,800]{2,1,0:T(8,128)(2,1)}, bf16[4,160,800]{2,1,0:T(8,128)(2,1)S(1)}, u32[]{:S(2)}, u32[]{:S(2)}) collective-permute-start(bf16[4,160,800]{2,1,0:T(8,128)(2,1)} %collective-permute-done.3.refs_1_), channel_id=1, source_target_pairs={{0,4},{4,0},{1,5},{5,1},{2,6},{6,2},{3,7},{7,3},{8,12},{12,8},{9,1... | collective-permute-start | bytes 3072008 | tf_op jit(solution)/shard_map/ppermute | solution.py:223
  322.1 90.7 %collective-permute-start.7 = (bf16[4,160,800]{2,1,0:T(8,128)(2,1)S(1)}, bf16[4,160,800]{2,1,0:T(8,128)(2,1)S(1)}, u32[]{:S(2)}, u32[]{:S(2)}) collective-permute-start(bf16[4,160,800]{2,1,0:T(8,128)(2,1)S(1)} %collective-permute-done.1.refs_1_), channel_id=1, source_target_pairs={{0,4},{4,0},{1,5},{5,1},{2,6},{6,2},{3,7},{7,3},{8,12},{12,8},{9,1... | collective-permute-start | bytes 3072008 | tf_op jit(solution)/shard_map/ppermute | solution.py:223
  328.7 91.7 %copy-start.3 = (bf16[16,160,800]{2,1,0:T(8,128)(2,1)}, bf16[16,160,800]{2,1,0:T(8,128)(2,1)S(1)}, u32[]{:S(2)}) copy-start(bf16[16,160,800]{2,1,0:T(8,128)(2,1)S(1)} %shard_map.306) | copy-start | bytes 12288004
  334.8 78.0 %copy-start.31 = (f32[256,2560]{1,0:T(8,128)}, f32[256,2560]{1,0:T(8,128)S(1)}, u32[]{:S(2)}) copy-start(f32[256,2560]{1,0:T(8,128)S(1)} %get-tuple-element.188) | copy-start | bytes 7864324
  335.1 77.7 %copy-start.15 = (bf16[4,160,800]{2,1,0:T(8,128)(2,1)S(1)}, bf16[4,160,800]{2,1,0:T(8,128)(2,1)}, u32[]{:S(2)}) copy-start(bf16[4,160,800]{2,1,0:T(8,128)(2,1)} %get-tuple-element.124.refs_0_) | copy-start | bytes 3072004
  435.4 16.3 %copy-start.5 = (bf16[16,160,800]{2,1,0:T(8,128)(2,1)S(1)}, bf16[16,160,800]{2,1,0:T(8,128)(2,1)}, u32[]{:S(2)}) copy-start(bf16[16,160,800]{2,1,0:T(8,128)(2,1)} %copy-done.4) | copy-start | bytes 12288004
  489.4 52.5 %collective-permute-start.9 = (bf16[4,320,800]{2,1,0:T(8,128)(2,1)}, bf16[4,320,800]{2,1,0:T(8,128)(2,1)}, u32[]{:S(2)}, u32[]{:S(2)}) collective-permute-start(bf16[4,320,800]{2,1,0:T(8,128)(2,1)} %get-tuple-element.133), channel_id=1, source_target_pairs={{0,4},{4,0},{1,5},{5,1},{2,6},{6,2},{3,7},{7,3},{8,12},{12,8},{9,1... | collective-permute-start | bytes 6144008 | tf_op jit(solution)/shard_map/ppermute | solution.py:223
  547.0 9.0 collective-permute-start.10
  565.0 42.3 %collective-permute-start.11 = (bf16[1,1,1,256,2560]{4,3,2,1,0:T(8,128)(2,1)}, bf16[1,1,1,256,2560]{4,3,2,1,0:T(8,128)(2,1)S(1)}, u32[]{:S(2)}, u32[]{:S(2)}) collective-permute-start(bf16[1,1,1,256,2560]{4,3,2,1,0:T(8,128)(2,1)} %get-tuple-element.192), channel_id=1, source_target_pairs={{0,2},{2,0},{1,3},{3,1},{4,6},{6,4},{5,7},{7,5},{8,10},{10,8},{9,1... | collective-permute-start | bytes 3932168 | tf_op jit(solution)/shard_map/ppermute | solution.py:223
  565.6 56.6 %collective-permute-start.12 = (bf16[1,1,1,256,2560]{4,3,2,1,0:T(8,128)(2,1)}, bf16[1,1,1,256,2560]{4,3,2,1,0:T(8,128)(2,1)}, u32[]{:S(2)}, u32[]{:S(2)}) collective-permute-start(bf16[1,1,1,256,2560]{4,3,2,1,0:T(8,128)(2,1)} %get-tuple-element.194), channel_id=1, source_target_pairs={{0,8},{8,0},{1,9},{9,1},{2,10},{10,2},{3,11},{11,3},{4,12},{12,4},... | collective-permute-start | bytes 3932168 | tf_op jit(solution)/shard_map/ppermute | solution.py:223
  566.1 83.9 %collective-permute-start.13 = (bf16[1,1,1,256,2560]{4,3,2,1,0:T(8,128)(2,1)}, bf16[1,1,1,256,2560]{4,3,2,1,0:T(8,128)(2,1)}, u32[]{:S(2)}, u32[]{:S(2)}) collective-permute-start(bf16[1,1,1,256,2560]{4,3,2,1,0:T(8,128)(2,1)} %get-tuple-element.193), channel_id=1, source_target_pairs={{0,10},{2,8},{8,2},{10,0},{1,11},{3,9},{9,3},{11,1},{4,14},{6,12},... | collective-permute-start | bytes 3932168 | tf_op jit(solution)/shard_map/ppermute | solution.py:227
  568.5 84.2 %collective-permute-start.15 = (bf16[4,320,800]{2,1,0:T(8,128)(2,1)}, bf16[4,320,800]{2,1,0:T(8,128)(2,1)}, u32[]{:S(2)}, u32[]{:S(2)}) collective-permute-start(bf16[4,320,800]{2,1,0:T(8,128)(2,1)} %get-tuple-element.138), channel_id=1, source_target_pairs={{0,4},{4,0},{1,5},{5,1},{2,6},{6,2},{3,7},{7,3},{8,12},{12,8},{9,1... | collective-permute-start | bytes 6144008 | tf_op jit(solution)/shard_map/ppermute | solution.py:223
  573.9 78.9 %collective-permute-start.14 = (bf16[1,2,2,160,800]{4,3,2,1,0:T(8,128)(2,1)}, bf16[1,2,2,160,800]{4,3,2,1,0:T(8,128)(2,1)}, u32[]{:S(2)}, u32[]{:S(2)}) collective-permute-start(bf16[1,2,2,160,800]{4,3,2,1,0:T(8,128)(2,1)} %get-tuple-element.200), channel_id=1, source_target_pairs={{0,16},{16,0},{1,17},{17,1},{2,18},{18,2},{3,19},{19,3},{4,20},{20... | collective-permute-start | bytes 3072008 | tf_op jit(solution)/shard_map/ppermute | solution.py:223
  607.3 45.4 %copy-start.32 = (f32[256,2560]{1,0:T(8,128)S(1)}, f32[256,2560]{1,0:T(8,128)}, u32[]{:S(2)}) copy-start(f32[256,2560]{1,0:T(8,128)} %copy-done.31) | copy-start | bytes 7864324
  656.6 9.1 collective-permute-start.16
  657.3 58.5 %collective-permute-start.18 = (bf16[4,320,800]{2,1,0:T(8,128)(2,1)}, bf16[4,320,800]{2,1,0:T(8,128)(2,1)}, u32[]{:S(2)}, u32[]{:S(2)}) collective-permute-start(bf16[4,320,800]{2,1,0:T(8,128)(2,1)} %get-tuple-element.152), channel_id=1, source_target_pairs={{0,4},{4,0},{1,5},{5,1},{2,6},{6,2},{3,7},{7,3},{8,12},{12,8},{9,1... | collective-permute-start | bytes 6144008 | tf_op jit(solution)/shard_map/ppermute | solution.py:223
  662.7 53.0 %collective-permute-start.17 = (bf16[1,2,2,160,800]{4,3,2,1,0:T(8,128)(2,1)}, bf16[1,2,2,160,800]{4,3,2,1,0:T(8,128)(2,1)}, u32[]{:S(2)}, u32[]{:S(2)}) collective-permute-start(bf16[1,2,2,160,800]{4,3,2,1,0:T(8,128)(2,1)} %get-tuple-element.198), channel_id=1, source_target_pairs={{0,16},{16,0},{1,17},{17,1},{2,18},{18,2},{3,19},{19,3},{4,20},{20... | collective-permute-start | bytes 3072008 | tf_op jit(solution)/shard_map/ppermute | solution.py:223
  674.0 21.2 %copy-start.9 = (bf16[512,768]{1,0:T(8,128)(2,1)S(1)}, bf16[512,768]{1,0:T(8,128)(2,1)}, u32[]{:S(2)}) copy-start(bf16[512,768]{1,0:T(8,128)(2,1)} %copy-done.8) | copy-start | bytes 2359300
  699.0 16.8 %copy-start.53 = (bf16[4,4,16,2560]{3,2,1,0:T(8,128)(2,1)S(1)}, bf16[4,4,16,2560]{3,2,1,0:T(8,128)(2,1)}, u32[]{:S(2)}) copy-start(bf16[4,4,16,2560]{3,2,1,0:T(8,128)(2,1)} %get-tuple-element.98) | copy-start | bytes 3932164
  700.7 16.0 %copy-start.49 = (bf16[4,4,48,2560]{3,2,1,0:T(8,128)(2,1)S(1)}, bf16[4,4,48,2560]{3,2,1,0:T(8,128)(2,1)}, u32[]{:S(2)}) copy-start(bf16[4,4,48,2560]{3,2,1,0:T(8,128)(2,1)} %get-tuple-element.97) | copy-start | bytes 11796484
  719.2 15.1 %collective-permute-start.19 = (f32[256,1152]{1,0:T(8,128)S(1)}, f32[256,1152]{1,0:T(8,128)S(1)}, u32[]{:S(2)}, u32[]{:S(2)}) collective-permute-start(f32[256,1152]{1,0:T(8,128)S(1)} %constant_dynamic-slice_fusion), channel_id=1, source_target_pairs={{0,1},{1,0},{2,3},{3,2},{4,5},{5,4},{6,7},{7,6},{8,9},{9,8},{10,11... | collective-permute-start | bytes 3538952 | tf_op jit(solution)/shard_map/ppermute | solution.py:223
  (79 other events, 251.4 us)
Sparse Core Ops, SparseCore 0:
  141.8 169.1 all-gather.2
  313.2 81.7 all-gather.4
  656.7 100.8 reduce-scatter.1

commit v4 on v3

--- a/solution.py
+++ b/solution.py
@@ -287,6 +287,73 @@
         * len(pairs),
         out_specs=pl.BlockSpec((tile, width), lambda i: (i, 0)),
         compiler_params=pltpu.CompilerParams(vmem_limit_bytes=56 << 20),
+        cost_estimate=pl.CostEstimate(flops=1, transcendentals=0, bytes_accessed=1),
+    )(*(array for pair in pairs for array in pair))
+
+
+def core_features_kernel(*refs):
+    *operands, out_ref, total, sent, got, send_sems, recv_sems = refs
+    step = pl.program_id(0)
+    core = lax.axis_index("c")
+    half = total.shape[1]
+
+    @pl.when(step == 0)
+    def _():
+        meet([("c",)])
+
+    def copy(at):
+        return pltpu.make_async_remote_copy(
+            src_ref=sent.at[at],
+            dst_ref=got.at[at],
+            send_sem=send_sems.at[at],
+            recv_sem=recv_sems.at[at],
+            device_id=other_of(("c",)),
+            device_id_type=pl.DeviceIdType.MESH,
+        )
+
+    value = contract(operands[0][...], operands[1][...], 1, 1)
+    for i in range(2, len(operands), 2):
+        value += contract(operands[i][...], operands[i + 1][...], 1, 1)
+    total[0] = value[:half].astype(bf16)
+    total[1] = value[half:].astype(bf16)
+    sent[step] = total[1 - core]
+    copy(step).start()
+    out_ref[step] = total[core]
+
+    @pl.when(step == pl.num_programs(0) - 1)
+    def _():
+        for at in range(out_ref.shape[0]):
+            copy(at).wait()
+            out_ref[at] = (out_ref[at].astype(f32) + got[at].astype(f32)).astype(bf16)
+
+
+def core_features(rows, number, *pairs):
+    cols = pairs[0][0].shape[1]
+    width = pairs[0][1].shape[0]
+    block = (4, rows, width)
+    return pl.pallas_call(
+        core_features_kernel,
+        grid=(4,),
+        out_shape=jax.ShapeDtypeStruct(block, bf16),
+        in_specs=[
+            pl.BlockSpec((2 * rows, cols), lambda i: (i, 0)),
+            pl.BlockSpec((width, cols), lambda i: (0, 0), pipeline_mode=pl.Buffered(1)),
+        ]
+        * len(pairs),
+        out_specs=pl.BlockSpec(block, lambda i: (0, 0, 0)),
+        scratch_shapes=[
+            pltpu.VMEM((2, rows, width), bf16),
+            pltpu.VMEM(block, bf16),
+            pltpu.VMEM(block, bf16),
+            pltpu.SemaphoreType.DMA((4,)),
+            pltpu.SemaphoreType.DMA((4,)),
+        ],
+        compiler_params=pltpu.CompilerParams(
+            dimension_semantics=("arbitrary",),
+            collective_id=number,
+            has_side_effects=True,
+            vmem_limit_bytes=58 << 20,
+        ),
         cost_estimate=pl.CostEstimate(flops=1, transcendentals=0, bytes_accessed=1),
     )(*(array for pair in pairs for array in pair))
 
@@ -527,6 +594,97 @@
     )(small, gains, q_up, kv_up, gate, up, down)
 
 
+def second_kernel(
+    squares,
+    pair,
+    over,
+    rows_ref,
+    value_ref,
+    piece_ref,
+    rows_out,
+    tokens_out,
+    piece_out,
+    send_sems,
+    recv_sems,
+):
+    core = lax.axis_index("c")
+    places = [place_of(*square) for square in squares]
+    me = place_of(*pair)
+    one, two = pair
+    half = value_ref.shape[0] // 2
+    sender = Sender(send_sems, recv_sems)
+    rows_out[tuple(places)] = rows_ref[...]
+    tokens_out[me, core] = value_ref[...]
+    partners = [axes for one_, two_ in squares for axes in ((two_,), (one_,), (one_, two_))]
+    meet(partners + [("c",)])
+
+    def blocks(stage, place, lead=()):
+        index = lead + (slice(None),) * (stage - len(lead)) + (place,) + tuple(places[stage + 1 :])
+        return rows_out.at[index]
+
+    def send_rows(place, axes, rows=slice(None)):
+        mine = tokens_out.at[place, core, rows]
+        return sender.start(mine, mine, axes)
+
+    mine = blocks(0, places[0])
+    first = [sender.start(mine, mine, axes) for axes in partners[:3]]
+    near = send_rows(me, (two,))
+    wide = send_rows(me, (one,))
+    got = [send_rows(me, ("c",))]
+    for copy in first:
+        copy.wait_recv()
+    crossing = sender.start(piece_ref, piece_out, (over,))
+    for stage in range(1, len(squares)):
+        up, across = squares[stage]
+        mine = blocks(stage, places[stage])
+        beside = sender.start(mine, mine, (across,))
+        above = sender.start(mine, mine, (up,))
+        if stage == 1:
+            near.wait_recv()
+            corner = [send_rows(me ^ 1, (one,), slice(0, half))]
+            got.append(send_rows(me ^ 1, ("c",)))
+            wide.wait_recv()
+            corner.append(send_rows(me ^ 2, (two,), slice(half, 2 * half)))
+            got.append(send_rows(me ^ 2, ("c",)))
+        beside.wait_recv()
+        part = blocks(stage, places[stage] ^ 1, (slice(0, 2),))
+        passed = [sender.start(part, part, (up,))]
+        above.wait_recv()
+        part = blocks(stage, places[stage] ^ 2, (slice(2, 4),))
+        passed.append(sender.start(part, part, (across,)))
+        if stage == 1:
+            for copy in corner:
+                copy.wait_recv()
+            got.append(send_rows(me ^ 3, ("c",)))
+        for copy in passed:
+            copy.wait_recv()
+    for copy in got:
+        copy.wait_recv()
+    crossing.wait_recv()
+    sender.finish()
+
+
+def second_gather(squares, pair, over, rows, value, piece):
+    vmem = pl.BlockSpec(memory_space=pltpu.VMEM)
+    copies = 3 + 4 * (len(squares) - 1) + 9
+    gathered, tokens, crossed = pl.pallas_call(
+        functools.partial(second_kernel, squares, pair, over),
+        out_shape=(
+            jax.ShapeDtypeStruct((4,) * len(squares) + rows.shape, bf16),
+            jax.ShapeDtypeStruct((4, 2) + value.shape, bf16),
+            jax.ShapeDtypeStruct(piece.shape, bf16),
+        ),
+        in_specs=[vmem] * 3,
+        out_specs=(vmem,) * 3,
+        scratch_shapes=[pltpu.SemaphoreType.DMA((copies,)), pltpu.SemaphoreType.DMA((copies,))],
+        compiler_params=pltpu.CompilerParams(
+            collective_id=4, has_side_effects=True, vmem_limit_bytes=40 << 20
+        ),
+        cost_estimate=pl.CostEstimate(flops=1, transcendentals=0, bytes_accessed=1),
+    )(rows, value, piece)
+    return gathered.reshape(-1, rows.shape[1]), tokens.reshape(-1, value.shape[1]), crossed
+
+
 def lay_copies(fsdp, pair, spread, pieces, target, sems):
     copies = []
     for number, piece in enumerate(pieces):
@@ -870,7 +1028,6 @@
     q_gain_float = gain(2, q_gain.shape[0])
     kv_gain_float = gain(3, kv_gain.shape[0])
 
-    out_full = lax.all_gather(after(out_proj, gains_all), chips, axis=0, tiled=True)
     cot_float = cotangent.astype(f32)
 
     def over(pieces, axis, *ready):
@@ -880,12 +1037,8 @@
         at, dim = lax.axis_index(axis), dims.index(axis)
         return swap(pick(held, 1 - at, dim), axis), pick(held, at, dim)
 
-    def sum_of_cores(value):
-        held = value.reshape(2, 2, 2, tokens_here, width)
-        other = swap(pick(held, 1 - core, 2), "c")
-        return (pick(held, core, 2).astype(f32) + other.astype(f32)).astype(bf16)
-
     def sum_of_chips(held):
+        held = held.reshape(2, 2, tokens_here, width)
         return square_scatter(held, wide, near, 0).reshape(tokens_here, width)
 
     def core_both(value):
@@ -922,28 +1075,30 @@
     gate_pieces = [gate_held, gate_over, gate_last, swap(gate_over, axes[1])]
     for axis in axes[2:]:
         gate_pieces += over(gate_pieces, axis)
-    other_pieces = []
-    for piece in (up_held, down_held):
-        other_pieces += [swap(piece, axes[0]), swap(piece, axes[1])]
+    up_pieces = [swap(up_held, axes[0]), swap(up_held, axes[1])]
     attn, queries, log_total, local_peak = attend(
         q_full, kv_full, key_rot_all, tables(all_cos, all_sin), bias, score_scale
     )
-    attn, *early = lax.optimization_barrier((attn, *other_pieces, *gate_pieces))
-    other_pieces, gate_pieces = early[:4], early[4:]
     d_ffn = (resid_scale * cot_float).astype(bf16)
-    d_ffn_all = lax.all_gather(after(d_ffn, attn), (wide, near, "c"), axis=0, tiled=True)
+    out_full, d_ffn_all, down_over = second_gather(
+        squares, pair, axes[0], after(out_proj, attn), d_ffn, down_held
+    )
+    attn, out_full, down_over, *early = lax.optimization_barrier(
+        (attn, out_full, down_over, *up_pieces, *gate_pieces)
+    )
+    up_pieces, gate_pieces = early[:2], early[2:]
     branch = core_sum(contract(attn, out_full, 1, 1))
     mid = x_float + resid_scale * branch
     mid_normed = rms_scale(mid, post_float).astype(bf16)
     gate_full = lay(gate_pieces, fsdp, pair, spread)
     mid_all = tokens_of_chips(after(mid_normed, gate_full), pair, 1)
-    up_pieces = [up_held, *other_pieces[:2], swap(after(other_pieces[0], attn), axes[1])]
-    down_pieces = [down_held, *other_pieces[2:], swap(after(other_pieces[2], attn), axes[1])]
+    up_pieces = [up_held, *up_pieces, swap(after(up_pieces[0], attn), axes[1])]
+    down_last = swap(after(down_held, attn), axes[1])
+    mid_all, down_last, *up_pieces = lax.optimization_barrier((mid_all, down_last, *up_pieces))
+    down_pieces = [down_held, down_over, down_last, swap(after(down_over, mid_all), axes[1])]
     for axis in axes[2:]:
         up_pieces += over(up_pieces, axis)
         down_pieces += over(down_pieces, axis)
-    mid_all, *late = lax.optimization_barrier((mid_all, *up_pieces, *down_pieces))
-    up_pieces, down_pieces = late[: len(up_pieces)], late[len(up_pieces) :]
     up_full = lay(up_pieces, fsdp, pair, spread)
     gate = jnp.dot(mid_all, gate_full, preferred_element_type=f32)
     up_value = jnp.dot(mid_all, up_full, preferred_element_type=f32)
@@ -980,9 +1135,10 @@
     d_gate_late, _ = lax.optimization_barrier((d_gate, down_grad))
     gate_keep, gate_send = grad_halves(mid_all, d_gate_late, width // count, last)
     d_up_late, d_gate_late, _ = lax.optimization_barrier((d_up, d_gate, gate_keep))
-    d_mid_part = features((d_gate_late, gate_full), (d_up_late, up_full))
-    d_mid_part, *down_parts = lax.optimization_barrier((d_mid_part, *down_parts))
-    d_mid_held = sum_of_cores(d_mid_part)
+    d_mid_held = core_features(
+        tokens_here, 3, (d_gate_late, gate_full), (d_up_late, up_full)
+    )
+    d_mid_held, *down_parts = lax.optimization_barrier((d_mid_held, *down_parts))
     d_mid_normed = sum_of_chips(d_mid_held)
     mid_late, gate_send, _ = lax.optimization_barrier((mid_all, gate_send, d_mid_held))
     shape = [2] * (len(fsdp) - 1) + [width // count, -1]

time: 957 us -> 898 us (0.938)
  waiting for transfers between devices: 193 us -> 66.2 us
  Pallas kernels: 518 us -> 608 us
  local copies, waits for them, and re-layouts: 56.1 us -> 44 us
    pallas_call x0 -> x2, Pallas kernels: none -> 147 us  [the longest x1 114 us: second_gather(): pl.pallas_call(functools.partial(second_kernel, squares, pair, over), out...]
    ppermute x19 -> x17, waiting for transfers between devices: 122 us -> 39.2 us  [swap(): return lax.ppermute(value, axis, SWAP)]
    all_gather x2 -> x0, waiting for transfers between devices: 43 us -> none  [the longest x1 43 us: shards(): lax.all_gather(after(out_proj, gains_all), chips, axis=0, tiled=True)]
    pallas_call x1, Pallas kernels: 77.7 us -> 49.5 us  [tokens_of_chips(): pl.pallas_call(functools.partial(tokens_kernel, pair), out_shape=jax.Shap...]
    pallas_call x2 -> x1, Pallas kernels: 44 us -> 16.1 us  [features(): pl.pallas_call(features_kernel, grid=(rows // tile,), out_shape=jax.Shape...]
    unnamed x181 -> x203, local copies, waits for them, and re-layouts: 35.6 us -> 26.5 us
  transfers between devices with their start and end apart: 23 -> 19, of which waited for: 8 -> 5; matrix products, arithmetic and copies ran while one was open for 11% -> 12% of each run, Pallas kernels for 40% -> 52%
where the time goes in v4:
time: 898 us; the launch traced here: 892 us
  Pallas kernels  608 us (68%)
  matrix products  90.2 us (10%)
  waiting for transfers between devices  66.2 us (7%)
  other arithmetic  52.8 us (6%)
  local copies, waits for them, and re-layouts  44 us (5%)
  between operations  16.5 us (2%)
  starting transfers between devices  15 us (2%)
    pallas_call x1, Pallas kernels, last_scatter(): pl.pallas_call(functools.partial(last_kernel, fsdp, pair), out_shape=tupl...  166 us
    pallas_call x1, Pallas kernels, first_gather(): pl.pallas_call(functools.partial(first_kernel, squares, pair, spread), ou...  126 us
    pallas_call x1, Pallas kernels, second_gather(): pl.pallas_call(functools.partial(second_kernel, squares, pair, over), out...  114 us
    pallas_call x1, Pallas kernels, tokens_of_chips(): pl.pallas_call(functools.partial(tokens_kernel, pair), out_shape=jax.Shap...  49.5 us
    pallas_call x3, Pallas kernels, grad_halves(): pl.pallas_call(functools.partial(grad_kernel, axis), grid=(width // tile,...  48.3 us
    ppermute x17, waiting for transfers between devices, swap(): return lax.ppermute(value, axis, SWAP)  39.2 us
    pallas_call x1, Pallas kernels, core_features(): pl.pallas_call(core_features_kernel, grid=(4,), out_shape=jax.ShapeDtypeS...  33.6 us
    ppermute x1, waiting for transfers between devices, far(): return lax.ppermute(value, pair, [(i, 3 - i) for i in range(4)])  26.9 us
  transfers between devices with their start and end apart: 19, of which 5 were waited for; matrix products, arithmetic and copies ran while one was open for 12% of the time, Pallas kernels for 52%

profile of v4, /device:TPU:0, one launch (start us, length us, event | category | flops | bytes accessed | tf_op | source)
XLA Modules:
  0.0 892.4 jit_solution(9252009650460524624)
XLA Ops:
  14.4 125.7 %shard_map.304 = (bf16[4,4,2,80,1056]{4,3,2,1,0:T(8,128)(2,1)}, bf16[4,4,2,8,128]{4,3,2,1,0:T(8,128)(2,1)S(1)}, bf16[4,4,48,2560]{3,2,1,0:T(8,128)(2,1)}, bf16[4...) custom-call(bf16[80,1056]{1,0:T(8,128)(2,1)S(1)} %pad_maximum_fusion, ...), custom_call_target="tpu_custom_call" | custom-call | tf_op jit(solution)/shard_map/pallas_call | solution.py:575
  144.1 4.6 fusion.14
  170.8 16.7 %shard_map.305 = (bf16[512,1280]{1,0:T(8,128)(2,1)S(1)}, bf16[512,2560]{1,0:T(8,128)(2,1)S(1)}, f32[10,2,512]{2,1,0:T(2,128)S(1)}, f32[8,128]{1,0:T(8,128)S(1)}) custom-call(f32[512,2560]{1,0:T(8,128)S(1)} %fusion.51.q_ref, bf16[512,2560]{1,0:T(8,128)(2,1)S(1)} %convolution_convert_fusion.2.kv_ref, bf16[512,128]{1,0:T(8,128)(2,1)S(1)} %pad_maximum_fusion.3.rot_ref, ...), custom_call_target="tpu_custom_call" | custom-call | flops 1 | bytes 1 | tf_op jit(solution)/shard_map/pallas_call | solution.py:122
  189.0 113.7 %shard_map.306 = (bf16[4,4,160,1280]{3,2,1,0:T(8,128)(2,1)S(1)}, bf16[4,2,256,2560]{3,2,1,0:T(8,128)(2,1)}, bf16[4,160,800]{2,1,0:T(8,128)(2,1)S(1)}) custom-call(bf16[160,1280]{1,0:T(8,128)(2,1)S(1)} %copy-done.27, bf16[256,2560]{1,0:T(8,128)(2,1)S(1)} %fusion.5.value_ref, bf16[4,160,800]{2,1,0:T(8,128)(2,1)S(1)} %copy-done.9), custom_call_target="tpu_custom_call" | custom-call | flops 1 | bytes 1 | tf_op jit(solution)/shard_map/pallas_call | solution.py:670
  302.7 3.6 fusion.52
  321.6 49.5 %shard_map.308 = bf16[4,2,256,2560]{3,2,1,0:T(8,128)(2,1)S(1)} custom-call(bf16[256,2560]{1,0:T(8,128)(2,1)S(1)} %multiply_convert_fusion.4.value_ref), custom_call_target="tpu_custom_call" | custom-call | flops 1 | bytes 1 | tf_op jit(solution)/shard_map/pallas_call | solution.py:764
  372.0 3.0 copy-done
  375.1 13.1 %fusion.54 = f32[2048,800]{1,0:T(8,128)} fusion(bf16[2048,2560]{1,0:T(8,128)(2,1)S(1)} %bitcast.98, bf16[2560,800]{1,0:T(8,128)(2,1)S(1)} %bitcast.104), kind=kOutput, calls=%fused_computation.165 | convolution fusion | flops 8388608000 | bytes 21135360 | tf_op jit(solution)/shard_map/dot_general | solution.py:1103
  390.0 8.8 collective-permute-done.7.refs_3_
  399.8 16.5 %fusion.53 = f32[2048,800]{1,0:T(8,128)} fusion(bf16[2048,2560]{1,0:T(8,128)(2,1)} %bitcast.118, bf16[2560,800]{1,0:T(8,128)(2,1)S(1)} %bitcast.102), kind=kOutput, calls=%fused_computation.164 | convolution fusion | flops 8388608000 | bytes 21135360 | tf_op jit(solution)/shard_map/dot_general | solution.py:1110
  416.3 21.1 %multiply_convert_fusion = (bf16[2048,800]{1,0:T(8,128)(2,1)}, bf16[2048,800]{1,0:T(8,128)(2,1)}, bf16[2048,800]{1,0:T(8,128)(2,1)}) fusion(f32[2048,800]{1,0:T(8,128)} %fusion.54, f32[2048,800]{1,0:T(8,128)} %fusion.53, bf16[2048,2560]{1,0:T(8,128)(2,1)} %bitcast.99, bf16[2560,800]{1,0:T(8,128)(2,1)S(1)} %bitcast.106), kind=kOutput, calls=%fused_computation.2 | convolution fusion | flops 8413184000 | bytes 37519360 | tf_op jit(solution)/shard_map/dot_general | solution.py:1104
  437.4 16.1 %shard_map.311 = (bf16[4,320,800]{2,1,0:T(8,128)(2,1)}, bf16[4,320,800]{2,1,0:T(8,128)(2,1)}) custom-call(bf16[2048,2560]{1,0:T(8,128)(2,1)} %bitcast.119, bf16[2048,800]{1,0:T(8,128)(2,1)} %get-tuple-element.141.right_ref.refs_0_), custom_call_target="tpu_custom_call" | custom-call | flops 1 | bytes 1 | tf_op jit(solution)/shard_map/pallas_call | solution.py:380
  454.4 16.1 %shard_map.312 = (bf16[4,320,800]{2,1,0:T(8,128)(2,1)}, bf16[4,320,800]{2,1,0:T(8,128)(2,1)}) custom-call(bf16[2048,2560]{1,0:T(8,128)(2,1)} %bitcast.100, bf16[2048,800]{1,0:T(8,128)(2,1)} %get-tuple-element.131.right_ref.refs_0_), custom_call_target="tpu_custom_call" | custom-call | flops 1 | bytes 1 | tf_op jit(solution)/shard_map/pallas_call | solution.py:380
  470.5 33.6 %shard_map.313 = bf16[4,256,2560]{2,1,0:T(8,128)(2,1)} custom-call(bf16[2048,800]{1,0:T(8,128)(2,1)} %get-tuple-element.131.right_ref.refs_0_, bf16[2560,800]{1,0:T(8,128)(2,1)} %bitcast.105, bf16[2048,800]{1,0:T(8,128)(2,1)} %get-tuple-element.132.refs_2_.right_ref, bf16[2560,800]{1,0:T(8,128)(2,1)} %bitcast.107), custom_call_target="tpu_custom_call" | custom-call | flops 1 | bytes 1 | tf_op jit(solution)/shard_map/pallas_call | solution.py:334
  506.4 4.3 constant_dynamic-slice_fusion.7
  518.9 16.1 %shard_map.314 = (bf16[4,320,800]{2,1,0:T(8,128)(2,1)}, bf16[4,320,800]{2,1,0:T(8,128)(2,1)}) custom-call(bf16[2048,2560]{1,0:T(8,128)(2,1)} %bitcast.101, bf16[2048,800]{1,0:T(8,128)(2,1)} %get-tuple-element.132.refs_2_.right_ref), custom_call_target="tpu_custom_call" | custom-call | flops 1 | bytes 1 | tf_op jit(solution)/shard_map/pallas_call | solution.py:380
  535.0 16.1 %shard_map.315 = bf16[2048,2560]{1,0:T(8,128)(2,1)} custom-call(bf16[2048,800]{1,0:T(8,128)(2,1)} %get-tuple-element.141.right_ref.refs_0_, bf16[2560,800]{1,0:T(8,128)(2,1)} %bitcast.103), custom_call_target="tpu_custom_call" | custom-call | flops 1 | bytes 1 | tf_op jit(solution)/shard_map/pallas_call | solution.py:279
  551.2 16.1 %collective-permute-done.10 = bf16[1,1,256,2560]{3,2,1,0:T(8,128)(2,1)} collective-permute-done((bf16[1,1,256,2560]{3,2,1,0:T(8,128)(2,1)}, bf16[1,1,256,2560]{3,2,1,0:T(8,128)(2,1)}, u32[]{:S(2)}, u32[]{:S(2)}) %collective-permute-start.10) | collective-permute-done | bytes 1310752 | tf_op jit(solution)/shard_map/ppermute | solution.py:223
  567.3 26.9 %collective-permute-done.11 = bf16[1,1,256,2560]{3,2,1,0:T(8,128)(2,1)} collective-permute-done((bf16[1,1,256,2560]{3,2,1,0:T(8,128)(2,1)}, bf16[1,1,256,2560]{3,2,1,0:T(8,128)(2,1)}, u32[]{:S(2)}, u32[]{:S(2)}) %collective-permute-start.11) | collective-permute-done | bytes 1310752 | tf_op jit(solution)/shard_map/ppermute | solution.py:227
  594.2 3.1 add_bitcast_fusion
  603.8 2.9 add_convert_fusion.1
  613.8 6.7 convolution_convert_fusion.4.d_mixed_ref
  620.5 20.9 %shard_map.316 = (bf16[512,2560]{1,0:T(8,128)(2,1)S(1)}, bf16[512,2560]{1,0:T(8,128)(2,1)S(1)}, f32[512,128]{1,0:T(8,128)S(1)}) custom-call(bf16[512,2560]{1,0:T(8,128)(2,1)S(1)} %copy-done.11, bf16[512,2560]{1,0:T(8,128)(2,1)S(1)} %copy-done.2, bf16[512,1280]{1,0:T(8,128)(2,1)S(1)} %convolution_convert_fusion.4.d_mixed_ref, ...), custom_call_target="tpu_custom_call" | custom-call | flops 1 | bytes 1 | tf_op jit(solution)/shard_map/pallas_call | solution.py:195
  641.4 4.1 shard_map.317
  647.1 13.4 %collective-permute-done.15 = bf16[1,2,2,160,800]{4,3,2,1,0:T(8,128)(2,1)} collective-permute-done((bf16[1,2,2,160,800]{4,3,2,1,0:T(8,128)(2,1)}, bf16[1,2,2,160,800]{4,3,2,1,0:T(8,128)(2,1)}, u32[]{:S(2)}, u32[]{:S(2)}) %collective-permute-start.15) | collective-permute-done | bytes 1024032 | tf_op jit(solution)/shard_map/ppermute | solution.py:223
  669.6 3.7 add_convert_fusion
  673.2 5.6 convolution_convert_fusion
  682.1 6.4 fusion.4
  689.5 4.5 convolution_convert_fusion.1
  694.1 165.8 %shard_map.318 = (f32[80,1056]{1,0:T(8,128)}, f32[8,128]{1,0:T(8,128)}, f32[48,1920]{1,0:T(8,128)}, f32[16,2560]{1,0:T(8,128)}, f32[160,1280]{1,0:T(8,128)}, /*i...) custom-call(f32[8,128]{1,0:T(8,128)} %copy-done.30, bf16[2,2,2,2,2,80,1056]{6,5,4,3,2,1,0:T(8,128)(2,1)} %bitcast.115, ...), custom_call_target="tpu_custom_call" | custom-call | tf_op jit(solution)/shard_map/pallas_call | solution.py:946
  865.6 2.9 shard_map.321
  874.3 5.8 fusion.6
  (349 shorter events, 108.5 us)
Async XLA Ops:
  7.2 872.9 %reduce-scatter.2.cloned.1.call-start = ((), (), s32[]{:S(2)}) async-start(), calls=%async_computation.1 | async-start | bytes 11796480 | tf_op jit(solution)/shard_map/reduce_scatter | solution.py:1155
  14.4 129.3 %copy-start.37 = (bf16[256,2560]{1,0:T(8,128)(2,1)S(1)}, bf16[256,2560]{1,0:T(8,128)(2,1)}, u32[]{:S(2)}) copy-start(bf16[256,2560]{1,0:T(8,128)(2,1)} %param.17) | copy-start | bytes 3932164
  141.1 161.6 %collective-permute-start.1 = (bf16[4,160,800]{2,1,0:T(8,128)(2,1)}, bf16[4,160,800]{2,1,0:T(8,128)(2,1)S(1)}, u32[]{:S(2)}, u32[]{:S(2)}) collective-permute-start(bf16[4,160,800]{2,1,0:T(8,128)(2,1)} %get-tuple-element.124.refs_0_), channel_id=1, source_target_pairs={{0,16},{16,0},{1,17},{17,1},{2,18},{18,2},{3,19},{19,3},{4,20},{20... | collective-permute-start | bytes 3072008 | tf_op jit(solution)/shard_map/ppermute | solution.py:223
  142.4 160.3 %collective-permute-start.2 = (bf16[4,160,800]{2,1,0:T(8,128)(2,1)}, bf16[4,160,800]{2,1,0:T(8,128)(2,1)}, u32[]{:S(2)}, u32[]{:S(2)}) collective-permute-start(bf16[4,160,800]{2,1,0:T(8,128)(2,1)} %get-tuple-element.124.refs_0_), channel_id=1, source_target_pairs={{0,4},{4,0},{1,5},{5,1},{2,6},{6,2},{3,7},{7,3},{8,12},{12,8},{9,1... | collective-permute-start | bytes 3072008 | tf_op jit(solution)/shard_map/ppermute | solution.py:223
  155.7 7.6 collective-permute-start
  155.7 147.0 %collective-permute-start.3 = (bf16[4,160,800]{2,1,0:T(8,128)(2,1)}, bf16[4,160,800]{2,1,0:T(8,128)(2,1)}, u32[]{:S(2)}, u32[]{:S(2)}) collective-permute-start(bf16[4,160,800]{2,1,0:T(8,128)(2,1)} %get-tuple-element.113.refs_1_), channel_id=1, source_target_pairs={{0,4},{4,0},{1,5},{5,1},{2,6},{6,2},{3,7},{7,3},{8,12},{12,8},{9,1... | collective-permute-start | bytes 3072008 | tf_op jit(solution)/shard_map/ppermute | solution.py:223
  170.8 18.2 %copy-start.9 = (bf16[4,160,800]{2,1,0:T(8,128)(2,1)S(1)}, bf16[4,160,800]{2,1,0:T(8,128)(2,1)}, u32[]{:S(2)}) copy-start(bf16[4,160,800]{2,1,0:T(8,128)(2,1)} %get-tuple-element.117.piece_ref.refs_0_) | copy-start | bytes 3072004
  170.8 18.2 %copy-start.27 = (bf16[160,1280]{1,0:T(8,128)(2,1)S(1)}, bf16[160,1280]{1,0:T(8,128)(2,1)}, u32[]{:S(2)}) copy-start(bf16[160,1280]{1,0:T(8,128)(2,1)} %rows_ref) | copy-start | bytes 1228804
  189.0 117.3 %copy-start.30 = (f32[8,128]{1,0:T(8,128)}, f32[8,128]{1,0:T(8,128)S(1)}, u32[]{:S(2)}) copy-start(f32[8,128]{1,0:T(8,128)S(1)} %get-tuple-element.156.peak_ref) | copy-start | bytes 12292
  189.0 117.3 %copy-start.32 = (bf16[512,1280]{1,0:T(8,128)(2,1)}, bf16[512,1280]{1,0:T(8,128)(2,1)S(1)}, u32[]{:S(2)}) copy-start(bf16[512,1280]{1,0:T(8,128)(2,1)S(1)} %get-tuple-element.108) | copy-start | bytes 3932164
  309.5 6.8 collective-permute-start.4
  309.6 61.6 %collective-permute-start.6 = (bf16[4,160,800]{2,1,0:T(8,128)(2,1)S(1)}, bf16[4,160,800]{2,1,0:T(8,128)(2,1)S(1)}, u32[]{:S(2)}, u32[]{:S(2)}) collective-permute-start(bf16[4,160,800]{2,1,0:T(8,128)(2,1)S(1)} %collective-permute-done.1.refs_1_), channel_id=1, source_target_pairs={{0,4},{4,0},{1,5},{5,1},{2,6},{6,2},{3,7},{7,3},{8,12},{12,8},{9,1... | collective-permute-start | bytes 3072008 | tf_op jit(solution)/shard_map/ppermute | solution.py:223
  311.2 60.0 %collective-permute-start.5 = (bf16[4,160,800]{2,1,0:T(8,128)(2,1)S(1)}, bf16[4,160,800]{2,1,0:T(8,128)(2,1)S(1)}, u32[]{:S(2)}, u32[]{:S(2)}) collective-permute-start(bf16[4,160,800]{2,1,0:T(8,128)(2,1)S(1)} %copy-done.9), channel_id=1, source_target_pairs={{0,4},{4,0},{1,5},{5,1},{2,6},{6,2},{3,7},{7,3},{8,12},{12,8},{9,1... | collective-permute-start | bytes 3072008 | tf_op jit(solution)/shard_map/ppermute | solution.py:223
  316.2 55.8 %copy-start.4 = (bf16[16,160,800]{2,1,0:T(8,128)(2,1)}, bf16[16,160,800]{2,1,0:T(8,128)(2,1)S(1)}, u32[]{:S(2)}) copy-start(bf16[16,160,800]{2,1,0:T(8,128)(2,1)S(1)} %shard_map.307) | copy-start | bytes 12288004
  321.3 49.8 %copy-start.34 = (f32[256,2560]{1,0:T(8,128)}, f32[256,2560]{1,0:T(8,128)S(1)}, u32[]{:S(2)}) copy-start(f32[256,2560]{1,0:T(8,128)S(1)} %get-tuple-element.188) | copy-start | bytes 7864324
  321.6 49.5 %copy-start.21 = (bf16[4,160,800]{2,1,0:T(8,128)(2,1)S(1)}, bf16[4,160,800]{2,1,0:T(8,128)(2,1)}, u32[]{:S(2)}) copy-start(bf16[4,160,800]{2,1,0:T(8,128)(2,1)} %copy-done.20) | copy-start | bytes 3072004
  371.2 17.1 %copy-start.16 = (bf16[4,160,800]{2,1,0:T(8,128)(2,1)S(1)}, bf16[4,160,800]{2,1,0:T(8,128)(2,1)}, u32[]{:S(2)}) copy-start(bf16[4,160,800]{2,1,0:T(8,128)(2,1)} %get-tuple-element.124.refs_0_) | copy-start | bytes 3072004
  371.2 27.6 %collective-permute-start.7 = (bf16[4,160,800]{2,1,0:T(8,128)(2,1)S(1)}, bf16[4,160,800]{2,1,0:T(8,128)(2,1)S(1)}, u32[]{:S(2)}, u32[]{:S(2)}) collective-permute-start(bf16[4,160,800]{2,1,0:T(8,128)(2,1)S(1)} %copy-done.21), channel_id=1, source_target_pairs={{0,4},{4,0},{1,5},{5,1},{2,6},{6,2},{3,7},{7,3},{8,12},{12,8},{9,1... | collective-permute-start | bytes 3072008 | tf_op jit(solution)/shard_map/ppermute | solution.py:223
  390.0 26.3 %copy-start.5 = (bf16[16,160,800]{2,1,0:T(8,128)(2,1)}, bf16[16,160,800]{2,1,0:T(8,128)(2,1)S(1)}, u32[]{:S(2)}) copy-start(bf16[16,160,800]{2,1,0:T(8,128)(2,1)S(1)} %shard_map.310) | copy-start | bytes 12288004
  453.5 51.5 %collective-permute-start.8 = (bf16[4,320,800]{2,1,0:T(8,128)(2,1)}, bf16[4,320,800]{2,1,0:T(8,128)(2,1)S(1)}, u32[]{:S(2)}, u32[]{:S(2)}) collective-permute-start(bf16[4,320,800]{2,1,0:T(8,128)(2,1)} %get-tuple-element.133), channel_id=1, source_target_pairs={{0,4},{4,0},{1,5},{5,1},{2,6},{6,2},{3,7},{7,3},{8,12},{12,8},{9,1... | collective-permute-start | bytes 6144008 | tf_op jit(solution)/shard_map/ppermute | solution.py:223
  510.7 56.6 %collective-permute-start.10 = (bf16[1,1,256,2560]{3,2,1,0:T(8,128)(2,1)}, bf16[1,1,256,2560]{3,2,1,0:T(8,128)(2,1)}, u32[]{:S(2)}, u32[]{:S(2)}) collective-permute-start(bf16[1,1,256,2560]{3,2,1,0:T(8,128)(2,1)} %get-tuple-element.194), channel_id=1, source_target_pairs={{0,8},{8,0},{1,9},{9,1},{2,10},{10,2},{3,11},{11,3},{4,12},{12,4},... | collective-permute-start | bytes 3932168 | tf_op jit(solution)/shard_map/ppermute | solution.py:223
  512.3 81.9 %collective-permute-start.11 = (bf16[1,1,256,2560]{3,2,1,0:T(8,128)(2,1)}, bf16[1,1,256,2560]{3,2,1,0:T(8,128)(2,1)}, u32[]{:S(2)}, u32[]{:S(2)}) collective-permute-start(bf16[1,1,256,2560]{3,2,1,0:T(8,128)(2,1)} %get-tuple-element.193), channel_id=1, source_target_pairs={{0,10},{2,8},{8,2},{10,0},{1,11},{3,9},{9,3},{11,1},{4,14},{6,12},... | collective-permute-start | bytes 3932168 | tf_op jit(solution)/shard_map/ppermute | solution.py:227
  513.7 80.5 %collective-permute-start.9 = (bf16[1,1,256,2560]{3,2,1,0:T(8,128)(2,1)}, bf16[1,1,256,2560]{3,2,1,0:T(8,128)(2,1)}, u32[]{:S(2)}, u32[]{:S(2)}) collective-permute-start(bf16[1,1,256,2560]{3,2,1,0:T(8,128)(2,1)} %get-tuple-element.192), channel_id=1, source_target_pairs={{0,2},{2,0},{1,3},{3,1},{4,6},{6,4},{5,7},{7,5},{8,10},{10,8},{9,1... | collective-permute-start | bytes 3932168 | tf_op jit(solution)/shard_map/ppermute | solution.py:223
  514.1 83.2 %collective-permute-start.13 = (bf16[4,320,800]{2,1,0:T(8,128)(2,1)}, bf16[4,320,800]{2,1,0:T(8,128)(2,1)}, u32[]{:S(2)}, u32[]{:S(2)}) collective-permute-start(bf16[4,320,800]{2,1,0:T(8,128)(2,1)} %get-tuple-element.138), channel_id=1, source_target_pairs={{0,4},{4,0},{1,5},{5,1},{2,6},{6,2},{3,7},{7,3},{8,12},{12,8},{9,1... | collective-permute-start | bytes 6144008 | tf_op jit(solution)/shard_map/ppermute | solution.py:223
  517.4 79.9 %collective-permute-start.12 = (bf16[1,2,2,160,800]{4,3,2,1,0:T(8,128)(2,1)S(1)}, bf16[1,2,2,160,800]{4,3,2,1,0:T(8,128)(2,1)}, u32[]{:S(2)}, u32[]{:S(2)}) collective-permute-start(bf16[1,2,2,160,800]{4,3,2,1,0:T(8,128)(2,1)S(1)} %get-tuple-element.200), channel_id=1, source_target_pairs={{0,16},{16,0},{1,17},{17,1},{2,18},{18,2},{3,19},{19,3},{4,20},{20... | collective-permute-start | bytes 3072008 | tf_op jit(solution)/shard_map/ppermute | solution.py:223
  551.2 46.2 %copy-start.35 = (f32[256,2560]{1,0:T(8,128)S(1)}, f32[256,2560]{1,0:T(8,128)}, u32[]{:S(2)}) copy-start(f32[256,2560]{1,0:T(8,128)} %copy-done.34) | copy-start | bytes 7864324
  551.2 46.2 %copy-start.69 = (f32[2560]{0:T(1024)S(1)}, f32[2560]{0:T(1024)}, u32[]{:S(2)}) copy-start(f32[2560]{0:T(1024)} %copy-done.68) | copy-start | bytes 30724
  601.2 10.9 %collective-permute-start.14 = (bf16[256,2560]{1,0:T(8,128)(2,1)S(1)}, bf16[256,2560]{1,0:T(8,128)(2,1)}, u32[]{:S(2)}, u32[]{:S(2)}) collective-permute-start(bf16[256,2560]{1,0:T(8,128)(2,1)S(1)} %get-tuple-element.185), channel_id=1, source_target_pairs={{0,1},{1,0},{2,3},{3,2},{4,5},{5,4},{6,7},{7,6},{8,9},{9,8},{10,11... | collective-permute-start | bytes 3932168 | tf_op jit(solution)/shard_map/ppermute | solution.py:223
  602.0 58.5 %collective-permute-start.16 = (bf16[4,320,800]{2,1,0:T(8,128)(2,1)}, bf16[4,320,800]{2,1,0:T(8,128)(2,1)}, u32[]{:S(2)}, u32[]{:S(2)}) collective-permute-start(bf16[4,320,800]{2,1,0:T(8,128)(2,1)} %get-tuple-element.152), channel_id=1, source_target_pairs={{0,4},{4,0},{1,5},{5,1},{2,6},{6,2},{3,7},{7,3},{8,12},{12,8},{9,1... | collective-permute-start | bytes 6144008 | tf_op jit(solution)/shard_map/ppermute | solution.py:223
  608.2 52.3 %collective-permute-start.15 = (bf16[1,2,2,160,800]{4,3,2,1,0:T(8,128)(2,1)}, bf16[1,2,2,160,800]{4,3,2,1,0:T(8,128)(2,1)}, u32[]{:S(2)}, u32[]{:S(2)}) collective-permute-start(bf16[1,2,2,160,800]{4,3,2,1,0:T(8,128)(2,1)} %get-tuple-element.198), channel_id=1, source_target_pairs={{0,16},{16,0},{1,17},{17,1},{2,18},{18,2},{3,19},{19,3},{4,20},{20... | collective-permute-start | bytes 3072008 | tf_op jit(solution)/shard_map/ppermute | solution.py:223
  620.5 20.9 %copy-start.8 = (bf16[512,768]{1,0:T(8,128)(2,1)S(1)}, bf16[512,768]{1,0:T(8,128)(2,1)}, u32[]{:S(2)}) copy-start(bf16[512,768]{1,0:T(8,128)(2,1)} %copy-done.7) | copy-start | bytes 2359300
  663.9 15.0 %collective-permute-start.17 = (f32[256,1152]{1,0:T(8,128)S(1)}, f32[256,1152]{1,0:T(8,128)S(1)}, u32[]{:S(2)}, u32[]{:S(2)}) collective-permute-start(f32[256,1152]{1,0:T(8,128)S(1)} %constant_dynamic-slice_fusion), channel_id=1, source_target_pairs={{0,1},{1,0},{2,3},{3,2},{4,5},{5,4},{6,7},{7,6},{8,9},{9,8},{10,11... | collective-permute-start | bytes 3538952 | tf_op jit(solution)/shard_map/ppermute | solution.py:223
  (86 other events, 396.2 us)
Sparse Core Ops, SparseCore 0:
  601.4 102.6 reduce-scatter.1

commit v5 on v4

--- a/solution.py
+++ b/solution.py
@@ -238,6 +238,28 @@
 def both(own, other, axis, dim):
     here = lax.axis_index(axis) == 0
     return jnp.concatenate([jnp.where(here, own, other), jnp.where(here, other, own)], axis=dim)
+
+
+def plain_grad_kernel(left_ref, right_ref, out_ref):
+    out_ref[...] = contract(left_ref[...], right_ref[...], 0, 0).astype(bf16)
+
+
+def plain_grad(left, right):
+    rows, width = left.shape
+    cols = right.shape[1]
+    tile = 512
+    return pl.pallas_call(
+        plain_grad_kernel,
+        grid=(width // tile,),
+        out_shape=jax.ShapeDtypeStruct((width, cols), bf16),
+        in_specs=[
+            pl.BlockSpec((rows, tile), lambda i: (0, i)),
+            pl.BlockSpec((rows, cols), lambda i: (0, 0)),
+        ],
+        out_specs=pl.BlockSpec((tile, cols), lambda i: (i, 0)),
+        compiler_params=pltpu.CompilerParams(vmem_limit_bytes=32 << 20),
+        cost_estimate=pl.CostEstimate(flops=1, transcendentals=0, bytes_accessed=1),
+    )(left, right)
 
 
 def heads_grad_kernel(latent_ref, d_ref, out_ref):
@@ -874,7 +896,7 @@
     for rows, order in zip(halves_of(out_sum.shape[0]), (turned, upward)):
         part = out_ref.at[(slice(None),) * stages + (rows,)]
         outs.append(Reduction(sender, part, fsdp, order, buffers(stages), out_sum.at[rows]))
-    over = buffers(1)[0]
+    over = buffers(2)
     peaks = buffers(stages)
     me = place_of(*pair)
     row = lax.axis_index(fsdp[0])
@@ -901,22 +923,27 @@
     for part in (small, gains, q, outs[0], kv):
         part.begin()
     peak_sent = send_peaks(0)
-    crossing = sender.start(up_ref.at[1 - row], over, (fsdp[0],))
+    crossing = sender.start(down_ref.at[1 - row], over[0], (fsdp[0],))
     outs[1].begin()
-    columns = send_columns(0, down_ref)
+    columns = send_columns(1, gate_ref)
     small.end()
     gains.end()
-    columns += send_columns(1, gate_ref)
     peak_sent = next_peaks(0, peak_sent)
     for part in (q, kv, outs[0]):
         part.end()
-    crossing.wait_recv()
-    over[...] = (up_ref[row].astype(f32) + over[...].astype(f32)).astype(bf16)
-    columns += send_columns(2, over)
+    def crossed(which, ref, buffer):
+        crossing.wait_recv()
+        buffer[...] = (ref[row].astype(f32) + buffer[...].astype(f32)).astype(bf16)
+        return send_columns(which, buffer)
+
+    columns += crossed(0, down_ref, over[0])
+    crossing = sender.start(up_ref.at[1 - row], over[1], (fsdp[0],))
     for stage in range(1, stages):
         peak_sent = next_peaks(stage, peak_sent)
         for part in (outs[1], small, gains, q, kv, outs[0]):
             part.end()
+        if stage == 1:
+            columns += crossed(2, up_ref, over[1])
     for reduction in (q, kv, outs[0], small, gains, outs[1]):
         reduction.finish()
     for copy in columns:
@@ -939,15 +966,15 @@
         + buffers(q, stages)
         + buffers(kv, stages)
         + [buf for rows in halves_of(out.shape[-2]) for buf in buffers(out, stages, rows.size)]
-        + [pltpu.VMEM(down.shape, bf16)]
+        + [pltpu.VMEM(gate.shape, bf16)] * 2
         + [pltpu.VMEM(peak.shape, f32)] * stages
     )
-    copies = 2 * (stages + 1) + 4 * stages + 1 + 9 + stages
+    copies = 2 * (stages + 1) + 4 * stages + 2 + 9 + stages
     return pl.pallas_call(
         functools.partial(last_kernel, fsdp, pair),
         out_shape=tuple(jax.ShapeDtypeStruct(x.shape[-2:], f32) for x in (small, gains, q, kv, out))
         + (
-            jax.ShapeDtypeStruct((3,) + down.shape, bf16),
+            jax.ShapeDtypeStruct((3,) + gate.shape, bf16),
             jax.ShapeDtypeStruct(peak.shape, f32),
         ),
         in_specs=[vmem] * 9,
@@ -1143,14 +1170,14 @@
     mid_late, gate_send, _ = lax.optimization_barrier((mid_all, gate_send, d_mid_held))
     shape = [2] * (len(fsdp) - 1) + [width // count, -1]
     gate_parts = (swap(gate_send, last).reshape(shape), gate_keep.reshape(shape))
-    down_parts = cross(inner(added(down_parts)))
+    down_held = inner(added(down_parts))
     *up_parts, up_grad = begin(mid_late, d_up, gate_parts[0])
     ffn_part = features((after(act, up_grad), down_proj_full))
     post_pull = jax.vjp(rms_scale, mid, post_float)[1]
     d_mid_normed, *early = lax.optimization_barrier(
-        (d_mid_normed, *down_parts, *gate_parts, ffn_part)
-    )
-    down_parts, gate_parts, ffn_part = early[:2], early[2:4], early[4]
+        (d_mid_normed, down_held, *gate_parts, ffn_part)
+    )
+    down_held, gate_parts, ffn_part = early[0], early[1:3], early[3]
     d_mid_norm, post_grad = post_pull(d_mid_normed)
     ffn = lax.psum_scatter(
         after(ffn_part, d_mid_norm), (wide, near, "c"), scatter_dimension=0, tiled=True
@@ -1172,14 +1199,14 @@
         score_scale,
     )
     q_up_grad = heads_grad(q_lat_all, d_q)
-    d_q, d_kv, q_up_grad, *early = lax.optimization_barrier(
-        (d_q, d_kv, q_up_grad, *gate_parts, *up_parts)
-    )
-    gate_parts, up_parts = early[:2], early[2:]
-    out_grad = rows_first(contract(after(d_branch_all, d_q), attn, 0, 0).astype(bf16))
-    kv_up_grad = rows_first(contract(kv_lat_all, d_kv, 0, 0).astype(bf16))
+    out_grad = plain_grad(after(d_branch_all, q_up_grad), attn)
     d_q_lat_part = contract(d_q, q_up_full, 1, 1)
     d_kv_lat_part = contract(d_kv, kv_up_full, 1, 1)
+    d_q_lat_part, d_kv_lat_part, d_kv, out_grad, *early = lax.optimization_barrier(
+        (d_q_lat_part, d_kv_lat_part, d_kv, out_grad, *gate_parts, *up_parts)
+    )
+    gate_parts, up_parts = early[:2], early[2:]
+    kv_up_grad = rows_first(contract(kv_lat_all, d_kv, 0, 0).astype(bf16))
     d_latents = core_sum(jnp.concatenate([d_q_lat_part, d_kv_lat_part, d_rot_part], axis=1))
     q_pull = jax.vjp(rms_scale, q_pre, q_gain_float)[1]
     d_q_pre, q_gain_grad = q_pull(d_latents[:, :q_rank])
@@ -1197,7 +1224,7 @@
 
     rows_here = width // count
     ffn_held = [
-        added(down_parts).reshape(4, rows_here, -1),
+        down_held.reshape(2, 4, rows_here, -1),
         added(gate_parts).reshape(4, rows_here, -1),
         inner(added(up_parts)).reshape(2, 4, rows_here, -1),
     ]

time: 898 us -> 889 us (0.990)
  waiting for transfers between devices: 66.2 us -> 35 us
  Pallas kernels: 608 us -> 629 us
    ppermute x17 -> x16, waiting for transfers between devices: 39.2 us -> 16.5 us  [swap(): return lax.ppermute(value, axis, SWAP)]
    pallas_call x1, Pallas kernels: 166 us -> 183 us  [last_scatter(): pl.pallas_call(functools.partial(last_kernel, fsdp, pair), out_shape=tupl...]
    dot_general x7 -> x6, matrix products: 25.1 us -> 19.7 us  [contract(): lax.dot_general(left, right, (((left_dim,), (right_dim,)), ((), ())), pre...]
  transfers between devices with their start and end apart: 19 -> 18, of which waited for: 5 -> 5; matrix products, arithmetic and copies ran while one was open for 12% -> 11% of each run, Pallas kernels for 52% -> 55%
where the time goes in v5:
time: 889 us; the launch traced here: 880 us
  Pallas kernels  629 us (71%)
  matrix products  81.7 us (9%)
  other arithmetic  53 us (6%)
  local copies, waits for them, and re-layouts  49.7 us (6%)
  waiting for transfers between devices  35 us (4%)
  between operations  16.9 us (2%)
  starting transfers between devices  14.9 us (2%)
    pallas_call x1, Pallas kernels, last_scatter(): pl.pallas_call(functools.partial(last_kernel, fsdp, pair), out_shape=tupl...  183 us
    pallas_call x1, Pallas kernels, first_gather(): pl.pallas_call(functools.partial(first_kernel, squares, pair, spread), ou...  126 us
    pallas_call x1, Pallas kernels, second_gather(): pl.pallas_call(functools.partial(second_kernel, squares, pair, over), out...  114 us
    pallas_call x1, Pallas kernels, tokens_of_chips(): pl.pallas_call(functools.partial(tokens_kernel, pair), out_shape=jax.Shap...  49.4 us
    pallas_call x3, Pallas kernels, grad_halves(): pl.pallas_call(functools.partial(grad_kernel, axis), grid=(width // tile,...  48.4 us
    pallas_call x1, Pallas kernels, core_features(): pl.pallas_call(core_features_kernel, grid=(4,), out_shape=jax.ShapeDtypeS...  33.9 us
    unnamed x203, local copies, waits for them, and re-layouts  31.9 us
    dot_general x1, matrix products, shards(): up_value = jnp.dot(mid_all, up_full, preferred_element_type=f32)  21.1 us
  transfers between devices with their start and end apart: 18, of which 5 were waited for; matrix products, arithmetic and copies ran while one was open for 11% of the time, Pallas kernels for 55%

profile of v5, /device:TPU:0, one launch (start us, length us, event | category | flops | bytes accessed | tf_op | source)
XLA Modules:
  0.0 880.4 jit_solution(5555111208394007446)
XLA Ops:
  14.4 125.6 %shard_map.304 = (bf16[4,4,2,80,1056]{4,3,2,1,0:T(8,128)(2,1)}, bf16[4,4,2,8,128]{4,3,2,1,0:T(8,128)(2,1)S(1)}, bf16[4,4,48,2560]{3,2,1,0:T(8,128)(2,1)}, bf16[4...) custom-call(bf16[80,1056]{1,0:T(8,128)(2,1)S(1)} %pad_maximum_fusion, ...), custom_call_target="tpu_custom_call" | custom-call | tf_op jit(solution)/shard_map/pallas_call | solution.py:597
  144.1 4.6 fusion.14
  170.1 16.7 %shard_map.305 = (bf16[512,1280]{1,0:T(8,128)(2,1)S(1)}, bf16[512,2560]{1,0:T(8,128)(2,1)S(1)}, f32[10,2,512]{2,1,0:T(2,128)S(1)}, f32[8,128]{1,0:T(8,128)S(1)}) custom-call(f32[512,2560]{1,0:T(8,128)S(1)} %fusion.51.q_ref, bf16[512,2560]{1,0:T(8,128)(2,1)S(1)} %convolution_convert_fusion.1.kv_ref, bf16[512,128]{1,0:T(8,128)(2,1)S(1)} %pad_maximum_fusion.2.rot_ref, ...), custom_call_target="tpu_custom_call" | custom-call | flops 1 | bytes 1 | tf_op jit(solution)/shard_map/pallas_call | solution.py:122
  188.3 113.6 %shard_map.306 = (bf16[4,4,160,1280]{3,2,1,0:T(8,128)(2,1)S(1)}, bf16[4,2,256,2560]{3,2,1,0:T(8,128)(2,1)}, bf16[4,160,800]{2,1,0:T(8,128)(2,1)S(1)}) custom-call(bf16[160,1280]{1,0:T(8,128)(2,1)S(1)} %copy-done.30, bf16[256,2560]{1,0:T(8,128)(2,1)S(1)} %fusion.5.value_ref, bf16[4,160,800]{2,1,0:T(8,128)(2,1)S(1)} %copy-done.10), custom_call_target="tpu_custom_call" | custom-call | flops 1 | bytes 1 | tf_op jit(solution)/shard_map/pallas_call | solution.py:692
  301.9 3.6 fusion.52
  322.2 49.4 %shard_map.308 = bf16[4,2,256,2560]{3,2,1,0:T(8,128)(2,1)S(1)} custom-call(bf16[256,2560]{1,0:T(8,128)(2,1)S(1)} %multiply_convert_fusion.4.value_ref), custom_call_target="tpu_custom_call" | custom-call | flops 1 | bytes 1 | tf_op jit(solution)/shard_map/pallas_call | solution.py:786
  375.6 13.2 %fusion.54 = f32[2048,800]{1,0:T(8,128)} fusion(bf16[2048,2560]{1,0:T(8,128)(2,1)S(1)} %bitcast.96, bf16[2560,800]{1,0:T(8,128)(2,1)S(1)} %bitcast.103), kind=kOutput, calls=%fused_computation.163 | convolution fusion | flops 8388608000 | bytes 21135360 | tf_op jit(solution)/shard_map/dot_general | solution.py:1130
  390.7 8.6 collective-permute-done.7.refs_3_
  400.3 16.5 %fusion.53 = f32[2048,800]{1,0:T(8,128)} fusion(bf16[2048,2560]{1,0:T(8,128)(2,1)} %bitcast.119, bf16[2560,800]{1,0:T(8,128)(2,1)S(1)} %bitcast.101), kind=kOutput, calls=%fused_computation.162 | convolution fusion | flops 8388608000 | bytes 21135360 | tf_op jit(solution)/shard_map/dot_general | solution.py:1137
  416.8 21.1 %multiply_convert_fusion = (bf16[2048,800]{1,0:T(8,128)(2,1)}, bf16[2048,800]{1,0:T(8,128)(2,1)}, bf16[2048,800]{1,0:T(8,128)(2,1)}) fusion(f32[2048,800]{1,0:T(8,128)} %fusion.54, f32[2048,800]{1,0:T(8,128)} %fusion.53, bf16[2048,2560]{1,0:T(8,128)(2,1)} %bitcast.97, bf16[2560,800]{1,0:T(8,128)(2,1)S(1)} %bitcast.105), kind=kOutput, calls=%fused_computation.1 | convolution fusion | flops 8413184000 | bytes 37519360 | tf_op jit(solution)/shard_map/dot_general | solution.py:1131
  437.9 16.1 %shard_map.311 = (bf16[4,320,800]{2,1,0:T(8,128)(2,1)}, bf16[4,320,800]{2,1,0:T(8,128)(2,1)}) custom-call(bf16[2048,2560]{1,0:T(8,128)(2,1)} %bitcast.120, bf16[2048,800]{1,0:T(8,128)(2,1)} %get-tuple-element.141.right_ref.refs_0_), custom_call_target="tpu_custom_call" | custom-call | flops 1 | bytes 1 | tf_op jit(solution)/shard_map/pallas_call | solution.py:402
  455.0 16.2 %shard_map.312 = (bf16[4,320,800]{2,1,0:T(8,128)(2,1)}, bf16[4,320,800]{2,1,0:T(8,128)(2,1)}) custom-call(bf16[2048,2560]{1,0:T(8,128)(2,1)} %bitcast.98, bf16[2048,800]{1,0:T(8,128)(2,1)} %get-tuple-element.131.right_ref.refs_0_), custom_call_target="tpu_custom_call" | custom-call | flops 1 | bytes 1 | tf_op jit(solution)/shard_map/pallas_call | solution.py:402
  471.1 33.9 %shard_map.313 = bf16[4,256,2560]{2,1,0:T(8,128)(2,1)} custom-call(bf16[2048,800]{1,0:T(8,128)(2,1)} %get-tuple-element.131.right_ref.refs_0_, bf16[2560,800]{1,0:T(8,128)(2,1)} %bitcast.104, bf16[2048,800]{1,0:T(8,128)(2,1)} %get-tuple-element.132.refs_2_.right_ref, bf16[2560,800]{1,0:T(8,128)(2,1)} %bitcast.106), custom_call_target="tpu_custom_call" | custom-call | flops 1 | bytes 1 | tf_op jit(solution)/shard_map/pallas_call | solution.py:356
  505.7 4.1 constant_dynamic-slice_fusion.5
  514.2 16.1 %shard_map.314 = (bf16[4,320,800]{2,1,0:T(8,128)(2,1)}, bf16[4,320,800]{2,1,0:T(8,128)(2,1)}) custom-call(bf16[2048,2560]{1,0:T(8,128)(2,1)} %bitcast.99, bf16[2048,800]{1,0:T(8,128)(2,1)} %get-tuple-element.132.refs_2_.right_ref), custom_call_target="tpu_custom_call" | custom-call | flops 1 | bytes 1 | tf_op jit(solution)/shard_map/pallas_call | solution.py:402
  530.3 15.9 %shard_map.315 = bf16[2048,2560]{1,0:T(8,128)(2,1)} custom-call(bf16[2048,800]{1,0:T(8,128)(2,1)} %get-tuple-element.141.right_ref.refs_0_, bf16[2560,800]{1,0:T(8,128)(2,1)} %bitcast.102), custom_call_target="tpu_custom_call" | custom-call | flops 1 | bytes 1 | tf_op jit(solution)/shard_map/pallas_call | solution.py:301
  546.2 4.3 add_convert_fusion.2
  550.5 18.5 %collective-permute-done.11 = bf16[1,1,256,2560]{3,2,1,0:T(8,128)(2,1)} collective-permute-done((bf16[1,1,256,2560]{3,2,1,0:T(8,128)(2,1)}, bf16[1,1,256,2560]{3,2,1,0:T(8,128)(2,1)}, u32[]{:S(2)}, u32[]{:S(2)}) %collective-permute-start.11) | collective-permute-done | bytes 1310752 | tf_op jit(solution)/shard_map/ppermute | solution.py:227
  570.4 3.1 add_bitcast_fusion
  579.8 3.0 add_convert_fusion.1
  587.0 3.5 convolution_convert_fusion.3.d_mixed_ref
  593.1 20.9 %shard_map.316 = (bf16[512,2560]{1,0:T(8,128)(2,1)S(1)}, bf16[512,2560]{1,0:T(8,128)(2,1)S(1)}, f32[512,128]{1,0:T(8,128)S(1)}) custom-call(bf16[512,2560]{1,0:T(8,128)(2,1)S(1)} %copy-done.12, bf16[512,2560]{1,0:T(8,128)(2,1)S(1)} %copy-done.2, bf16[512,1280]{1,0:T(8,128)(2,1)S(1)} %convolution_convert_fusion.3.d_mixed_ref, ...), custom_call_target="tpu_custom_call" | custom-call | flops 1 | bytes 1 | tf_op jit(solution)/shard_map/pallas_call | solution.py:195
  614.1 3.9 shard_map.317
  619.5 4.7 shard_map.318
  625.2 3.6 copy-done.55
  631.0 5.8 collective-permute-done.14
  640.7 3.0 add_convert_fusion.4
  645.7 3.9 add_convert_fusion
  653.3 6.5 fusion.4
  660.8 4.5 convolution_convert_fusion
  665.3 182.6 %shard_map.319 = (f32[80,1056]{1,0:T(8,128)}, f32[8,128]{1,0:T(8,128)}, f32[48,1920]{1,0:T(8,128)}, f32[16,2560]{1,0:T(8,128)}, f32[160,1280]{1,0:T(8,128)}, /*i...) custom-call(f32[8,128]{1,0:T(8,128)} %copy-done.33, bf16[2,2,2,2,2,80,1056]{6,5,4,3,2,1,0:T(8,128)(2,1)} %bitcast.116, ...), custom_call_target="tpu_custom_call" | custom-call | tf_op jit(solution)/shard_map/pallas_call | solution.py:973
  862.4 5.8 fusion.6
  (346 shorter events, 110.5 us)
Async XLA Ops:
  7.2 861.0 %reduce-scatter.2.cloned.1.call-start = ((), (), s32[]{:S(2)}) async-start(), calls=%async_computation.1 | async-start | bytes 11796480 | tf_op jit(solution)/shard_map/reduce_scatter | solution.py:1182
  14.4 129.3 %copy-start.38 = (bf16[256,2560]{1,0:T(8,128)(2,1)S(1)}, bf16[256,2560]{1,0:T(8,128)(2,1)}, u32[]{:S(2)}) copy-start(bf16[256,2560]{1,0:T(8,128)(2,1)} %param.17) | copy-start | bytes 3932164
  141.1 160.9 %collective-permute-start.1 = (bf16[4,160,800]{2,1,0:T(8,128)(2,1)}, bf16[4,160,800]{2,1,0:T(8,128)(2,1)}, u32[]{:S(2)}, u32[]{:S(2)}) collective-permute-start(bf16[4,160,800]{2,1,0:T(8,128)(2,1)} %get-tuple-element.124.refs_0_), channel_id=1, source_target_pairs={{0,16},{16,0},{1,17},{17,1},{2,18},{18,2},{3,19},{19,3},{4,20},{20... | collective-permute-start | bytes 3072008 | tf_op jit(solution)/shard_map/ppermute | solution.py:223
  142.4 159.6 %collective-permute-start.2 = (bf16[4,160,800]{2,1,0:T(8,128)(2,1)}, bf16[4,160,800]{2,1,0:T(8,128)(2,1)}, u32[]{:S(2)}, u32[]{:S(2)}) collective-permute-start(bf16[4,160,800]{2,1,0:T(8,128)(2,1)} %get-tuple-element.124.refs_0_), channel_id=1, source_target_pairs={{0,4},{4,0},{1,5},{5,1},{2,6},{6,2},{3,7},{7,3},{8,12},{12,8},{9,1... | collective-permute-start | bytes 3072008 | tf_op jit(solution)/shard_map/ppermute | solution.py:223
  155.9 6.7 collective-permute-start
  155.9 146.0 %collective-permute-start.3 = (bf16[4,160,800]{2,1,0:T(8,128)(2,1)}, bf16[4,160,800]{2,1,0:T(8,128)(2,1)}, u32[]{:S(2)}, u32[]{:S(2)}) collective-permute-start(bf16[4,160,800]{2,1,0:T(8,128)(2,1)} %get-tuple-element.113.refs_1_), channel_id=1, source_target_pairs={{0,4},{4,0},{1,5},{5,1},{2,6},{6,2},{3,7},{7,3},{8,12},{12,8},{9,1... | collective-permute-start | bytes 3072008 | tf_op jit(solution)/shard_map/ppermute | solution.py:223
  170.1 18.2 %copy-start.10 = (bf16[4,160,800]{2,1,0:T(8,128)(2,1)S(1)}, bf16[4,160,800]{2,1,0:T(8,128)(2,1)}, u32[]{:S(2)}) copy-start(bf16[4,160,800]{2,1,0:T(8,128)(2,1)} %get-tuple-element.117.piece_ref.refs_0_) | copy-start | bytes 3072004
  170.1 18.2 %copy-start.30 = (bf16[160,1280]{1,0:T(8,128)(2,1)S(1)}, bf16[160,1280]{1,0:T(8,128)(2,1)}, u32[]{:S(2)}) copy-start(bf16[160,1280]{1,0:T(8,128)(2,1)} %rows_ref) | copy-start | bytes 1228804
  188.3 117.3 %copy-start.33 = (f32[8,128]{1,0:T(8,128)}, f32[8,128]{1,0:T(8,128)S(1)}, u32[]{:S(2)}) copy-start(f32[8,128]{1,0:T(8,128)S(1)} %get-tuple-element.157.peak_ref) | copy-start | bytes 12292
  308.7 8.0 collective-permute-start.4
  310.1 61.5 %collective-permute-start.6 = (bf16[4,160,800]{2,1,0:T(8,128)(2,1)}, bf16[4,160,800]{2,1,0:T(8,128)(2,1)S(1)}, u32[]{:S(2)}, u32[]{:S(2)}) collective-permute-start(bf16[4,160,800]{2,1,0:T(8,128)(2,1)} %collective-permute-done.1.refs_1_), channel_id=1, source_target_pairs={{0,4},{4,0},{1,5},{5,1},{2,6},{6,2},{3,7},{7,3},{8,12},{12,8},{9,1... | collective-permute-start | bytes 3072008 | tf_op jit(solution)/shard_map/ppermute | solution.py:223
  311.7 60.0 %collective-permute-start.5 = (bf16[4,160,800]{2,1,0:T(8,128)(2,1)S(1)}, bf16[4,160,800]{2,1,0:T(8,128)(2,1)S(1)}, u32[]{:S(2)}, u32[]{:S(2)}) collective-permute-start(bf16[4,160,800]{2,1,0:T(8,128)(2,1)S(1)} %copy-done.10), channel_id=1, source_target_pairs={{0,4},{4,0},{1,5},{5,1},{2,6},{6,2},{3,7},{7,3},{8,12},{12,8},{9,1... | collective-permute-start | bytes 3072008 | tf_op jit(solution)/shard_map/ppermute | solution.py:223
  316.8 55.9 %copy-start.5 = (bf16[16,160,800]{2,1,0:T(8,128)(2,1)}, bf16[16,160,800]{2,1,0:T(8,128)(2,1)S(1)}, u32[]{:S(2)}) copy-start(bf16[16,160,800]{2,1,0:T(8,128)(2,1)S(1)} %shard_map.307) | copy-start | bytes 12288004
  321.8 49.8 %copy-start.35 = (f32[256,2560]{1,0:T(8,128)}, f32[256,2560]{1,0:T(8,128)S(1)}, u32[]{:S(2)}) copy-start(f32[256,2560]{1,0:T(8,128)S(1)} %get-tuple-element.188) | copy-start | bytes 7864324
  321.8 49.8 %copy-start.87 = (f32[256]{0:T(256)}, f32[256]{0:T(256)S(1)}, u32[]{:S(2)}) copy-start(f32[256]{0:T(256)S(1)} %get-tuple-element.187) | copy-start | bytes 3076
  321.9 49.8 %copy-start.75 = (f32[256]{0:T(256)}, f32[256]{0:T(256)S(1)}, u32[]{:S(2)}) copy-start(f32[256]{0:T(256)S(1)} %fusion.47) | copy-start | bytes 3076
  322.2 49.5 %copy-start.24 = (bf16[4,160,800]{2,1,0:T(8,128)(2,1)S(1)}, bf16[4,160,800]{2,1,0:T(8,128)(2,1)}, u32[]{:S(2)}) copy-start(bf16[4,160,800]{2,1,0:T(8,128)(2,1)} %copy-done.23) | copy-start | bytes 3072004
  371.7 27.6 %collective-permute-start.7 = (bf16[4,160,800]{2,1,0:T(8,128)(2,1)S(1)}, bf16[4,160,800]{2,1,0:T(8,128)(2,1)S(1)}, u32[]{:S(2)}, u32[]{:S(2)}) collective-permute-start(bf16[4,160,800]{2,1,0:T(8,128)(2,1)S(1)} %copy-done.24), channel_id=1, source_target_pairs={{0,4},{4,0},{1,5},{5,1},{2,6},{6,2},{3,7},{7,3},{8,12},{12,8},{9,1... | collective-permute-start | bytes 3072008 | tf_op jit(solution)/shard_map/ppermute | solution.py:223
  390.7 26.1 %copy-start.6 = (bf16[16,160,800]{2,1,0:T(8,128)(2,1)}, bf16[16,160,800]{2,1,0:T(8,128)(2,1)S(1)}, u32[]{:S(2)}) copy-start(bf16[16,160,800]{2,1,0:T(8,128)(2,1)S(1)} %shard_map.310) | copy-start | bytes 12288004
  454.1 51.6 %collective-permute-start.8 = (bf16[4,320,800]{2,1,0:T(8,128)(2,1)}, bf16[4,320,800]{2,1,0:T(8,128)(2,1)}, u32[]{:S(2)}, u32[]{:S(2)}) collective-permute-start(bf16[4,320,800]{2,1,0:T(8,128)(2,1)} %get-tuple-element.133), channel_id=1, source_target_pairs={{0,4},{4,0},{1,5},{5,1},{2,6},{6,2},{3,7},{7,3},{8,12},{12,8},{9,1... | collective-permute-start | bytes 6144008 | tf_op jit(solution)/shard_map/ppermute | solution.py:223
  509.8 40.7 %collective-permute-start.10 = (bf16[1,1,256,2560]{3,2,1,0:T(8,128)(2,1)}, bf16[1,1,256,2560]{3,2,1,0:T(8,128)(2,1)}, u32[]{:S(2)}, u32[]{:S(2)}) collective-permute-start(bf16[1,1,256,2560]{3,2,1,0:T(8,128)(2,1)} %get-tuple-element.194), channel_id=1, source_target_pairs={{0,8},{8,0},{1,9},{9,1},{2,10},{10,2},{3,11},{11,3},{4,12},{12,4},... | collective-permute-start | bytes 3932168 | tf_op jit(solution)/shard_map/ppermute | solution.py:223
  511.4 57.6 %collective-permute-start.11 = (bf16[1,1,256,2560]{3,2,1,0:T(8,128)(2,1)}, bf16[1,1,256,2560]{3,2,1,0:T(8,128)(2,1)}, u32[]{:S(2)}, u32[]{:S(2)}) collective-permute-start(bf16[1,1,256,2560]{3,2,1,0:T(8,128)(2,1)} %get-tuple-element.193), channel_id=1, source_target_pairs={{0,10},{2,8},{8,2},{10,0},{1,11},{3,9},{9,3},{11,1},{4,14},{6,12},... | collective-permute-start | bytes 3932168 | tf_op jit(solution)/shard_map/ppermute | solution.py:227
  512.9 57.5 %collective-permute-start.9 = (bf16[1,1,256,2560]{3,2,1,0:T(8,128)(2,1)}, bf16[1,1,256,2560]{3,2,1,0:T(8,128)(2,1)}, u32[]{:S(2)}, u32[]{:S(2)}) collective-permute-start(bf16[1,1,256,2560]{3,2,1,0:T(8,128)(2,1)} %get-tuple-element.192), channel_id=1, source_target_pairs={{0,2},{2,0},{1,3},{3,1},{4,6},{6,4},{5,7},{7,5},{8,10},{10,8},{9,1... | collective-permute-start | bytes 3932168 | tf_op jit(solution)/shard_map/ppermute | solution.py:223
  513.3 60.2 %collective-permute-start.12 = (bf16[4,320,800]{2,1,0:T(8,128)(2,1)}, bf16[4,320,800]{2,1,0:T(8,128)(2,1)}, u32[]{:S(2)}, u32[]{:S(2)}) collective-permute-start(bf16[4,320,800]{2,1,0:T(8,128)(2,1)} %get-tuple-element.138), channel_id=1, source_target_pairs={{0,4},{4,0},{1,5},{5,1},{2,6},{6,2},{3,7},{7,3},{8,12},{12,8},{9,1... | collective-permute-start | bytes 6144008 | tf_op jit(solution)/shard_map/ppermute | solution.py:223
  550.5 23.0 %copy-start.36 = (f32[256,2560]{1,0:T(8,128)S(1)}, f32[256,2560]{1,0:T(8,128)}, u32[]{:S(2)}) copy-start(f32[256,2560]{1,0:T(8,128)} %copy-done.35) | copy-start | bytes 7864324
  550.5 23.1 %copy-start.64 = (f32[2560]{0:T(1024)S(1)}, f32[2560]{0:T(1024)}, u32[]{:S(2)}) copy-start(f32[2560]{0:T(1024)} %reshape.320) | copy-start | bytes 30724
  550.5 23.1 %copy-start.76 = (f32[256]{0:T(256)S(1)}, f32[256]{0:T(256)}, u32[]{:S(2)}) copy-start(f32[256]{0:T(256)} %copy-done.75) | copy-start | bytes 3076
  577.9 7.6 collective-permute-start.13
  577.9 58.9 %collective-permute-start.15 = (bf16[4,320,800]{2,1,0:T(8,128)(2,1)}, bf16[4,320,800]{2,1,0:T(8,128)(2,1)}, u32[]{:S(2)}, u32[]{:S(2)}) collective-permute-start(bf16[4,320,800]{2,1,0:T(8,128)(2,1)} %get-tuple-element.153), channel_id=1, source_target_pairs={{0,4},{4,0},{1,5},{5,1},{2,6},{6,2},{3,7},{7,3},{8,12},{12,8},{9,1... | collective-permute-start | bytes 6144008 | tf_op jit(solution)/shard_map/ppermute | solution.py:223
  584.0 52.9 %collective-permute-start.14 = (bf16[1,2,2,160,800]{4,3,2,1,0:T(8,128)(2,1)S(1)}, bf16[1,2,2,160,800]{4,3,2,1,0:T(8,128)(2,1)}, u32[]{:S(2)}, u32[]{:S(2)}) collective-permute-start(bf16[1,2,2,160,800]{4,3,2,1,0:T(8,128)(2,1)S(1)} %get-tuple-element.198), channel_id=1, source_target_pairs={{0,16},{16,0},{1,17},{17,1},{2,18},{18,2},{3,19},{19,3},{4,20},{20... | collective-permute-start | bytes 3072008 | tf_op jit(solution)/shard_map/ppermute | solution.py:223
  593.1 20.9 %copy-start.9 = (bf16[512,768]{1,0:T(8,128)(2,1)S(1)}, bf16[512,768]{1,0:T(8,128)(2,1)}, u32[]{:S(2)}) copy-start(bf16[512,768]{1,0:T(8,128)(2,1)} %copy-done.8) | copy-start | bytes 2359300
  639.5 10.1 %collective-permute-start.16 = (f32[256,1152]{1,0:T(8,128)}, f32[256,1152]{1,0:T(8,128)}, u32[]{:S(2)}, u32[]{:S(2)}) collective-permute-start(f32[256,1152]{1,0:T(8,128)} %constant_dynamic-slice_fusion), channel_id=1, source_target_pairs={{0,1},{1,0},{2,3},{3,2},{4,5},{5,4},{6,7},{7,6},{8,9},{9,8},{10,11... | collective-permute-start | bytes 3538952 | tf_op jit(solution)/shard_map/ppermute | solution.py:223
  (84 other events, 335.1 us)
Sparse Core Ops, SparseCore 0:
  578.0 104.1 reduce-scatter.1

commit v6 on v5

--- a/solution.py
+++ b/solution.py
@@ -865,7 +865,8 @@
     out_ref,
     down_ref,
     gate_ref,
-    up_ref,
+    gate_got,
+    up_refs,
     small_sum,
     gains_sum,
     q_sum,
@@ -897,6 +898,7 @@
         part = out_ref.at[(slice(None),) * stages + (rows,)]
         outs.append(Reduction(sender, part, fsdp, order, buffers(stages), out_sum.at[rows]))
     over = buffers(2)
+    gate_sum, up_sum = buffers(2)
     peaks = buffers(stages)
     me = place_of(*pair)
     row = lax.axis_index(fsdp[0])
@@ -925,9 +927,11 @@
     peak_sent = send_peaks(0)
     crossing = sender.start(down_ref.at[1 - row], over[0], (fsdp[0],))
     outs[1].begin()
-    columns = send_columns(1, gate_ref)
+    gate_sum[...] = (gate_ref[...].astype(f32) + gate_got[...].astype(f32)).astype(bf16)
+    columns = send_columns(1, gate_sum)
     small.end()
     gains.end()
+    up_sum[...] = sum(ref[...].astype(f32) for ref in up_refs).astype(bf16)
     peak_sent = next_peaks(0, peak_sent)
     for part in (q, kv, outs[0]):
         part.end()
@@ -937,13 +941,13 @@
         return send_columns(which, buffer)
 
     columns += crossed(0, down_ref, over[0])
-    crossing = sender.start(up_ref.at[1 - row], over[1], (fsdp[0],))
+    crossing = sender.start(up_sum.at[1 - row], over[1], (fsdp[0],))
     for stage in range(1, stages):
         peak_sent = next_peaks(stage, peak_sent)
         for part in (outs[1], small, gains, q, kv, outs[0]):
             part.end()
         if stage == 1:
-            columns += crossed(2, up_ref, over[1])
+            columns += crossed(2, up_sum, over[1])
     for reduction in (q, kv, outs[0], small, gains, outs[1]):
         reduction.finish()
     for copy in columns:
@@ -966,25 +970,26 @@
         + buffers(q, stages)
         + buffers(kv, stages)
         + [buf for rows in halves_of(out.shape[-2]) for buf in buffers(out, stages, rows.size)]
-        + [pltpu.VMEM(gate.shape, bf16)] * 2
+        + [pltpu.VMEM(gate[0].shape, bf16)] * 3
+        + [pltpu.VMEM(down.shape, bf16)]
         + [pltpu.VMEM(peak.shape, f32)] * stages
     )
     copies = 2 * (stages + 1) + 4 * stages + 2 + 9 + stages
     return pl.pallas_call(
-        functools.partial(last_kernel, fsdp, pair),
+        lambda *refs: last_kernel(fsdp, pair, *refs[:9], refs[9 : 9 + len(up)], *refs[9 + len(up) :]),
         out_shape=tuple(jax.ShapeDtypeStruct(x.shape[-2:], f32) for x in (small, gains, q, kv, out))
         + (
-            jax.ShapeDtypeStruct((3,) + gate.shape, bf16),
+            jax.ShapeDtypeStruct((3,) + gate[0].shape, bf16),
             jax.ShapeDtypeStruct(peak.shape, f32),
         ),
-        in_specs=[vmem] * 9,
+        in_specs=[vmem] * (9 + len(up)),
         out_specs=(vmem,) * 7,
         scratch_shapes=scratch
         + [pltpu.SemaphoreType.DMA((copies,)), pltpu.SemaphoreType.DMA((copies,))],
         compiler_params=pltpu.CompilerParams(
             collective_id=2, has_side_effects=True, vmem_limit_bytes=60 << 20
         ),
-    )(peak, small, gains, q, kv, out, down, gate, up)
+    )(peak, small, gains, q, kv, out, down, *gate, *up)
 
 
 def shards(
@@ -1223,10 +1228,13 @@
     input_grad = d_mid + d_x_norm
 
     rows_here = width // count
+    block = (4, rows_here, gate_parts[0].shape[-1])
+    if len(spread) > 2:
+        up_parts = (inner(added(up_parts)),)
     ffn_held = [
-        down_held.reshape(2, 4, rows_here, -1),
-        added(gate_parts).reshape(4, rows_here, -1),
-        inner(added(up_parts)).reshape(2, 4, rows_here, -1),
+        down_held.reshape((2,) + block),
+        tuple(part.reshape(block) for part in gate_parts),
+        tuple(part.reshape((2,) + block) for part in up_parts),
     ]
     gain_grads = rows_of(
         *(grad.reshape(devices, -1) for grad in (in_grad, post_grad, q_gain_grad, kv_gain_grad))

time: 889 us -> 888 us (level)
    unnamed x203 -> x199, local copies, waits for them, and re-layouts: 31.9 us -> 31.8 us
  transfers between devices with their start and end apart: 18 -> 18, of which waited for: 5 -> 5; matrix products, arithmetic and copies ran while one was open for 11% -> 10% of each run, Pallas kernels for 55% -> 56%
where the time goes in v6:
time: 888 us; the launch traced here: 879 us
  Pallas kernels  634 us (71%)
  matrix products  82.7 us (9%)
  local copies, waits for them, and re-layouts  49.6 us (6%)
  other arithmetic  46.4 us (5%)
  waiting for transfers between devices  34.9 us (4%)
  between operations  16.5 us (2%)
  starting transfers between devices  14.7 us (2%)
    pallas_call x1, Pallas kernels, last_scatter(): pl.pallas_call(lambda *refs: last_kernel(fsdp, pair, *refs[:9], refs[9:9...  188 us
    pallas_call x1, Pallas kernels, first_gather(): pl.pallas_call(functools.partial(first_kernel, squares, pair, spread), ou...  126 us
    pallas_call x1, Pallas kernels, second_gather(): pl.pallas_call(functools.partial(second_kernel, squares, pair, over), out...  114 us
    pallas_call x1, Pallas kernels, tokens_of_chips(): pl.pallas_call(functools.partial(tokens_kernel, pair), out_shape=jax.Shap...  49.5 us
    pallas_call x3, Pallas kernels, grad_halves(): pl.pallas_call(functools.partial(grad_kernel, axis), grid=(width // tile,...  48.4 us
    pallas_call x1, Pallas kernels, core_features(): pl.pallas_call(core_features_kernel, grid=(4,), out_shape=jax.ShapeDtypeS...  33.6 us
    unnamed x199, local copies, waits for them, and re-layouts  31.8 us
    dot_general x1, matrix products, shards(): up_value = jnp.dot(mid_all, up_full, preferred_element_type=f32)  21.1 us
  transfers between devices with their start and end apart: 18, of which 5 were waited for; matrix products, arithmetic and copies ran while one was open for 10% of the time, Pallas kernels for 56%

profile of v6, /device:TPU:0, one launch (start us, length us, event | category | flops | bytes accessed | tf_op | source)
XLA Modules:
  0.0 879.3 jit_solution(8206160248735302803)
XLA Ops:
  14.4 125.6 %shard_map.304 = (bf16[4,4,2,80,1056]{4,3,2,1,0:T(8,128)(2,1)}, bf16[4,4,2,8,128]{4,3,2,1,0:T(8,128)(2,1)S(1)}, bf16[4,4,48,2560]{3,2,1,0:T(8,128)(2,1)}, bf16[4...) custom-call(bf16[80,1056]{1,0:T(8,128)(2,1)S(1)} %pad_maximum_fusion, ...), custom_call_target="tpu_custom_call" | custom-call | tf_op jit(solution)/shard_map/pallas_call | solution.py:597
  144.0 4.6 fusion.14
  170.4 16.7 %shard_map.305 = (bf16[512,1280]{1,0:T(8,128)(2,1)S(1)}, bf16[512,2560]{1,0:T(8,128)(2,1)S(1)}, f32[10,2,512]{2,1,0:T(2,128)S(1)}, f32[8,128]{1,0:T(8,128)S(1)}) custom-call(f32[512,2560]{1,0:T(8,128)S(1)} %fusion.51.q_ref, bf16[512,2560]{1,0:T(8,128)(2,1)S(1)} %convolution_convert_fusion.1.kv_ref, bf16[512,128]{1,0:T(8,128)(2,1)S(1)} %pad_maximum_fusion.2.rot_ref, ...), custom_call_target="tpu_custom_call" | custom-call | flops 1 | bytes 1 | tf_op jit(solution)/shard_map/pallas_call | solution.py:122
  188.5 113.6 %shard_map.306 = (bf16[4,4,160,1280]{3,2,1,0:T(8,128)(2,1)S(1)}, bf16[4,2,256,2560]{3,2,1,0:T(8,128)(2,1)}, bf16[4,160,800]{2,1,0:T(8,128)(2,1)S(1)}) custom-call(bf16[160,1280]{1,0:T(8,128)(2,1)S(1)} %copy-done.30, bf16[256,2560]{1,0:T(8,128)(2,1)S(1)} %fusion.5.value_ref, bf16[4,160,800]{2,1,0:T(8,128)(2,1)S(1)} %copy-done.10), custom_call_target="tpu_custom_call" | custom-call | flops 1 | bytes 1 | tf_op jit(solution)/shard_map/pallas_call | solution.py:692
  302.2 3.6 fusion.52
  322.4 49.5 %shard_map.308 = bf16[4,2,256,2560]{3,2,1,0:T(8,128)(2,1)S(1)} custom-call(bf16[256,2560]{1,0:T(8,128)(2,1)S(1)} %multiply_convert_fusion.4.value_ref), custom_call_target="tpu_custom_call" | custom-call | flops 1 | bytes 1 | tf_op jit(solution)/shard_map/pallas_call | solution.py:786
  372.8 3.1 copy-done
  375.9 13.1 %fusion.54 = f32[2048,800]{1,0:T(8,128)} fusion(bf16[2048,2560]{1,0:T(8,128)(2,1)S(1)} %bitcast.98, bf16[2560,800]{1,0:T(8,128)(2,1)S(1)} %bitcast.105), kind=kOutput, calls=%fused_computation.161 | convolution fusion | flops 8388608000 | bytes 21135360 | tf_op jit(solution)/shard_map/dot_general | solution.py:1135
  390.9 8.6 collective-permute-done.7.refs_3_
  400.6 16.5 %fusion.53 = f32[2048,800]{1,0:T(8,128)} fusion(bf16[2048,2560]{1,0:T(8,128)(2,1)} %bitcast.121, bf16[2560,800]{1,0:T(8,128)(2,1)S(1)} %bitcast.103), kind=kOutput, calls=%fused_computation.160 | convolution fusion | flops 8388608000 | bytes 21135360 | tf_op jit(solution)/shard_map/dot_general | solution.py:1142
  417.1 21.1 %multiply_convert_fusion = (bf16[2048,800]{1,0:T(8,128)(2,1)}, bf16[2048,800]{1,0:T(8,128)(2,1)}, bf16[2048,800]{1,0:T(8,128)(2,1)}) fusion(f32[2048,800]{1,0:T(8,128)} %fusion.54, f32[2048,800]{1,0:T(8,128)} %fusion.53, bf16[2048,2560]{1,0:T(8,128)(2,1)} %bitcast.99, bf16[2560,800]{1,0:T(8,128)(2,1)S(1)} %bitcast.107), kind=kOutput, calls=%fused_computation.1 | convolution fusion | flops 8413184000 | bytes 37519360 | tf_op jit(solution)/shard_map/dot_general | solution.py:1136
  438.2 16.1 %shard_map.311 = (bf16[4,320,800]{2,1,0:T(8,128)(2,1)}, bf16[4,320,800]{2,1,0:T(8,128)(2,1)}) custom-call(bf16[2048,2560]{1,0:T(8,128)(2,1)} %bitcast.122, bf16[2048,800]{1,0:T(8,128)(2,1)} %get-tuple-element.141.right_ref.refs_0_), custom_call_target="tpu_custom_call" | custom-call | flops 1 | bytes 1 | tf_op jit(solution)/shard_map/pallas_call | solution.py:402
  455.2 16.1 %shard_map.312 = (bf16[4,320,800]{2,1,0:T(8,128)(2,1)}, bf16[4,320,800]{2,1,0:T(8,128)(2,1)}) custom-call(bf16[2048,2560]{1,0:T(8,128)(2,1)} %bitcast.100, bf16[2048,800]{1,0:T(8,128)(2,1)} %get-tuple-element.131.right_ref.refs_0_), custom_call_target="tpu_custom_call" | custom-call | flops 1 | bytes 1 | tf_op jit(solution)/shard_map/pallas_call | solution.py:402
  471.3 33.6 %shard_map.313 = bf16[4,256,2560]{2,1,0:T(8,128)(2,1)} custom-call(bf16[2048,800]{1,0:T(8,128)(2,1)} %get-tuple-element.131.right_ref.refs_0_, bf16[2560,800]{1,0:T(8,128)(2,1)} %bitcast.106, bf16[2048,800]{1,0:T(8,128)(2,1)} %get-tuple-element.132.refs_2_.right_ref, bf16[2560,800]{1,0:T(8,128)(2,1)} %bitcast.108), custom_call_target="tpu_custom_call" | custom-call | flops 1 | bytes 1 | tf_op jit(solution)/shard_map/pallas_call | solution.py:356
  506.0 4.1 constant_dynamic-slice_fusion.5
  514.4 16.1 %shard_map.314 = (bf16[4,320,800]{2,1,0:T(8,128)(2,1)}, bf16[4,320,800]{2,1,0:T(8,128)(2,1)}) custom-call(bf16[2048,2560]{1,0:T(8,128)(2,1)} %bitcast.101, bf16[2048,800]{1,0:T(8,128)(2,1)} %get-tuple-element.132.refs_2_.right_ref), custom_call_target="tpu_custom_call" | custom-call | flops 1 | bytes 1 | tf_op jit(solution)/shard_map/pallas_call | solution.py:402
  530.6 16.2 %shard_map.315 = bf16[2048,2560]{1,0:T(8,128)(2,1)} custom-call(bf16[2048,800]{1,0:T(8,128)(2,1)} %get-tuple-element.141.right_ref.refs_0_, bf16[2560,800]{1,0:T(8,128)(2,1)} %bitcast.104), custom_call_target="tpu_custom_call" | custom-call | flops 1 | bytes 1 | tf_op jit(solution)/shard_map/pallas_call | solution.py:301
  546.8 4.3 add_convert_fusion.1
  551.1 18.0 %collective-permute-done.11 = bf16[1,1,256,2560]{3,2,1,0:T(8,128)(2,1)} collective-permute-done((bf16[1,1,256,2560]{3,2,1,0:T(8,128)(2,1)}, bf16[1,1,256,2560]{3,2,1,0:T(8,128)(2,1)}, u32[]{:S(2)}, u32[]{:S(2)}) %collective-permute-start.11) | collective-permute-done | bytes 1310752 | tf_op jit(solution)/shard_map/ppermute | solution.py:227
  570.4 3.1 add_bitcast_fusion
  579.8 3.0 add_convert_fusion
  586.9 3.5 convolution_convert_fusion.3.d_mixed_ref
  593.0 20.9 %shard_map.316 = (bf16[512,2560]{1,0:T(8,128)(2,1)S(1)}, bf16[512,2560]{1,0:T(8,128)(2,1)S(1)}, f32[512,128]{1,0:T(8,128)S(1)}) custom-call(bf16[512,2560]{1,0:T(8,128)(2,1)S(1)} %copy-done.12, bf16[512,2560]{1,0:T(8,128)(2,1)S(1)} %copy-done.2, bf16[512,1280]{1,0:T(8,128)(2,1)S(1)} %convolution_convert_fusion.3.d_mixed_ref, ...), custom_call_target="tpu_custom_call" | custom-call | flops 1 | bytes 1 | tf_op jit(solution)/shard_map/pallas_call | solution.py:195
  614.0 3.9 shard_map.317
  619.4 4.7 shard_map.318
  625.1 3.6 copy-done.54
  631.0 5.9 collective-permute-done.14
  640.3 3.0 convolution_convert_fusion.2
  646.9 6.5 fusion.4
  654.4 4.5 convolution_convert_fusion
  659.0 187.8 %shard_map.319 = (f32[80,1056]{1,0:T(8,128)}, f32[8,128]{1,0:T(8,128)}, f32[48,1920]{1,0:T(8,128)}, f32[16,2560]{1,0:T(8,128)}, f32[160,1280]{1,0:T(8,128)}, /*i...) custom-call(f32[8,128]{1,0:T(8,128)} %copy-done.33, bf16[2,2,2,2,2,80,1056]{6,5,4,3,2,1,0:T(8,128)(2,1)} %bitcast.118, ...), custom_call_target="tpu_custom_call" | custom-call | tf_op jit(solution)/shard_map/pallas_call | solution.py:978
  861.3 5.8 fusion.6
  (340 shorter events, 105.8 us)
Async XLA Ops:
  7.2 859.9 %reduce-scatter.2.cloned.1.call-start = ((), (), s32[]{:S(2)}) async-start(), calls=%async_computation.1 | async-start | bytes 11796480 | tf_op jit(solution)/shard_map/reduce_scatter | solution.py:1187
  14.4 129.2 %copy-start.38 = (bf16[256,2560]{1,0:T(8,128)(2,1)S(1)}, bf16[256,2560]{1,0:T(8,128)(2,1)}, u32[]{:S(2)}) copy-start(bf16[256,2560]{1,0:T(8,128)(2,1)} %param.17) | copy-start | bytes 3932164
  141.0 161.1 %collective-permute-start.1 = (bf16[4,160,800]{2,1,0:T(8,128)(2,1)}, bf16[4,160,800]{2,1,0:T(8,128)(2,1)}, u32[]{:S(2)}, u32[]{:S(2)}) collective-permute-start(bf16[4,160,800]{2,1,0:T(8,128)(2,1)} %get-tuple-element.124.refs_0_), channel_id=1, source_target_pairs={{0,16},{16,0},{1,17},{17,1},{2,18},{18,2},{3,19},{19,3},{4,20},{20... | collective-permute-start | bytes 3072008 | tf_op jit(solution)/shard_map/ppermute | solution.py:223
  142.3 159.8 %collective-permute-start.2 = (bf16[4,160,800]{2,1,0:T(8,128)(2,1)}, bf16[4,160,800]{2,1,0:T(8,128)(2,1)}, u32[]{:S(2)}, u32[]{:S(2)}) collective-permute-start(bf16[4,160,800]{2,1,0:T(8,128)(2,1)} %get-tuple-element.124.refs_0_), channel_id=1, source_target_pairs={{0,4},{4,0},{1,5},{5,1},{2,6},{6,2},{3,7},{7,3},{8,12},{12,8},{9,1... | collective-permute-start | bytes 3072008 | tf_op jit(solution)/shard_map/ppermute | solution.py:223
  155.9 7.0 collective-permute-start
  155.9 146.3 %collective-permute-start.3 = (bf16[4,160,800]{2,1,0:T(8,128)(2,1)}, bf16[4,160,800]{2,1,0:T(8,128)(2,1)}, u32[]{:S(2)}, u32[]{:S(2)}) collective-permute-start(bf16[4,160,800]{2,1,0:T(8,128)(2,1)} %get-tuple-element.113.refs_1_), channel_id=1, source_target_pairs={{0,4},{4,0},{1,5},{5,1},{2,6},{6,2},{3,7},{7,3},{8,12},{12,8},{9,1... | collective-permute-start | bytes 3072008 | tf_op jit(solution)/shard_map/ppermute | solution.py:223
  170.3 18.2 %copy-start.10 = (bf16[4,160,800]{2,1,0:T(8,128)(2,1)S(1)}, bf16[4,160,800]{2,1,0:T(8,128)(2,1)}, u32[]{:S(2)}) copy-start(bf16[4,160,800]{2,1,0:T(8,128)(2,1)} %get-tuple-element.117.piece_ref.refs_0_) | copy-start | bytes 3072004
  170.3 18.2 %copy-start.30 = (bf16[160,1280]{1,0:T(8,128)(2,1)S(1)}, bf16[160,1280]{1,0:T(8,128)(2,1)}, u32[]{:S(2)}) copy-start(bf16[160,1280]{1,0:T(8,128)(2,1)} %rows_ref) | copy-start | bytes 1228804
  188.5 117.3 %copy-start.33 = (f32[8,128]{1,0:T(8,128)}, f32[8,128]{1,0:T(8,128)S(1)}, u32[]{:S(2)}) copy-start(f32[8,128]{1,0:T(8,128)S(1)} %get-tuple-element.157.refs_0_) | copy-start | bytes 12292
  309.0 8.0 collective-permute-start.4
  310.4 61.5 %collective-permute-start.6 = (bf16[4,160,800]{2,1,0:T(8,128)(2,1)}, bf16[4,160,800]{2,1,0:T(8,128)(2,1)S(1)}, u32[]{:S(2)}, u32[]{:S(2)}) collective-permute-start(bf16[4,160,800]{2,1,0:T(8,128)(2,1)} %collective-permute-done.1.refs_1_), channel_id=1, source_target_pairs={{0,4},{4,0},{1,5},{5,1},{2,6},{6,2},{3,7},{7,3},{8,12},{12,8},{9,1... | collective-permute-start | bytes 3072008 | tf_op jit(solution)/shard_map/ppermute | solution.py:223
  311.9 60.0 %collective-permute-start.5 = (bf16[4,160,800]{2,1,0:T(8,128)(2,1)S(1)}, bf16[4,160,800]{2,1,0:T(8,128)(2,1)S(1)}, u32[]{:S(2)}, u32[]{:S(2)}) collective-permute-start(bf16[4,160,800]{2,1,0:T(8,128)(2,1)S(1)} %copy-done.10), channel_id=1, source_target_pairs={{0,4},{4,0},{1,5},{5,1},{2,6},{6,2},{3,7},{7,3},{8,12},{12,8},{9,1... | collective-permute-start | bytes 3072008 | tf_op jit(solution)/shard_map/ppermute | solution.py:223
  317.0 55.9 %copy-start.5 = (bf16[16,160,800]{2,1,0:T(8,128)(2,1)}, bf16[16,160,800]{2,1,0:T(8,128)(2,1)S(1)}, u32[]{:S(2)}) copy-start(bf16[16,160,800]{2,1,0:T(8,128)(2,1)S(1)} %shard_map.307) | copy-start | bytes 12288004
  322.1 49.8 %copy-start.35 = (f32[256,2560]{1,0:T(8,128)}, f32[256,2560]{1,0:T(8,128)S(1)}, u32[]{:S(2)}) copy-start(f32[256,2560]{1,0:T(8,128)S(1)} %get-tuple-element.188) | copy-start | bytes 7864324
  322.1 49.8 %copy-start.85 = (f32[256]{0:T(256)}, f32[256]{0:T(256)S(1)}, u32[]{:S(2)}) copy-start(f32[256]{0:T(256)S(1)} %get-tuple-element.187) | copy-start | bytes 3076
  322.1 49.8 %copy-start.73 = (f32[256]{0:T(256)}, f32[256]{0:T(256)S(1)}, u32[]{:S(2)}) copy-start(f32[256]{0:T(256)S(1)} %fusion.47) | copy-start | bytes 3076
  322.4 49.5 %copy-start.24 = (bf16[4,160,800]{2,1,0:T(8,128)(2,1)S(1)}, bf16[4,160,800]{2,1,0:T(8,128)(2,1)}, u32[]{:S(2)}) copy-start(bf16[4,160,800]{2,1,0:T(8,128)(2,1)} %copy-done.23) | copy-start | bytes 3072004
  372.0 27.6 %collective-permute-start.7 = (bf16[4,160,800]{2,1,0:T(8,128)(2,1)S(1)}, bf16[4,160,800]{2,1,0:T(8,128)(2,1)S(1)}, u32[]{:S(2)}, u32[]{:S(2)}) collective-permute-start(bf16[4,160,800]{2,1,0:T(8,128)(2,1)S(1)} %copy-done.24), channel_id=1, source_target_pairs={{0,4},{4,0},{1,5},{5,1},{2,6},{6,2},{3,7},{7,3},{8,12},{12,8},{9,1... | collective-permute-start | bytes 3072008 | tf_op jit(solution)/shard_map/ppermute | solution.py:223
  390.9 26.1 %copy-start.6 = (bf16[16,160,800]{2,1,0:T(8,128)(2,1)}, bf16[16,160,800]{2,1,0:T(8,128)(2,1)S(1)}, u32[]{:S(2)}) copy-start(bf16[16,160,800]{2,1,0:T(8,128)(2,1)S(1)} %shard_map.310) | copy-start | bytes 12288004
  454.3 51.6 %collective-permute-start.8 = (bf16[4,320,800]{2,1,0:T(8,128)(2,1)}, bf16[4,320,800]{2,1,0:T(8,128)(2,1)}, u32[]{:S(2)}, u32[]{:S(2)}) collective-permute-start(bf16[4,320,800]{2,1,0:T(8,128)(2,1)} %get-tuple-element.133), channel_id=1, source_target_pairs={{0,4},{4,0},{1,5},{5,1},{2,6},{6,2},{3,7},{7,3},{8,12},{12,8},{9,1... | collective-permute-start | bytes 6144008 | tf_op jit(solution)/shard_map/ppermute | solution.py:223
  510.1 41.0 %collective-permute-start.10 = (bf16[1,1,256,2560]{3,2,1,0:T(8,128)(2,1)}, bf16[1,1,256,2560]{3,2,1,0:T(8,128)(2,1)}, u32[]{:S(2)}, u32[]{:S(2)}) collective-permute-start(bf16[1,1,256,2560]{3,2,1,0:T(8,128)(2,1)} %get-tuple-element.194), channel_id=1, source_target_pairs={{0,8},{8,0},{1,9},{9,1},{2,10},{10,2},{3,11},{11,3},{4,12},{12,4},... | collective-permute-start | bytes 3932168 | tf_op jit(solution)/shard_map/ppermute | solution.py:223
  511.7 57.4 %collective-permute-start.11 = (bf16[1,1,256,2560]{3,2,1,0:T(8,128)(2,1)}, bf16[1,1,256,2560]{3,2,1,0:T(8,128)(2,1)}, u32[]{:S(2)}, u32[]{:S(2)}) collective-permute-start(bf16[1,1,256,2560]{3,2,1,0:T(8,128)(2,1)} %get-tuple-element.193), channel_id=1, source_target_pairs={{0,10},{2,8},{8,2},{10,0},{1,11},{3,9},{9,3},{11,1},{4,14},{6,12},... | collective-permute-start | bytes 3932168 | tf_op jit(solution)/shard_map/ppermute | solution.py:227
  513.1 57.3 %collective-permute-start.9 = (bf16[1,1,256,2560]{3,2,1,0:T(8,128)(2,1)}, bf16[1,1,256,2560]{3,2,1,0:T(8,128)(2,1)}, u32[]{:S(2)}, u32[]{:S(2)}) collective-permute-start(bf16[1,1,256,2560]{3,2,1,0:T(8,128)(2,1)} %get-tuple-element.192), channel_id=1, source_target_pairs={{0,2},{2,0},{1,3},{3,1},{4,6},{6,4},{5,7},{7,5},{8,10},{10,8},{9,1... | collective-permute-start | bytes 3932168 | tf_op jit(solution)/shard_map/ppermute | solution.py:223
  513.6 60.0 %collective-permute-start.12 = (bf16[4,320,800]{2,1,0:T(8,128)(2,1)}, bf16[4,320,800]{2,1,0:T(8,128)(2,1)}, u32[]{:S(2)}, u32[]{:S(2)}) collective-permute-start(bf16[4,320,800]{2,1,0:T(8,128)(2,1)} %get-tuple-element.138), channel_id=1, source_target_pairs={{0,4},{4,0},{1,5},{5,1},{2,6},{6,2},{3,7},{7,3},{8,12},{12,8},{9,1... | collective-permute-start | bytes 6144008 | tf_op jit(solution)/shard_map/ppermute | solution.py:223
  551.1 22.5 %copy-start.36 = (f32[256,2560]{1,0:T(8,128)S(1)}, f32[256,2560]{1,0:T(8,128)}, u32[]{:S(2)}) copy-start(f32[256,2560]{1,0:T(8,128)} %copy-done.35) | copy-start | bytes 7864324
  551.1 22.5 %copy-start.62 = (f32[2560]{0:T(1024)S(1)}, f32[2560]{0:T(1024)}, u32[]{:S(2)}) copy-start(f32[2560]{0:T(1024)} %reshape.328) | copy-start | bytes 30724
  551.1 22.5 %copy-start.74 = (f32[256]{0:T(256)S(1)}, f32[256]{0:T(256)}, u32[]{:S(2)}) copy-start(f32[256]{0:T(256)} %copy-done.73) | copy-start | bytes 3076
  577.9 7.5 collective-permute-start.13
  577.9 58.9 %collective-permute-start.15 = (bf16[4,320,800]{2,1,0:T(8,128)(2,1)}, bf16[4,320,800]{2,1,0:T(8,128)(2,1)}, u32[]{:S(2)}, u32[]{:S(2)}) collective-permute-start(bf16[4,320,800]{2,1,0:T(8,128)(2,1)} %get-tuple-element.153), channel_id=1, source_target_pairs={{0,4},{4,0},{1,5},{5,1},{2,6},{6,2},{3,7},{7,3},{8,12},{12,8},{9,1... | collective-permute-start | bytes 6144008 | tf_op jit(solution)/shard_map/ppermute | solution.py:223
  584.0 52.8 %collective-permute-start.14 = (bf16[1,2,2,160,800]{4,3,2,1,0:T(8,128)(2,1)S(1)}, bf16[1,2,2,160,800]{4,3,2,1,0:T(8,128)(2,1)}, u32[]{:S(2)}, u32[]{:S(2)}) collective-permute-start(bf16[1,2,2,160,800]{4,3,2,1,0:T(8,128)(2,1)S(1)} %get-tuple-element.198), channel_id=1, source_target_pairs={{0,16},{16,0},{1,17},{17,1},{2,18},{18,2},{3,19},{19,3},{4,20},{20... | collective-permute-start | bytes 3072008 | tf_op jit(solution)/shard_map/ppermute | solution.py:223
  593.0 20.9 %copy-start.9 = (bf16[512,768]{1,0:T(8,128)(2,1)S(1)}, bf16[512,768]{1,0:T(8,128)(2,1)}, u32[]{:S(2)}) copy-start(bf16[512,768]{1,0:T(8,128)(2,1)} %copy-done.8) | copy-start | bytes 2359300
  639.5 3.8 collective-permute-start.16
  (82 other events, 324.8 us)
Sparse Core Ops, SparseCore 0:
  578.0 110.0 reduce-scatter.1

commit v7 on v6

--- a/solution.py
+++ b/solution.py
@@ -1185,7 +1185,7 @@
     down_held, gate_parts, ffn_part = early[0], early[1:3], early[3]
     d_mid_norm, post_grad = post_pull(d_mid_normed)
     ffn = lax.psum_scatter(
-        after(ffn_part, d_mid_norm), (wide, near, "c"), scatter_dimension=0, tiled=True
+        ffn_part, (wide, near, "c"), scatter_dimension=0, tiled=True
     )
     layer_out = (mid + resid_scale * ffn.astype(f32)).astype(bf16)
     d_mid = cot_float + d_mid_norm

time: 888 us -> 888 us (level)
    unnamed x199 -> x197, local copies, waits for them, and re-layouts: 31.8 us -> 31.9 us
  transfers between devices with their start and end apart: 18 -> 18, of which waited for: 5 -> 5; matrix products, arithmetic and copies ran while one was open for 10% -> 11% of each run, Pallas kernels for 56% -> 56%
where the time goes in v7:
time: 888 us; the launch traced here: 882 us
  Pallas kernels  635 us (72%)
  matrix products  82.5 us (9%)
  other arithmetic  49.9 us (6%)
  local copies, waits for them, and re-layouts  49.7 us (6%)
  waiting for transfers between devices  34.8 us (4%)
  between operations  16.4 us (2%)
  starting transfers between devices  14.2 us (2%)
    pallas_call x1, Pallas kernels, last_scatter(): pl.pallas_call(lambda *refs: last_kernel(fsdp, pair, *refs[:9], refs[9:9...  188 us
    pallas_call x1, Pallas kernels, first_gather(): pl.pallas_call(functools.partial(first_kernel, squares, pair, spread), ou...  126 us
    pallas_call x1, Pallas kernels, second_gather(): pl.pallas_call(functools.partial(second_kernel, squares, pair, over), out...  114 us
    pallas_call x1, Pallas kernels, tokens_of_chips(): pl.pallas_call(functools.partial(tokens_kernel, pair), out_shape=jax.Shap...  49.5 us
    pallas_call x3, Pallas kernels, grad_halves(): pl.pallas_call(functools.partial(grad_kernel, axis), grid=(width // tile,...  48.4 us
    pallas_call x1, Pallas kernels, core_features(): pl.pallas_call(core_features_kernel, grid=(4,), out_shape=jax.ShapeDtypeS...  33.7 us
    unnamed x197, local copies, waits for them, and re-layouts  31.9 us
    dot_general x1, matrix products, shards(): up_value = jnp.dot(mid_all, up_full, preferred_element_type=f32)  21.2 us
  transfers between devices with their start and end apart: 18, of which 5 were waited for; matrix products, arithmetic and copies ran while one was open for 11% of the time, Pallas kernels for 56%

profile of v7, /device:TPU:0, one launch (start us, length us, event | category | flops | bytes accessed | tf_op | source)
XLA Modules:
  0.0 882.4 jit_solution(1515580782221746228)
XLA Ops:
  14.4 125.6 %shard_map.304 = (bf16[4,4,2,80,1056]{4,3,2,1,0:T(8,128)(2,1)}, bf16[4,4,2,8,128]{4,3,2,1,0:T(8,128)(2,1)S(1)}, bf16[4,4,48,2560]{3,2,1,0:T(8,128)(2,1)}, bf16[4...) custom-call(bf16[80,1056]{1,0:T(8,128)(2,1)S(1)} %pad_maximum_fusion, ...), custom_call_target="tpu_custom_call" | custom-call | tf_op jit(solution)/shard_map/pallas_call | solution.py:597
  144.0 4.6 fusion.14
  170.4 16.7 %shard_map.305 = (bf16[512,1280]{1,0:T(8,128)(2,1)S(1)}, bf16[512,2560]{1,0:T(8,128)(2,1)S(1)}, f32[10,2,512]{2,1,0:T(2,128)S(1)}, f32[8,128]{1,0:T(8,128)S(1)}) custom-call(f32[512,2560]{1,0:T(8,128)S(1)} %fusion.51.q_ref, bf16[512,2560]{1,0:T(8,128)(2,1)S(1)} %convolution_convert_fusion.1.kv_ref, bf16[512,128]{1,0:T(8,128)(2,1)S(1)} %pad_maximum_fusion.2.rot_ref, ...), custom_call_target="tpu_custom_call" | custom-call | flops 1 | bytes 1 | tf_op jit(solution)/shard_map/pallas_call | solution.py:122
  188.6 113.7 %shard_map.306 = (bf16[4,4,160,1280]{3,2,1,0:T(8,128)(2,1)S(1)}, bf16[4,2,256,2560]{3,2,1,0:T(8,128)(2,1)}, bf16[4,160,800]{2,1,0:T(8,128)(2,1)S(1)}) custom-call(bf16[160,1280]{1,0:T(8,128)(2,1)S(1)} %copy-done.30, bf16[256,2560]{1,0:T(8,128)(2,1)S(1)} %fusion.5.value_ref, bf16[4,160,800]{2,1,0:T(8,128)(2,1)S(1)} %copy-done.10), custom_call_target="tpu_custom_call" | custom-call | flops 1 | bytes 1 | tf_op jit(solution)/shard_map/pallas_call | solution.py:692
  302.4 3.6 fusion.52
  322.4 49.5 %shard_map.308 = bf16[4,2,256,2560]{3,2,1,0:T(8,128)(2,1)S(1)} custom-call(bf16[256,2560]{1,0:T(8,128)(2,1)S(1)} %multiply_convert_fusion.4.value_ref), custom_call_target="tpu_custom_call" | custom-call | flops 1 | bytes 1 | tf_op jit(solution)/shard_map/pallas_call | solution.py:786
  375.8 13.1 %fusion.54 = f32[2048,800]{1,0:T(8,128)} fusion(bf16[2048,2560]{1,0:T(8,128)(2,1)S(1)} %bitcast.98, bf16[2560,800]{1,0:T(8,128)(2,1)S(1)} %bitcast.105), kind=kOutput, calls=%fused_computation.161 | convolution fusion | flops 8388608000 | bytes 21135360 | tf_op jit(solution)/shard_map/dot_general | solution.py:1135
  390.9 8.7 collective-permute-done.7.refs_3_
  400.6 16.5 %fusion.53 = f32[2048,800]{1,0:T(8,128)} fusion(bf16[2048,2560]{1,0:T(8,128)(2,1)} %bitcast.121, bf16[2560,800]{1,0:T(8,128)(2,1)S(1)} %bitcast.103), kind=kOutput, calls=%fused_computation.160 | convolution fusion | flops 8388608000 | bytes 21135360 | tf_op jit(solution)/shard_map/dot_general | solution.py:1142
  417.1 21.2 %multiply_convert_fusion = (bf16[2048,800]{1,0:T(8,128)(2,1)}, bf16[2048,800]{1,0:T(8,128)(2,1)}, bf16[2048,800]{1,0:T(8,128)(2,1)}) fusion(f32[2048,800]{1,0:T(8,128)} %fusion.54, f32[2048,800]{1,0:T(8,128)} %fusion.53, bf16[2048,2560]{1,0:T(8,128)(2,1)} %bitcast.99, bf16[2560,800]{1,0:T(8,128)(2,1)S(1)} %bitcast.107), kind=kOutput, calls=%fused_computation.1 | convolution fusion | flops 8413184000 | bytes 37519360 | tf_op jit(solution)/shard_map/dot_general | solution.py:1136
  438.3 16.1 %shard_map.311 = (bf16[4,320,800]{2,1,0:T(8,128)(2,1)}, bf16[4,320,800]{2,1,0:T(8,128)(2,1)}) custom-call(bf16[2048,2560]{1,0:T(8,128)(2,1)} %bitcast.122, bf16[2048,800]{1,0:T(8,128)(2,1)} %get-tuple-element.140.right_ref.refs_0_), custom_call_target="tpu_custom_call" | custom-call | flops 1 | bytes 1 | tf_op jit(solution)/shard_map/pallas_call | solution.py:402
  455.3 16.1 %shard_map.312 = (bf16[4,320,800]{2,1,0:T(8,128)(2,1)}, bf16[4,320,800]{2,1,0:T(8,128)(2,1)}) custom-call(bf16[2048,2560]{1,0:T(8,128)(2,1)} %bitcast.100, bf16[2048,800]{1,0:T(8,128)(2,1)} %get-tuple-element.130.right_ref.refs_0_), custom_call_target="tpu_custom_call" | custom-call | flops 1 | bytes 1 | tf_op jit(solution)/shard_map/pallas_call | solution.py:402
  471.4 33.7 %shard_map.313 = bf16[4,256,2560]{2,1,0:T(8,128)(2,1)} custom-call(bf16[2048,800]{1,0:T(8,128)(2,1)} %get-tuple-element.130.right_ref.refs_0_, bf16[2560,800]{1,0:T(8,128)(2,1)} %bitcast.106, bf16[2048,800]{1,0:T(8,128)(2,1)} %get-tuple-element.131.refs_2_.right_ref, bf16[2560,800]{1,0:T(8,128)(2,1)} %bitcast.108), custom_call_target="tpu_custom_call" | custom-call | flops 1 | bytes 1 | tf_op jit(solution)/shard_map/pallas_call | solution.py:356
  506.0 4.1 constant_dynamic-slice_fusion.5
  514.5 16.1 %shard_map.314 = (bf16[4,320,800]{2,1,0:T(8,128)(2,1)}, bf16[4,320,800]{2,1,0:T(8,128)(2,1)}) custom-call(bf16[2048,2560]{1,0:T(8,128)(2,1)} %bitcast.101, bf16[2048,800]{1,0:T(8,128)(2,1)} %get-tuple-element.131.refs_2_.right_ref), custom_call_target="tpu_custom_call" | custom-call | flops 1 | bytes 1 | tf_op jit(solution)/shard_map/pallas_call | solution.py:402
  530.6 16.2 %shard_map.315 = bf16[2048,2560]{1,0:T(8,128)(2,1)} custom-call(bf16[2048,800]{1,0:T(8,128)(2,1)} %get-tuple-element.140.right_ref.refs_0_, bf16[2560,800]{1,0:T(8,128)(2,1)} %bitcast.104), custom_call_target="tpu_custom_call" | custom-call | flops 1 | bytes 1 | tf_op jit(solution)/shard_map/pallas_call | solution.py:301
  546.8 4.3 add_convert_fusion.1
  551.1 18.1 %collective-permute-done.11 = bf16[1,1,256,2560]{3,2,1,0:T(8,128)(2,1)} collective-permute-done((bf16[1,1,256,2560]{3,2,1,0:T(8,128)(2,1)}, bf16[1,1,256,2560]{3,2,1,0:T(8,128)(2,1)}, u32[]{:S(2)}, u32[]{:S(2)}) %collective-permute-start.11) | collective-permute-done | bytes 1310752 | tf_op jit(solution)/shard_map/ppermute | solution.py:227
  570.6 4.7 add_bitcast_fusion
  576.0 3.9 multiply_reduce_fusion
  580.1 3.8 multiply_convert_fusion.3
  585.8 3.1 add_convert_fusion
  593.0 3.5 convolution_convert_fusion.3.d_mixed_ref
  599.2 20.9 %shard_map.316 = (bf16[512,2560]{1,0:T(8,128)(2,1)S(1)}, bf16[512,2560]{1,0:T(8,128)(2,1)S(1)}, f32[512,128]{1,0:T(8,128)S(1)}) custom-call(bf16[512,2560]{1,0:T(8,128)(2,1)S(1)} %copy-done.12, bf16[512,2560]{1,0:T(8,128)(2,1)S(1)} %copy-done.2, bf16[512,1280]{1,0:T(8,128)(2,1)S(1)} %convolution_convert_fusion.3.d_mixed_ref, ...), custom_call_target="tpu_custom_call" | custom-call | flops 1 | bytes 1 | tf_op jit(solution)/shard_map/pallas_call | solution.py:195
  620.1 3.9 shard_map.317
  625.6 4.7 shard_map.318
  631.2 3.6 copy-done.53
  637.1 5.6 collective-permute-done.14
  652.8 6.3 fusion.4
  660.1 4.6 convolution_convert_fusion
  664.7 187.9 %shard_map.319 = (f32[80,1056]{1,0:T(8,128)}, f32[8,128]{1,0:T(8,128)}, f32[48,1920]{1,0:T(8,128)}, f32[16,2560]{1,0:T(8,128)}, f32[160,1280]{1,0:T(8,128)}, /*i...) custom-call(f32[8,128]{1,0:T(8,128)} %copy-done.33, bf16[2,2,2,2,2,80,1056]{6,5,4,3,2,1,0:T(8,128)(2,1)} %bitcast.118, ...), custom_call_target="tpu_custom_call" | custom-call | tf_op jit(solution)/shard_map/pallas_call | solution.py:978
  867.2 5.9 fusion.6
  (337 shorter events, 105.4 us)
Async XLA Ops:
  7.2 860.0 %reduce-scatter.2.cloned.1.call-start = ((), (), s32[]{:S(2)}) async-start(), calls=%async_computation.1 | async-start | bytes 11796480 | tf_op jit(solution)/shard_map/reduce_scatter | solution.py:1187
  14.4 129.2 %copy-start.39 = (bf16[256,2560]{1,0:T(8,128)(2,1)S(1)}, bf16[256,2560]{1,0:T(8,128)(2,1)}, u32[]{:S(2)}) copy-start(bf16[256,2560]{1,0:T(8,128)(2,1)} %param.17) | copy-start | bytes 3932164
  141.0 161.3 %collective-permute-start.1 = (bf16[4,160,800]{2,1,0:T(8,128)(2,1)}, bf16[4,160,800]{2,1,0:T(8,128)(2,1)}, u32[]{:S(2)}, u32[]{:S(2)}) collective-permute-start(bf16[4,160,800]{2,1,0:T(8,128)(2,1)} %get-tuple-element.123.refs_0_), channel_id=1, source_target_pairs={{0,16},{16,0},{1,17},{17,1},{2,18},{18,2},{3,19},{19,3},{4,20},{20... | collective-permute-start | bytes 3072008 | tf_op jit(solution)/shard_map/ppermute | solution.py:223
  142.3 160.0 %collective-permute-start.2 = (bf16[4,160,800]{2,1,0:T(8,128)(2,1)}, bf16[4,160,800]{2,1,0:T(8,128)(2,1)}, u32[]{:S(2)}, u32[]{:S(2)}) collective-permute-start(bf16[4,160,800]{2,1,0:T(8,128)(2,1)} %get-tuple-element.123.refs_0_), channel_id=1, source_target_pairs={{0,4},{4,0},{1,5},{5,1},{2,6},{6,2},{3,7},{7,3},{8,12},{12,8},{9,1... | collective-permute-start | bytes 3072008 | tf_op jit(solution)/shard_map/ppermute | solution.py:223
  142.9 14.9 %copy-start.89 = (f32[16]{0:T(128)}, f32[16]{0:T(128)S(1)}, u32[]{:S(2)}) copy-start(f32[16]{0:T(128)S(1)} %multiply_power_fusion) | copy-start | bytes 196
  148.7 11.5 %copy-start.88 = (s32[1,512]{1,0:T(1,128)S(1)}, s32[1,512]{1,0:T(1,128)}, u32[]{:S(2)}) copy-start(s32[1,512]{1,0:T(1,128)} %param.19) | copy-start | bytes 6148
  155.9 7.0 collective-permute-start
  155.9 146.4 %collective-permute-start.3 = (bf16[4,160,800]{2,1,0:T(8,128)(2,1)}, bf16[4,160,800]{2,1,0:T(8,128)(2,1)}, u32[]{:S(2)}, u32[]{:S(2)}) collective-permute-start(bf16[4,160,800]{2,1,0:T(8,128)(2,1)} %get-tuple-element.112.refs_1_), channel_id=1, source_target_pairs={{0,4},{4,0},{1,5},{5,1},{2,6},{6,2},{3,7},{7,3},{8,12},{12,8},{9,1... | collective-permute-start | bytes 3072008 | tf_op jit(solution)/shard_map/ppermute | solution.py:223
  170.4 18.2 %copy-start.10 = (bf16[4,160,800]{2,1,0:T(8,128)(2,1)S(1)}, bf16[4,160,800]{2,1,0:T(8,128)(2,1)}, u32[]{:S(2)}) copy-start(bf16[4,160,800]{2,1,0:T(8,128)(2,1)} %get-tuple-element.116.piece_ref.refs_0_) | copy-start | bytes 3072004
  170.4 18.2 %copy-start.30 = (bf16[160,1280]{1,0:T(8,128)(2,1)S(1)}, bf16[160,1280]{1,0:T(8,128)(2,1)}, u32[]{:S(2)}) copy-start(bf16[160,1280]{1,0:T(8,128)(2,1)} %rows_ref) | copy-start | bytes 1228804
  188.6 117.4 %copy-start.33 = (f32[8,128]{1,0:T(8,128)}, f32[8,128]{1,0:T(8,128)S(1)}, u32[]{:S(2)}) copy-start(f32[8,128]{1,0:T(8,128)S(1)} %get-tuple-element.155.refs_0_) | copy-start | bytes 12292
  309.0 8.0 collective-permute-start.4
  310.4 61.5 %collective-permute-start.6 = (bf16[4,160,800]{2,1,0:T(8,128)(2,1)}, bf16[4,160,800]{2,1,0:T(8,128)(2,1)S(1)}, u32[]{:S(2)}, u32[]{:S(2)}) collective-permute-start(bf16[4,160,800]{2,1,0:T(8,128)(2,1)} %collective-permute-done.1.refs_1_), channel_id=1, source_target_pairs={{0,4},{4,0},{1,5},{5,1},{2,6},{6,2},{3,7},{7,3},{8,12},{12,8},{9,1... | collective-permute-start | bytes 3072008 | tf_op jit(solution)/shard_map/ppermute | solution.py:223
  312.0 60.0 %collective-permute-start.5 = (bf16[4,160,800]{2,1,0:T(8,128)(2,1)S(1)}, bf16[4,160,800]{2,1,0:T(8,128)(2,1)S(1)}, u32[]{:S(2)}, u32[]{:S(2)}) collective-permute-start(bf16[4,160,800]{2,1,0:T(8,128)(2,1)S(1)} %copy-done.10), channel_id=1, source_target_pairs={{0,4},{4,0},{1,5},{5,1},{2,6},{6,2},{3,7},{7,3},{8,12},{12,8},{9,1... | collective-permute-start | bytes 3072008 | tf_op jit(solution)/shard_map/ppermute | solution.py:223
  317.0 55.8 %copy-start.5 = (bf16[16,160,800]{2,1,0:T(8,128)(2,1)}, bf16[16,160,800]{2,1,0:T(8,128)(2,1)S(1)}, u32[]{:S(2)}) copy-start(bf16[16,160,800]{2,1,0:T(8,128)(2,1)S(1)} %shard_map.307) | copy-start | bytes 12288004
  322.1 49.8 %copy-start.35 = (f32[256,2560]{1,0:T(8,128)}, f32[256,2560]{1,0:T(8,128)S(1)}, u32[]{:S(2)}) copy-start(f32[256,2560]{1,0:T(8,128)S(1)} %get-tuple-element.184) | copy-start | bytes 7864324
  322.1 49.8 %copy-start.84 = (f32[256]{0:T(256)}, f32[256]{0:T(256)S(1)}, u32[]{:S(2)}) copy-start(f32[256]{0:T(256)S(1)} %get-tuple-element.183) | copy-start | bytes 3076
  322.4 49.5 %copy-start.24 = (bf16[4,160,800]{2,1,0:T(8,128)(2,1)S(1)}, bf16[4,160,800]{2,1,0:T(8,128)(2,1)}, u32[]{:S(2)}) copy-start(bf16[4,160,800]{2,1,0:T(8,128)(2,1)} %copy-done.23) | copy-start | bytes 3072004
  372.0 17.0 %copy-start.19 = (bf16[4,160,800]{2,1,0:T(8,128)(2,1)S(1)}, bf16[4,160,800]{2,1,0:T(8,128)(2,1)}, u32[]{:S(2)}) copy-start(bf16[4,160,800]{2,1,0:T(8,128)(2,1)} %get-tuple-element.123.refs_0_) | copy-start | bytes 3072004
  372.0 27.6 %collective-permute-start.7 = (bf16[4,160,800]{2,1,0:T(8,128)(2,1)S(1)}, bf16[4,160,800]{2,1,0:T(8,128)(2,1)S(1)}, u32[]{:S(2)}, u32[]{:S(2)}) collective-permute-start(bf16[4,160,800]{2,1,0:T(8,128)(2,1)S(1)} %copy-done.24), channel_id=1, source_target_pairs={{0,4},{4,0},{1,5},{5,1},{2,6},{6,2},{3,7},{7,3},{8,12},{12,8},{9,1... | collective-permute-start | bytes 3072008 | tf_op jit(solution)/shard_map/ppermute | solution.py:223
  390.9 26.2 %copy-start.6 = (bf16[16,160,800]{2,1,0:T(8,128)(2,1)}, bf16[16,160,800]{2,1,0:T(8,128)(2,1)S(1)}, u32[]{:S(2)}) copy-start(bf16[16,160,800]{2,1,0:T(8,128)(2,1)S(1)} %shard_map.310) | copy-start | bytes 12288004
  400.6 16.5 %copy-start.4 = (bf16[16,160,800]{2,1,0:T(8,128)(2,1)}, bf16[16,160,800]{2,1,0:T(8,128)(2,1)S(1)}, u32[]{:S(2)}) copy-start(bf16[16,160,800]{2,1,0:T(8,128)(2,1)S(1)} %shard_map.309) | copy-start | bytes 12288004
  454.4 51.6 %collective-permute-start.8 = (bf16[4,320,800]{2,1,0:T(8,128)(2,1)}, bf16[4,320,800]{2,1,0:T(8,128)(2,1)}, u32[]{:S(2)}, u32[]{:S(2)}) collective-permute-start(bf16[4,320,800]{2,1,0:T(8,128)(2,1)} %get-tuple-element.132), channel_id=1, source_target_pairs={{0,4},{4,0},{1,5},{5,1},{2,6},{6,2},{3,7},{7,3},{8,12},{12,8},{9,1... | collective-permute-start | bytes 6144008 | tf_op jit(solution)/shard_map/ppermute | solution.py:223
  510.1 41.0 %collective-permute-start.10 = (bf16[1,1,256,2560]{3,2,1,0:T(8,128)(2,1)}, bf16[1,1,256,2560]{3,2,1,0:T(8,128)(2,1)}, u32[]{:S(2)}, u32[]{:S(2)}) collective-permute-start(bf16[1,1,256,2560]{3,2,1,0:T(8,128)(2,1)} %get-tuple-element.190), channel_id=1, source_target_pairs={{0,8},{8,0},{1,9},{9,1},{2,10},{10,2},{3,11},{11,3},{4,12},{12,4},... | collective-permute-start | bytes 3932168 | tf_op jit(solution)/shard_map/ppermute | solution.py:223
  511.7 57.5 %collective-permute-start.11 = (bf16[1,1,256,2560]{3,2,1,0:T(8,128)(2,1)}, bf16[1,1,256,2560]{3,2,1,0:T(8,128)(2,1)}, u32[]{:S(2)}, u32[]{:S(2)}) collective-permute-start(bf16[1,1,256,2560]{3,2,1,0:T(8,128)(2,1)} %get-tuple-element.189), channel_id=1, source_target_pairs={{0,10},{2,8},{8,2},{10,0},{1,11},{3,9},{9,3},{11,1},{4,14},{6,12},... | collective-permute-start | bytes 3932168 | tf_op jit(solution)/shard_map/ppermute | solution.py:227
  513.2 57.4 %collective-permute-start.9 = (bf16[1,1,256,2560]{3,2,1,0:T(8,128)(2,1)}, bf16[1,1,256,2560]{3,2,1,0:T(8,128)(2,1)}, u32[]{:S(2)}, u32[]{:S(2)}) collective-permute-start(bf16[1,1,256,2560]{3,2,1,0:T(8,128)(2,1)} %get-tuple-element.188), channel_id=1, source_target_pairs={{0,2},{2,0},{1,3},{3,1},{4,6},{6,4},{5,7},{7,5},{8,10},{10,8},{9,1... | collective-permute-start | bytes 3932168 | tf_op jit(solution)/shard_map/ppermute | solution.py:223
  513.6 61.7 %collective-permute-start.12 = (bf16[4,320,800]{2,1,0:T(8,128)(2,1)}, bf16[4,320,800]{2,1,0:T(8,128)(2,1)}, u32[]{:S(2)}, u32[]{:S(2)}) collective-permute-start(bf16[4,320,800]{2,1,0:T(8,128)(2,1)} %get-tuple-element.137), channel_id=1, source_target_pairs={{0,4},{4,0},{1,5},{5,1},{2,6},{6,2},{3,7},{7,3},{8,12},{12,8},{9,1... | collective-permute-start | bytes 6144008 | tf_op jit(solution)/shard_map/ppermute | solution.py:223
  583.9 7.0 collective-permute-start.13
  583.9 58.8 %collective-permute-start.15 = (bf16[4,320,800]{2,1,0:T(8,128)(2,1)}, bf16[4,320,800]{2,1,0:T(8,128)(2,1)}, u32[]{:S(2)}, u32[]{:S(2)}) collective-permute-start(bf16[4,320,800]{2,1,0:T(8,128)(2,1)} %get-tuple-element.151), channel_id=1, source_target_pairs={{0,4},{4,0},{1,5},{5,1},{2,6},{6,2},{3,7},{7,3},{8,12},{12,8},{9,1... | collective-permute-start | bytes 6144008 | tf_op jit(solution)/shard_map/ppermute | solution.py:223
  590.1 52.6 %collective-permute-start.14 = (bf16[1,2,2,160,800]{4,3,2,1,0:T(8,128)(2,1)S(1)}, bf16[1,2,2,160,800]{4,3,2,1,0:T(8,128)(2,1)}, u32[]{:S(2)}, u32[]{:S(2)}) collective-permute-start(bf16[1,2,2,160,800]{4,3,2,1,0:T(8,128)(2,1)S(1)} %get-tuple-element.196), channel_id=1, source_target_pairs={{0,16},{16,0},{1,17},{17,1},{2,18},{18,2},{3,19},{19,3},{4,20},{20... | collective-permute-start | bytes 3072008 | tf_op jit(solution)/shard_map/ppermute | solution.py:223
  599.2 20.9 %copy-start.9 = (bf16[512,768]{1,0:T(8,128)(2,1)S(1)}, bf16[512,768]{1,0:T(8,128)(2,1)}, u32[]{:S(2)}) copy-start(bf16[512,768]{1,0:T(8,128)(2,1)} %copy-done.8) | copy-start | bytes 2359300
  645.4 3.8 collective-permute-start.16
  (81 other events, 297.9 us)
Sparse Core Ops, SparseCore 0:
  575.4 105.2 reduce-scatter.1
